TPU v7x, 32 devices: a whole 2x2x4 slice. The times are simulated.
32 devices in a mesh: grp: 2 (over y), ctx: 16 (over z, x, core).
Axes of the slice: x: 2, y: 2, z: 4, core: 2. Of those that a mesh axis runs over, the one named last changes fastest.
Arguments:
- query_main: bfloat16 [64, 128, 576], P(('grp', 'ctx')), parts along dimension 0, may hold values from -3 to 3
- key_codes: bfloat16 [4096, 576], P(('grp', 'ctx')), parts along dimension 0, may hold values from -4 to 4
- key_scales: int32 [4096, 4], P(('grp', 'ctx')), parts along dimension 0, may hold values from -2 to 2
- index_keys: bfloat16 [4096, 128], P(('grp', 'ctx')), parts along dimension 0, may hold values from -5 to 5
- index_query: bfloat16 [64, 64, 128], P(('grp', 'ctx')), parts along dimension 0, may hold values from -7 to 7
- index_weight: float32 [64, 64], P(('grp', 'ctx')), parts along dimension 0, may hold values from -4 to 4
- query_pos: int32 [64], P(('grp', 'ctx')), parts along dimension 0, may hold values from 1024 to 2047
Outputs:
- grad_index_query: float32 [64, 64, 128], P(('grp', 'ctx')), parts along dimension 0
- grad_index_weight: float32 [64, 64], P(('grp', 'ctx')), parts along dimension 0
- grad_index_keys: float32 [4096, 128], P(('grp', 'ctx')), parts along dimension 0
There are 2 independent parts, one for each index of `grp`. A program takes and returns all parts, laid end to end along the dimension named above; each array names one. Nothing has to cross between parts.
All inputs are finite; a program needn't handle non-finite values.
Results may differ from a plain program's by a relative error of at most 0.005.
Values may be sent and summed in bfloat16 or wider, within the bound.
No kernel may reach another device: no remote copies, remote signals or barrier semaphores. Data moves between devices by JAX's collectives and lax.ppermute only.
A program may use at most 192 MiB of HBM per device.

v0:
```python
import functools

import jax
import jax.numpy as jnp
from jax import lax
from jax.experimental import pallas as pl
from jax.experimental.pallas import tpu as pltpu
from jax.sharding import PartitionSpec as P


ROPE = 64
LANES = 128

f32, bf16 = jnp.float32, jnp.bfloat16
main_scale = 192.0 ** (-0.5)


def kernel_call(kernel, shapes, operands, scratch=(), flops=0):
    nbytes = sum(x.size * x.dtype.itemsize for x in (*operands, *shapes))
    return pl.pallas_call(
        kernel,
        out_shape=tuple(shapes),
        scratch_shapes=list(scratch),
        compiler_params=pltpu.CompilerParams(vmem_limit_bytes=24 << 20),
        cost_estimate=pl.CostEstimate(flops=flops, bytes_accessed=nbytes, transcendentals=0),
    )(*operands)


def contract(left, right, dims):
    return lax.dot_general(left, right, ((dims[:1], dims[1:]), ((), ())), preferred_element_type=f32)


def swap(array, mask, count):
    return lax.ppermute(array, "ctx", [(i, i ^ mask) for i in range(count)])


def swap_gather(block, stride, parts, count):
    held = {0: block}
    bit = parts // 2
    while bit:
        for k, own in list(held.items()):
            held[k ^ bit] = swap(own, stride * bit, count)
        bit //= 2
    return [held[k] for k in range(parts)]


def pack_kernel(
    scales_hbm, keys_hbm, weight_hbm, pos_hbm, main_hbm, query_hbm, codes_hbm, out_ref, query_ref,
    main_ref, codes_ref, scales_ref, weight_ref, pos_ref, sems
):
    groups, own_keys = scales_hbm.shape
    key_count = keys_hbm.shape[0]
    lines = query_hbm.shape[0]
    pairs = (
        (scales_hbm, scales_ref),
        (weight_hbm, weight_ref),
        (pos_hbm, pos_ref),
        (keys_hbm, out_ref.at[pl.ds(0, key_count), :]),
        (query_hbm, query_ref.at[pl.ds(0, lines), :]),
        (main_hbm, main_ref),
        (codes_hbm, codes_ref),
    )
    copies = [pltpu.make_async_copy(a, b, sems.at[n]) for n, (a, b) in enumerate(pairs)]
    for copy in copies:
        copy.start()
    for copy in copies[:3]:
        copy.wait()
    factors = jnp.exp2(scales_ref[...].astype(f32))
    spare = out_ref.shape[0] - key_count - groups
    factors = jnp.concatenate([factors, jnp.zeros((spare, own_keys), f32)], axis=0)
    out_ref[key_count:, :] = factors.astype(bf16)
    own_rows, index_heads = weight_ref.shape
    rest = jnp.concatenate([weight_ref[...], jnp.zeros((own_rows, LANES - index_heads), f32)], axis=1)
    lane = lax.broadcasted_iota(jnp.int32, (1, LANES), 1)
    tail = []
    for part in range(3):
        piece = rest.astype(bf16).astype(f32)
        rest = rest - piece
        for i in range(own_rows):
            pos = jnp.full((1, LANES), pos_ref[i], jnp.int32)
            at = ((pos // LANES) * LANES, pos % LANES, jnp.zeros_like(pos))[part].astype(f32)
            tail.append(jnp.where(lane == index_heads, at, piece[i : i + 1, :]))
    tail.append(jnp.zeros((query_ref.shape[0] - lines - len(tail), LANES), f32))
    query_ref[lines:, :] = jnp.concatenate(tail, axis=0).astype(bf16)
    for copy in copies[3:]:
        copy.wait()


def latent_of(codes_ref, keys_ref, groups):
    latent_width, own_keys = codes_ref.shape
    group_width = (latent_width - ROPE) // groups
    factors = keys_ref[own_keys:, :].astype(f32)
    latent = [
        (codes_ref[g * group_width : (g + 1) * group_width, :].astype(f32) * factors[g : g + 1, :]).astype(bf16)
        for g in range(groups)
    ]
    return jnp.concatenate([*latent, codes_ref[groups * group_width :, :]], axis=0)


def score_kernel(offsets, row_parts, groups, first, *refs):
    parts = len(offsets)
    if first:
        queries, iqueries = refs[:row_parts], refs[row_parts : 2 * row_parts]
        refs = refs[2 * row_parts :]
        codes, blocks, refs = refs[:parts], refs[parts : 2 * parts], refs[2 * parts :]
        exp_ref, index_ref, sums_ref, main_ref, flat_ref, column_ref, pos_ref, side_ref = refs
        own_rows, head_count = queries[0].shape[0], queries[0].shape[2]
        lines = flat_ref.shape[0] // row_parts
        index_heads = lines // own_rows
        for r in range(row_parts):
            tail = iqueries[r][lines:, :].astype(f32)
            side = tail[:own_rows] + tail[own_rows : 2 * own_rows]
            side = side + tail[2 * own_rows : 3 * own_rows]
            side_ref[r * own_rows : (r + 1) * own_rows, :] = side
            flat_ref[r * lines : (r + 1) * lines, :] = iqueries[r][:lines, :]
            for i in range(own_rows):
                t = r * own_rows + i
                main_ref[t * head_count : (t + 1) * head_count, :] = jnp.transpose(queries[r][i])
        side = side_ref[...]
        columns = jnp.transpose(side)
        column_ref[...] = columns[:index_heads, :]
        pos_ref[...] = jnp.broadcast_to(side[:, index_heads : index_heads + 1], pos_ref.shape)
    else:
        main_ref, flat_ref, column_ref, pos_ref = refs[:4]
        codes, blocks = refs[4 : 4 + parts], refs[4 + parts : 4 + 2 * parts]
        exp_ref, index_ref, sums_ref = refs[4 + 2 * parts :]
    rows = pos_ref.shape[0]
    own_rows = rows // row_parts
    index_heads = column_ref.shape[0]
    index_width = flat_ref.shape[1]
    head_count = main_ref.shape[0] // rows
    own_keys = blocks[0].shape[1]
    index_scale = float(index_heads * index_width) ** (-0.5)
    me = lax.axis_index("ctx")
    iota = lax.broadcasted_iota(jnp.int32, (1, own_keys), 1)
    key_pos = [((me ^ (row_parts * k)) * own_keys + iota).astype(f32) for k in offsets]
    key_pos = jnp.concatenate(key_pos, axis=1)
    latent = jnp.concatenate([latent_of(c, b, groups) for c, b in zip(codes, blocks)], axis=1)
    ikeys = jnp.concatenate([b[:own_keys, :] for b in blocks], axis=0)
    dots = contract(flat_ref[...], ikeys, (1, 1))
    scores = contract(main_ref[...], latent, (1, 0))
    sums_ref[...] = jnp.zeros_like(sums_ref)
    for t in range(rows):
        r, i = divmod(t, own_rows)
        visible = key_pos <= pos_ref[t : t + 1, :1]
        heads = jnp.maximum(dots[t * index_heads : (t + 1) * index_heads, :], 0.0)
        score = jnp.sum(column_ref[:, t : t + 1] * heads, axis=0, keepdims=True)
        index_exp = jnp.where(visible, jnp.exp(index_scale * score), 0.0)
        index_ref[t : t + 1, :] = index_exp
        score = scores[t * head_count : (t + 1) * head_count, :] * main_scale
        main_exp = jnp.where(visible, jnp.exp(score), 0.0)
        exp_ref[t] = main_exp
        total = main_exp[:, :own_keys]
        for k in range(1, parts):
            total = total + main_exp[:, k * own_keys : (k + 1) * own_keys]
        sums_ref[r, i : i + 1, :] = jnp.sum(jnp.transpose(total), axis=0, keepdims=True)
        index_total = jnp.sum(index_exp, axis=1, keepdims=True)
        sums_ref[r, own_rows + i : own_rows + i + 1, :] = jnp.broadcast_to(
            index_total, (1, head_count)
        )


def grad_kernel(key_total, row_parts, places, last, *refs):
    count = 1 + max(n for n, _ in places)
    near_ref, far_ref, flat_ref, column_ref = refs[:4]
    exps, indexes = refs[4 : 4 + count], refs[4 + count : 4 + 2 * count]
    refs = refs[4 + 2 * count :]
    blocks, refs = refs[: len(places)], refs[len(places) :]
    if last:
        early_dots, early_columns = refs[:2]
        early_blocks, refs = refs[2 : 2 + len(places)], refs[2 + len(places) :]
        key_ref, keep_ref, send_ref, dots_ref, total_ref = refs
    else:
        key_ref, dots_ref, columns_ref, total_ref = refs
    rows, own_rows = total_ref.shape[0], total_ref.shape[0] // row_parts
    index_heads, index_width = column_ref.shape[0], flat_ref.shape[1]
    head_count, own_keys = exps[0].shape[1], key_ref.shape[1]
    index_scale = float(index_heads * index_width) ** (-0.5)
    ikeys = jnp.concatenate([b[:own_keys, :] for b in blocks], axis=0)
    flat = flat_ref[...]
    dots = contract(flat, ikeys, (1, 1))
    for r in range(row_parts):
        lines = slice(0, own_rows)
        total_ref[r * own_rows : (r + 1) * own_rows, :] = near_ref[r, lines, :] + far_ref[r ^ 1, lines, :]
    shares = jnp.transpose(1.0 / total_ref[...])
    lane = lax.broadcasted_iota(jnp.int32, (index_heads, LANES), 1)
    columns = early_columns[...] if last else jnp.zeros((index_heads, LANES), f32)
    for t in range(rows):
        r, i = divmod(t, own_rows)
        share = shares[:, t : t + 1]
        at = own_rows + i
        index_total = near_ref[r, at : at + 1, :1] + far_ref[r ^ 1, at : at + 1, :1]
        target = jnp.concatenate(
            [
                jnp.sum(exps[n][t, :, p : p + own_keys] * share, axis=0, keepdims=True)
                for n, p in places
            ],
            axis=1,
        )
        index_exp = jnp.concatenate(
            [indexes[n][t : t + 1, p : p + own_keys] for n, p in places], axis=1
        )
        gradient = key_total * (index_exp / index_total - target / head_count)
        heads = dots[t * index_heads : (t + 1) * index_heads, :]
        column = index_scale * jnp.sum(gradient * jnp.maximum(heads, 0.0), axis=1, keepdims=True)
        columns = jnp.where(lane == t, columns + column, columns)
        weight = column_ref[:, t : t + 1]
        grad_dots = jnp.where(heads > 0, index_scale * gradient * weight, 0.0).astype(bf16)
        dots_ref[t * index_heads : (t + 1) * index_heads, :] = grad_dots
    grad_dots = dots_ref[...]
    key_grad = contract(grad_dots, flat, (0, 0))
    for k in range(len(blocks)):
        key_ref[k] = key_grad[k * own_keys : (k + 1) * own_keys, :].astype(key_ref.dtype)
    if not last:
        columns_ref[...] = columns
        return
    early_keys = jnp.concatenate([b[:own_keys, :] for b in early_blocks], axis=0)
    grad_query = contract(grad_dots, ikeys, (1, 0)) + contract(early_dots[...], early_keys, (1, 0))
    weights = jnp.transpose(jnp.concatenate([columns, jnp.zeros_like(columns)], axis=0)[:LANES])
    lines = own_rows * index_heads
    for r in range(row_parts):
        out, at = (keep_ref, r) if r < row_parts // 2 else (send_ref, r - row_parts // 2)
        out[at, :lines, :] = grad_query[r * lines : (r + 1) * lines, :]
        out[at, lines : lines + own_rows, :] = weights[r * own_rows : (r + 1) * own_rows, :]


def finish_kernel(key_ref, key_got_ref, row_ref, row_got_ref, query_ref, weight_ref, key_out_ref):
    lines = query_ref.shape[0]
    own_rows, index_heads = weight_ref.shape
    key_out_ref[...] = key_ref[...] + key_got_ref[...].astype(f32)
    query_ref[...] = row_ref[:lines, :] + row_got_ref[:lines, :]
    tail = slice(lines, lines + own_rows)
    weight_ref[...] = (row_ref[tail, :] + row_got_ref[tail, :])[:, :index_heads]


def body(query_main, key_codes, key_scales, index_keys, index_query, index_weight, query_pos):
    own_rows, head_count, latent_width = query_main.shape
    index_heads, index_width = index_query.shape[1:]
    own_keys = key_codes.shape[0]
    count = lax.axis_size("ctx")
    row_parts = 4
    key_parts = count // row_parts
    key_total = own_keys * count
    rows = own_rows * row_parts
    lines = own_rows * index_heads
    tall = lines + 8
    struct = jax.ShapeDtypeStruct

    codes = key_codes.T
    groups = key_scales.shape[1]
    main_raw = jnp.transpose(query_main, (0, 2, 1))
    sources = (
        key_scales.T,
        index_keys,
        index_weight,
        query_pos,
        main_raw,
        index_query.reshape(lines, index_width),
        codes,
    )
    key_pack, index_own, main_own, codes_own = pl.pallas_call(
        pack_kernel,
        out_shape=(
            struct((own_keys + 16, own_keys), bf16),
            struct((lines + 16, index_width), bf16),
            struct(main_raw.shape, bf16),
            struct(codes.shape, bf16),
        ),
        in_specs=[pl.BlockSpec(memory_space=pltpu.HBM)] * len(sources),
        scratch_shapes=[
            pltpu.VMEM((groups, own_keys), jnp.int32),
            pltpu.VMEM((own_rows, index_heads), f32),
            pltpu.SMEM((own_rows,), jnp.int32),
            pltpu.SemaphoreType.DMA((len(sources),)),
        ],
        compiler_params=pltpu.CompilerParams(vmem_limit_bytes=8 << 20),
        name="pack",
    )(*(pltpu.with_memory_space_constraint(x, pltpu.HBM) for x in sources))
    codes = swap_gather(codes, row_parts, key_parts, count)
    codes[0] = codes_own
    blocks = swap_gather(key_pack, row_parts, key_parts, count)
    queries = swap_gather(main_raw, 1, row_parts, count)
    queries[0] = main_own
    iqueries = swap_gather(index_own, 1, row_parts, count)

    step = 4
    if key_parts <= step:
        pieces = [list(range(key_parts - 1)), [key_parts - 1]]
    else:
        pieces = [list(range(k, k + step)) for k in range(0, key_parts, step)]
    exps, indexes, sums, laid = [], [], None, None
    for n, piece in enumerate(pieces):
        wide = len(piece) * own_keys
        shapes = (
            struct((rows, head_count, wide), f32),
            struct((rows, wide), f32),
            struct((row_parts, 2 * own_rows, head_count), f32),
        )
        if n == 0:
            shapes += (
                struct((rows * head_count, latent_width), bf16),
                struct((rows * index_heads, index_width), bf16),
                struct((index_heads, rows), f32),
                struct((rows, LANES), f32),
            )
        out = kernel_call(
            functools.partial(score_kernel, tuple(piece), row_parts, groups, n == 0),
            shapes,
            (
                *(laid or (*queries, *iqueries)),
                *(codes[k] for k in piece),
                *(blocks[k] for k in piece),
            ),
            scratch=(pltpu.VMEM((rows, LANES), f32),) if n == 0 else (),
            flops=2 * rows * head_count * latent_width * wide,
        )
        laid = laid or out[3:]
        exps.append(out[0])
        indexes.append(out[1])
        sums = out[2] if sums is None else sums + out[2]

    bit = row_parts // 2
    while bit > 1:
        got = swap(sums, bit, count)
        sums = sums + jnp.stack([got[r ^ bit] for r in range(row_parts)])
        bit //= 2
    got = swap(sums, 1, count)

    place = {k: (n, p * own_keys) for n, piece in enumerate(pieces) for p, k in enumerate(piece)}
    teams = [list(range(key_parts))] if key_parts <= step else pieces
    even, odd, keep, send = [], [], None, None
    for ids in teams:
        half = len(ids) // 2
        early = None
        for part in (1, 0):
            mine = ids[part::2]
            used = sorted({place[k][0] for k in mine})
            places = tuple((used.index(place[k][0]), place[k][1]) for k in mine)
            operands = (
                sums,
                got,
                *laid[1:3],
                *(exps[n] for n in used),
                *(indexes[n] for n in used),
                *(blocks[k] for k in mine),
            )
            shapes = (struct((half, own_keys, index_width), bf16 if part else f32),)
            more = struct((rows * index_heads, half * own_keys), bf16)
            scratch = (pltpu.VMEM((rows, head_count), f32),)
            if part:
                shapes += (more, struct((index_heads, LANES), f32))
            else:
                operands += (*early, *(blocks[k] for k in ids[1::2]))
                shapes += (struct((row_parts // 2, tall, index_width), f32),) * 2
                scratch = (pltpu.VMEM(more.shape, bf16), *scratch)
            out = kernel_call(
                functools.partial(grad_kernel, key_total, row_parts, places, not part),
                shapes,
                operands,
                scratch=scratch,
                flops=6 * rows * index_heads * index_width * half * own_keys,
            )
            if part:
                odd.append(out[0])
                early = out[1:]
            else:
                even.append(out[0])
                keep = out[1] if keep is None else keep + out[1]
                send = out[2] if send is None else send + out[2]
    key_sum = even[0] if len(even) == 1 else jnp.concatenate(even)
    key_send = odd[0] if len(odd) == 1 else jnp.concatenate(odd)

    key_got = swap(key_send, row_parts, count)
    row_got = swap(send, row_parts // 2, count)
    bit = 2
    while bit < key_parts:
        key_sum = key_sum + key_got.astype(f32)
        key_got = swap(key_sum[1::2].astype(bf16), row_parts * bit, count)
        key_sum = key_sum[0::2]
        bit *= 2
    row_sum = keep + row_got
    row_got = swap(row_sum[1], 1, count)
    grad_query, grad_weight, key_grad = kernel_call(
        finish_kernel,
        (
            struct((lines, index_width), f32),
            struct((own_rows, index_heads), f32),
            struct((own_keys, index_width), f32),
        ),
        (key_sum[0], key_got[0], row_sum[0], row_got),
    )
    return grad_query.reshape(own_rows, index_heads, index_width), grad_weight, key_grad


def solution(mesh):
    placed = (
        P(("grp", "ctx"), None, None),
        P(("grp", "ctx"), None),
        P(("grp", "ctx"), None),
        P(("grp", "ctx"), None),
        P(("grp", "ctx"), None, None),
        P(("grp", "ctx"), None),
        P(("grp", "ctx")),
    )

    return jax.shard_map(
        body,
        mesh=mesh,
        in_specs=placed,
        out_specs=(P(("grp", "ctx"), None, None), P(("grp", "ctx"), None), P(("grp", "ctx"), None)),
        check_vma=False,
    )
```

profile of v0, /device:TPU:0, one launch (start us, length us, event | category | flops | bytes accessed | tf_op | source)
XLA Modules:
  0.0 50.3 jit_solution(7928247995019718598)
XLA Ops:
  0.6 3.0 %collective-permute-start.1 = (bf16[2,576,128]{2,1,0:T(8,128)(2,1)}, bf16[2,576,128]{2,1,0:T(8,128)(2,1)S(1)}, u32[]{:S(2)}, u32[]{:S(2)}) collective-permute-start(bf16[2,576,128]{2,1,0:T(8,128)(2,1)} %bitcast.13), channel_id=1, source_target_pairs={{0,2},{1,3},{2,0},{3,1},{4,6},{5,7},{6,4},{7,5},{8,10},{9,11},{10,... | collective-permute-start | bytes 884744 | tf_op jit(solution)/shard_map/ppermute | solution.py:34
  3.7 0.0 collective-permute-start
  3.7 7.2 %collective-permute-done.1.refs_2_ = bf16[2,576,128]{2,1,0:T(8,128)(2,1)S(1)} collective-permute-done((bf16[2,576,128]{2,1,0:T(8,128)(2,1)}, bf16[2,576,128]{2,1,0:T(8,128)(2,1)S(1)}, u32[]{:S(2)}, u32[]{:S(2)}) %collective-permute-start.1) | collective-permute-done | bytes 294944 | tf_op jit(solution)/shard_map/ppermute | solution.py:34
  10.9 0.0 collective-permute-start.2
  10.9 2.8 %collective-permute-start.7 = (bf16[576,128]{1,0:T(8,128)(2,1)}, bf16[576,128]{1,0:T(8,128)(2,1)S(1)}, u32[]{:S(2)}, u32[]{:S(2)}) collective-permute-start(bf16[576,128]{1,0:T(8,128)(2,1)} %bitcast.16), channel_id=1, source_target_pairs={{0,8},{1,9},{2,10},{3,11},{4,12},{5,13},{6,14},{7,15},{8,0},{9,1},... | collective-permute-start | bytes 442376 | tf_op jit(solution)/shard_map/ppermute | solution.py:34
  13.7 1.1 %pack.1 = (bf16[144,128]{1,0:T(8,128)(2,1)S(1)}, bf16[144,128]{1,0:T(8,128)(2,1)S(1)}, bf16[2,576,128]{2,1,0:T(8,128)(2,1)S(1)}, bf16[576,128]{1,0:T(8,128)(2,1)S(1)}) custom-call(s32[4,128]{1,0:T(4,128)} %bitcast.20, bf16[128,128]{1,0:T(8,128)(2,1)} %keys_hbm.1, f32[2,64]{1,0:T(2,128)} %weight_hbm.1, s32[2]{0:T(128)} %pos_hbm.1, ...), custom_call_target="tpu_custom_call" | custom-call | tf_op jit(solution)/shard_map/pack/pallas_call | solution.py:261
  14.9 1.6 %collective-permute-start.8 = (bf16[144,128]{1,0:T(8,128)(2,1)S(1)}, bf16[144,128]{1,0:T(8,128)(2,1)S(1)}, u32[]{:S(2)}, u32[]{:S(2)}) collective-permute-start(bf16[144,128]{1,0:T(8,128)(2,1)S(1)} %get-tuple-element.29.refs_11_.refs_6_), channel_id=1, source_target_pairs={{0,4},{1,5},{2,6},{3,7},{4,0},{5,1},{6,2},{7,3},{8,12},{9,13},{10,... | collective-permute-start | bytes 110600 | tf_op jit(solution)/shard_map/ppermute | solution.py:34
  16.5 0.3 collective-permute-start.9
  16.8 2.1 %collective-permute-done.8.refs_12_.refs_8_.refs_10_ = bf16[144,128]{1,0:T(8,128)(2,1)S(1)} collective-permute-done((bf16[144,128]{1,0:T(8,128)(2,1)S(1)}, bf16[144,128]{1,0:T(8,128)(2,1)S(1)}, u32[]{:S(2)}, u32[]{:S(2)}) %collective-permute-start.8) | collective-permute-done | bytes 36896 | tf_op jit(solution)/shard_map/ppermute | solution.py:34
  18.9 2.5 %collective-permute-start.6 = (bf16[576,128]{1,0:T(8,128)(2,1)}, bf16[576,128]{1,0:T(8,128)(2,1)S(1)}, u32[]{:S(2)}, u32[]{:S(2)}) collective-permute-start(bf16[576,128]{1,0:T(8,128)(2,1)} %bitcast.18), channel_id=1, source_target_pairs={{0,4},{1,5},{2,6},{3,7},{4,0},{5,1},{6,2},{7,3},{8,12},{9,13},{10,... | collective-permute-start | bytes 442376 | tf_op jit(solution)/shard_map/ppermute | solution.py:34
  21.4 1.9 %collective-permute-done.9.refs_13_.refs_7_ = bf16[144,128]{1,0:T(8,128)(2,1)S(1)} collective-permute-done((bf16[144,128]{1,0:T(8,128)(2,1)S(1)}, bf16[144,128]{1,0:T(8,128)(2,1)S(1)}, u32[]{:S(2)}, u32[]{:S(2)}) %collective-permute-start.9) | collective-permute-done | bytes 36896 | tf_op jit(solution)/shard_map/ppermute | solution.py:34
  23.3 1.5 %collective-permute-start.4 = (bf16[144,128]{1,0:T(8,128)(2,1)S(1)}, bf16[144,128]{1,0:T(8,128)(2,1)S(1)}, u32[]{:S(2)}, u32[]{:S(2)}) collective-permute-start(bf16[144,128]{1,0:T(8,128)(2,1)S(1)} %get-tuple-element.27.refs_4_), channel_id=1, source_target_pairs={{0,2},{1,3},{2,0},{3,1},{4,6},{5,7},{6,4},{7,5},{8,10},{9,11},{10,... | collective-permute-start | bytes 110600 | tf_op jit(solution)/shard_map/ppermute | solution.py:34
  24.8 0.0 collective-permute-done.7.refs_10_
  24.8 0.6 %collective-permute-start.10 = (bf16[576,128]{1,0:T(8,128)(2,1)S(1)}, bf16[576,128]{1,0:T(8,128)(2,1)S(1)}, u32[]{:S(2)}, u32[]{:S(2)}) collective-permute-start(bf16[576,128]{1,0:T(8,128)(2,1)S(1)} %collective-permute-done.7.refs_10_), channel_id=1, source_target_pairs={{0,4},{1,5},{2,6},{3,7},{4,0},{5,1},{6,2},{7,3},{8,12},{9,13},{10,... | collective-permute-start | bytes 442376 | tf_op jit(solution)/shard_map/ppermute | solution.py:34
  25.4 1.8 %collective-permute-done.4.refs_6_ = bf16[144,128]{1,0:T(8,128)(2,1)S(1)} collective-permute-done((bf16[144,128]{1,0:T(8,128)(2,1)S(1)}, bf16[144,128]{1,0:T(8,128)(2,1)S(1)}, u32[]{:S(2)}, u32[]{:S(2)}) %collective-permute-start.4) | collective-permute-done | bytes 36896 | tf_op jit(solution)/shard_map/ppermute | solution.py:34
  27.3 0.0 collective-permute-start.3
  27.3 1.2 %collective-permute-done.3.refs_5_ = bf16[144,128]{1,0:T(8,128)(2,1)S(1)} collective-permute-done((bf16[144,128]{1,0:T(8,128)(2,1)S(1)}, bf16[144,128]{1,0:T(8,128)(2,1)S(1)}, u32[]{:S(2)}, u32[]{:S(2)}) %collective-permute-start.3) | collective-permute-done | bytes 36896 | tf_op jit(solution)/shard_map/ppermute | solution.py:34
  28.5 0.2 collective-permute-start.5
  28.6 1.1 %collective-permute-done.5.refs_7_ = bf16[144,128]{1,0:T(8,128)(2,1)S(1)} collective-permute-done((bf16[144,128]{1,0:T(8,128)(2,1)S(1)}, bf16[144,128]{1,0:T(8,128)(2,1)S(1)}, u32[]{:S(2)}, u32[]{:S(2)}) %collective-permute-start.5) | collective-permute-done | bytes 36896 | tf_op jit(solution)/shard_map/ppermute | solution.py:34
  29.7 0.7 %collective-permute-start.11 = (bf16[144,128]{1,0:T(8,128)(2,1)S(1)}, bf16[144,128]{1,0:T(8,128)(2,1)S(1)}, u32[]{:S(2)}, u32[]{:S(2)}) collective-permute-start(bf16[144,128]{1,0:T(8,128)(2,1)S(1)} %collective-permute-done.9.refs_13_.refs_7_), channel_id=1, source_target_pairs={{0,4},{1,5},{2,6},{3,7},{4,0},{5,1},{6,2},{7,3},{8,12},{9,13},{10,... | collective-permute-start | bytes 110600 | tf_op jit(solution)/shard_map/ppermute | solution.py:34
  30.3 0.0 collective-permute-done.6.refs_9_
  30.3 0.0 collective-permute-done.refs_1_
  30.3 0.0 collective-permute-done.2.refs_3_
  30.3 1.6 %shard_map.94 = (f32[8,128,384]{2,1,0:T(8,128)S(1)}, f32[8,384]{1,0:T(8,128)S(1)}, f32[4,4,128]{2,1,0:T(4,128)S(1)}, bf16[1024,576]{1,0:T(8,128)(2,1)S(1)}, bf16...) custom-call(bf16[2,576,128]{2,1,0:T(8,128)(2,1)S(1)} %get-tuple-element.26.refs_0_, ...), custom_call_target="tpu_custom_call" | custom-call | flops 452984832 | bytes 4790272 | tf_op jit(solution)/shard_map/pallas_call | solution.py:20
  31.9 1.7 %collective-permute-done.11.refs_5_.refs_9_.refs_11_ = bf16[144,128]{1,0:T(8,128)(2,1)S(1)} collective-permute-done((bf16[144,128]{1,0:T(8,128)(2,1)S(1)}, bf16[144,128]{1,0:T(8,128)(2,1)S(1)}, u32[]{:S(2)}, u32[]{:S(2)}) %collective-permute-start.11) | collective-permute-done | bytes 36896 | tf_op jit(solution)/shard_map/ppermute | solution.py:34
  33.6 0.0 collective-permute-done.10.refs_4_
  33.6 0.7 %shard_map.95 = (f32[8,128,128]{2,1,0:T(8,128)S(1)}, f32[8,128]{1,0:T(8,128)S(1)}, f32[4,4,128]{2,1,0:T(4,128)S(1)}) custom-call(bf16[1024,576]{1,0:T(8,128)(2,1)S(1)} %get-tuple-element.31.refs_0_, bf16[512,128]{1,0:T(8,128)(2,1)S(1)} %get-tuple-element.32.refs_1_.refs_2_, f32[64,8]{1,0:T(8,128)S(1)} %get-tuple-element.33.refs_2_.refs_3_, ...), custom_call_target="tpu_custom_call" | custom-call | flops 150994944 | bytes 2037760 | tf_op jit(solution)/shard_map/pallas_call | solution.py:20
  34.3 1.6 %collective-permute-start.12 = (f32[4,4,128]{2,1,0:T(4,128)S(1)}, f32[4,4,128]{2,1,0:T(4,128)S(1)}, u32[]{:S(2)}, u32[]{:S(2)}) collective-permute-start(f32[4,4,128]{2,1,0:T(4,128)S(1)} %add.12), channel_id=1, source_target_pairs={{0,2},{1,3},{2,0},{3,1},{4,6},{5,7},{6,4},{7,5},{8,10},{9,11},{10,... | collective-permute-start | bytes 24584 | tf_op jit(solution)/shard_map/ppermute | solution.py:34
  35.9 2.1 %collective-permute-done.12 = f32[4,4,128]{2,1,0:T(4,128)S(1)} collective-permute-done((f32[4,4,128]{2,1,0:T(4,128)S(1)}, f32[4,4,128]{2,1,0:T(4,128)S(1)}, u32[]{:S(2)}, u32[]{:S(2)}) %collective-permute-start.12) | collective-permute-done | bytes 8224 | tf_op jit(solution)/shard_map/ppermute | solution.py:34
  38.1 0.1 collective-permute-start.13
  38.1 1.2 %collective-permute-done.13.refs_1_ = f32[4,4,128]{2,1,0:T(4,128)S(1)} collective-permute-done((f32[4,4,128]{2,1,0:T(4,128)S(1)}, f32[4,4,128]{2,1,0:T(4,128)S(1)}, u32[]{:S(2)}, u32[]{:S(2)}) %collective-permute-start.13) | collective-permute-done | bytes 8224 | tf_op jit(solution)/shard_map/ppermute | solution.py:34
  39.3 1.1 %shard_map.96 = (bf16[2,128,128]{2,1,0:T(8,128)(2,1)S(1)}, bf16[512,256]{1,0:T(8,128)(2,1)S(1)}, f32[64,128]{1,0:T(8,128)S(1)}) custom-call(f32[4,4,128]{2,1,0:T(4,128)S(1)} %maximum_add_fusion.refs_0_, f32[4,4,128]{2,1,0:T(4,128)S(1)} %collective-permute-done.13.refs_1_, bf16[512,128]{1,0:T(8,128)(2,1)S(1)} %get-tuple-element.32.refs_1_.refs_2_, ...), custom_call_target="tpu_custom_call" | custom-call | flops 100663296 | bytes 2697216 | tf_op jit(solution)/shard_map/pallas_call | solution.py:20
  40.4 0.7 %collective-permute-start.14 = (bf16[2,128,128]{2,1,0:T(8,128)(2,1)S(1)}, bf16[2,128,128]{2,1,0:T(8,128)(2,1)S(1)}, u32[]{:S(2)}, u32[]{:S(2)}) collective-permute-start(bf16[2,128,128]{2,1,0:T(8,128)(2,1)S(1)} %get-tuple-element.43), channel_id=1, source_target_pairs={{0,4},{1,5},{2,6},{3,7},{4,0},{5,1},{6,2},{7,3},{8,12},{9,13},{10,... | collective-permute-start | bytes 196616 | tf_op jit(solution)/shard_map/ppermute | solution.py:34
  41.1 1.1 %shard_map.97 = (f32[2,128,128]{2,1,0:T(8,128)S(1)}, f32[2,136,128]{2,1,0:T(8,128)S(1)}, f32[2,136,128]{2,1,0:T(8,128)S(1)}) custom-call(f32[4,4,128]{2,1,0:T(4,128)S(1)} %maximum_add_fusion.refs_0_, f32[4,4,128]{2,1,0:T(4,128)S(1)} %collective-permute-done.13.refs_1_, bf16[512,128]{1,0:T(8,128)(2,1)S(1)} %get-tuple-element.32.refs_1_.refs_2_, ...), custom_call_target="tpu_custom_call" | custom-call | flops 100663296 | bytes 2586624 | tf_op jit(solution)/shard_map/pallas_call | solution.py:20
  42.2 1.6 %collective-permute-start.16 = (f32[2,136,128]{2,1,0:T(8,128)S(1)}, f32[2,136,128]{2,1,0:T(8,128)S(1)}, u32[]{:S(2)}, u32[]{:S(2)}) collective-permute-start(f32[2,136,128]{2,1,0:T(8,128)S(1)} %get-tuple-element.45), channel_id=1, source_target_pairs={{0,2},{1,3},{2,0},{3,1},{4,6},{5,7},{6,4},{7,5},{8,10},{9,11},{10,... | collective-permute-start | bytes 417800 | tf_op jit(solution)/shard_map/ppermute | solution.py:34
  43.7 1.0 %collective-permute-done.14 = bf16[2,128,128]{2,1,0:T(8,128)(2,1)S(1)} collective-permute-done((bf16[2,128,128]{2,1,0:T(8,128)(2,1)S(1)}, bf16[2,128,128]{2,1,0:T(8,128)(2,1)S(1)}, u32[]{:S(2)}, u32[]{:S(2)}) %collective-permute-start.14) | collective-permute-done | bytes 65568 | tf_op jit(solution)/shard_map/ppermute | solution.py:34
  44.7 2.5 %collective-permute-start.15 = (bf16[1,128,128]{2,1,0:T(8,128)(2,1)S(1)}, bf16[1,128,128]{2,1,0:T(8,128)(2,1)S(1)}, u32[]{:S(2)}, u32[]{:S(2)}) collective-permute-start(bf16[1,128,128]{2,1,0:T(8,128)(2,1)S(1)} %slice.41), channel_id=1, source_target_pairs={{0,8},{1,9},{2,10},{3,11},{4,12},{5,13},{6,14},{7,15},{8,0},{9,1},... | collective-permute-start | bytes 98312 | tf_op jit(solution)/shard_map/ppermute | solution.py:34
  47.2 0.5 %collective-permute-done.16 = f32[2,136,128]{2,1,0:T(8,128)S(1)} collective-permute-done((f32[2,136,128]{2,1,0:T(8,128)S(1)}, f32[2,136,128]{2,1,0:T(8,128)S(1)}, u32[]{:S(2)}, u32[]{:S(2)}) %collective-permute-start.16) | collective-permute-done | bytes 139296 | tf_op jit(solution)/shard_map/ppermute | solution.py:34
  47.7 0.1 collective-permute-start.17
  47.8 1.8 %collective-permute-done.15 = bf16[1,128,128]{2,1,0:T(8,128)(2,1)S(1)} collective-permute-done((bf16[1,128,128]{2,1,0:T(8,128)(2,1)S(1)}, bf16[1,128,128]{2,1,0:T(8,128)(2,1)S(1)}, u32[]{:S(2)}, u32[]{:S(2)}) %collective-permute-start.15) | collective-permute-done | bytes 32800 | tf_op jit(solution)/shard_map/ppermute | solution.py:34
  49.6 0.0 collective-permute-done.17.row_got_ref
  49.6 0.7 %shard_map.98 = (f32[128,128]{1,0:T(8,128)}, f32[2,64]{1,0:T(2,128)}, f32[128,128]{1,0:T(8,128)}) custom-call(f32[128,128]{1,0:T(8,128)S(1)} %slice_bitcast_fusion.2.key_ref, bf16[128,128]{1,0:T(8,128)(2,1)S(1)} %bitcast.12, f32[136,128]{1,0:T(8,128)S(1)} %get-tuple-element.50.row_ref, f32[136,128]{1,0:T(8,128)S(1)} %collective-permute-done.17.row_got_ref), custom_call_target="tpu_custom_call" | custom-call | bytes 369152 | tf_op jit(solution)/shard_map/pallas_call | solution.py:20
  (8 shorter events, 0.1 us)
Async XLA Ops:
  0.6 10.2 %collective-permute-start.1 = (bf16[2,576,128]{2,1,0:T(8,128)(2,1)}, bf16[2,576,128]{2,1,0:T(8,128)(2,1)S(1)}, u32[]{:S(2)}, u32[]{:S(2)}) collective-permute-start(bf16[2,576,128]{2,1,0:T(8,128)(2,1)} %bitcast.13), channel_id=1, source_target_pairs={{0,2},{1,3},{2,0},{3,1},{4,6},{5,7},{6,4},{7,5},{8,10},{9,11},{10,... | collective-permute-start | bytes 884744 | tf_op jit(solution)/shard_map/ppermute | solution.py:34
  3.7 26.7 %collective-permute-start = (bf16[2,576,128]{2,1,0:T(8,128)(2,1)}, bf16[2,576,128]{2,1,0:T(8,128)(2,1)S(1)}, u32[]{:S(2)}, u32[]{:S(2)}) collective-permute-start(bf16[2,576,128]{2,1,0:T(8,128)(2,1)} %bitcast.14), channel_id=1, source_target_pairs={{0,1},{1,0},{2,3},{3,2},{4,5},{5,4},{6,7},{7,6},{8,9},{9,8},{10,11... | collective-permute-start | bytes 884744 | tf_op jit(solution)/shard_map/ppermute | solution.py:34
  10.9 19.5 %collective-permute-start.2 = (bf16[2,576,128]{2,1,0:T(8,128)(2,1)S(1)}, bf16[2,576,128]{2,1,0:T(8,128)(2,1)S(1)}, u32[]{:S(2)}, u32[]{:S(2)}) collective-permute-start(bf16[2,576,128]{2,1,0:T(8,128)(2,1)S(1)} %collective-permute-done.1.refs_2_), channel_id=1, source_target_pairs={{0,1},{1,0},{2,3},{3,2},{4,5},{5,4},{6,7},{7,6},{8,9},{9,8},{10,11... | collective-permute-start | bytes 884744 | tf_op jit(solution)/shard_map/ppermute | solution.py:34
  10.9 14.0 %collective-permute-start.7 = (bf16[576,128]{1,0:T(8,128)(2,1)}, bf16[576,128]{1,0:T(8,128)(2,1)S(1)}, u32[]{:S(2)}, u32[]{:S(2)}) collective-permute-start(bf16[576,128]{1,0:T(8,128)(2,1)} %bitcast.16), channel_id=1, source_target_pairs={{0,8},{1,9},{2,10},{3,11},{4,12},{5,13},{6,14},{7,15},{8,0},{9,1},... | collective-permute-start | bytes 442376 | tf_op jit(solution)/shard_map/ppermute | solution.py:34
  14.9 4.1 %collective-permute-start.8 = (bf16[144,128]{1,0:T(8,128)(2,1)S(1)}, bf16[144,128]{1,0:T(8,128)(2,1)S(1)}, u32[]{:S(2)}, u32[]{:S(2)}) collective-permute-start(bf16[144,128]{1,0:T(8,128)(2,1)S(1)} %get-tuple-element.29.refs_11_.refs_6_), channel_id=1, source_target_pairs={{0,4},{1,5},{2,6},{3,7},{4,0},{5,1},{6,2},{7,3},{8,12},{9,13},{10,... | collective-permute-start | bytes 110600 | tf_op jit(solution)/shard_map/ppermute | solution.py:34
  16.5 6.8 %collective-permute-start.9 = (bf16[144,128]{1,0:T(8,128)(2,1)S(1)}, bf16[144,128]{1,0:T(8,128)(2,1)S(1)}, u32[]{:S(2)}, u32[]{:S(2)}) collective-permute-start(bf16[144,128]{1,0:T(8,128)(2,1)S(1)} %get-tuple-element.29.refs_11_.refs_6_), channel_id=1, source_target_pairs={{0,8},{1,9},{2,10},{3,11},{4,12},{5,13},{6,14},{7,15},{8,0},{9,1},... | collective-permute-start | bytes 110600 | tf_op jit(solution)/shard_map/ppermute | solution.py:34
  18.9 11.4 %collective-permute-start.6 = (bf16[576,128]{1,0:T(8,128)(2,1)}, bf16[576,128]{1,0:T(8,128)(2,1)S(1)}, u32[]{:S(2)}, u32[]{:S(2)}) collective-permute-start(bf16[576,128]{1,0:T(8,128)(2,1)} %bitcast.18), channel_id=1, source_target_pairs={{0,4},{1,5},{2,6},{3,7},{4,0},{5,1},{6,2},{7,3},{8,12},{9,13},{10,... | collective-permute-start | bytes 442376 | tf_op jit(solution)/shard_map/ppermute | solution.py:34
  23.3 4.0 %collective-permute-start.4 = (bf16[144,128]{1,0:T(8,128)(2,1)S(1)}, bf16[144,128]{1,0:T(8,128)(2,1)S(1)}, u32[]{:S(2)}, u32[]{:S(2)}) collective-permute-start(bf16[144,128]{1,0:T(8,128)(2,1)S(1)} %get-tuple-element.27.refs_4_), channel_id=1, source_target_pairs={{0,2},{1,3},{2,0},{3,1},{4,6},{5,7},{6,4},{7,5},{8,10},{9,11},{10,... | collective-permute-start | bytes 110600 | tf_op jit(solution)/shard_map/ppermute | solution.py:34
  24.8 8.8 %collective-permute-start.10 = (bf16[576,128]{1,0:T(8,128)(2,1)S(1)}, bf16[576,128]{1,0:T(8,128)(2,1)S(1)}, u32[]{:S(2)}, u32[]{:S(2)}) collective-permute-start(bf16[576,128]{1,0:T(8,128)(2,1)S(1)} %collective-permute-done.7.refs_10_), channel_id=1, source_target_pairs={{0,4},{1,5},{2,6},{3,7},{4,0},{5,1},{6,2},{7,3},{8,12},{9,13},{10,... | collective-permute-start | bytes 442376 | tf_op jit(solution)/shard_map/ppermute | solution.py:34
  27.3 1.2 %collective-permute-start.3 = (bf16[144,128]{1,0:T(8,128)(2,1)S(1)}, bf16[144,128]{1,0:T(8,128)(2,1)S(1)}, u32[]{:S(2)}, u32[]{:S(2)}) collective-permute-start(bf16[144,128]{1,0:T(8,128)(2,1)S(1)} %get-tuple-element.27.refs_4_), channel_id=1, source_target_pairs={{0,1},{1,0},{2,3},{3,2},{4,5},{5,4},{6,7},{7,6},{8,9},{9,8},{10,11... | collective-permute-start | bytes 110600 | tf_op jit(solution)/shard_map/ppermute | solution.py:34
  28.5 1.2 %collective-permute-start.5 = (bf16[144,128]{1,0:T(8,128)(2,1)S(1)}, bf16[144,128]{1,0:T(8,128)(2,1)S(1)}, u32[]{:S(2)}, u32[]{:S(2)}) collective-permute-start(bf16[144,128]{1,0:T(8,128)(2,1)S(1)} %collective-permute-done.4.refs_6_), channel_id=1, source_target_pairs={{0,1},{1,0},{2,3},{3,2},{4,5},{5,4},{6,7},{7,6},{8,9},{9,8},{10,11... | collective-permute-start | bytes 110600 | tf_op jit(solution)/shard_map/ppermute | solution.py:34
  29.7 4.0 %collective-permute-start.11 = (bf16[144,128]{1,0:T(8,128)(2,1)S(1)}, bf16[144,128]{1,0:T(8,128)(2,1)S(1)}, u32[]{:S(2)}, u32[]{:S(2)}) collective-permute-start(bf16[144,128]{1,0:T(8,128)(2,1)S(1)} %collective-permute-done.9.refs_13_.refs_7_), channel_id=1, source_target_pairs={{0,4},{1,5},{2,6},{3,7},{4,0},{5,1},{6,2},{7,3},{8,12},{9,13},{10,... | collective-permute-start | bytes 110600 | tf_op jit(solution)/shard_map/ppermute | solution.py:34
  34.3 3.7 %collective-permute-start.12 = (f32[4,4,128]{2,1,0:T(4,128)S(1)}, f32[4,4,128]{2,1,0:T(4,128)S(1)}, u32[]{:S(2)}, u32[]{:S(2)}) collective-permute-start(f32[4,4,128]{2,1,0:T(4,128)S(1)} %add.12), channel_id=1, source_target_pairs={{0,2},{1,3},{2,0},{3,1},{4,6},{5,7},{6,4},{7,5},{8,10},{9,11},{10,... | collective-permute-start | bytes 24584 | tf_op jit(solution)/shard_map/ppermute | solution.py:34
  38.1 1.2 %collective-permute-start.13 = (f32[4,4,128]{2,1,0:T(4,128)S(1)}, f32[4,4,128]{2,1,0:T(4,128)S(1)}, u32[]{:S(2)}, u32[]{:S(2)}) collective-permute-start(f32[4,4,128]{2,1,0:T(4,128)S(1)} %maximum_add_fusion.refs_0_), channel_id=1, source_target_pairs={{0,1},{1,0},{2,3},{3,2},{4,5},{5,4},{6,7},{7,6},{8,9},{9,8},{10,11... | collective-permute-start | bytes 24584 | tf_op jit(solution)/shard_map/ppermute | solution.py:34
  40.4 4.3 %collective-permute-start.14 = (bf16[2,128,128]{2,1,0:T(8,128)(2,1)S(1)}, bf16[2,128,128]{2,1,0:T(8,128)(2,1)S(1)}, u32[]{:S(2)}, u32[]{:S(2)}) collective-permute-start(bf16[2,128,128]{2,1,0:T(8,128)(2,1)S(1)} %get-tuple-element.43), channel_id=1, source_target_pairs={{0,4},{1,5},{2,6},{3,7},{4,0},{5,1},{6,2},{7,3},{8,12},{9,13},{10,... | collective-permute-start | bytes 196616 | tf_op jit(solution)/shard_map/ppermute | solution.py:34
  42.2 5.5 %collective-permute-start.16 = (f32[2,136,128]{2,1,0:T(8,128)S(1)}, f32[2,136,128]{2,1,0:T(8,128)S(1)}, u32[]{:S(2)}, u32[]{:S(2)}) collective-permute-start(f32[2,136,128]{2,1,0:T(8,128)S(1)} %get-tuple-element.45), channel_id=1, source_target_pairs={{0,2},{1,3},{2,0},{3,1},{4,6},{5,7},{6,4},{7,5},{8,10},{9,11},{10,... | collective-permute-start | bytes 417800 | tf_op jit(solution)/shard_map/ppermute | solution.py:34
  44.7 4.9 %collective-permute-start.15 = (bf16[1,128,128]{2,1,0:T(8,128)(2,1)S(1)}, bf16[1,128,128]{2,1,0:T(8,128)(2,1)S(1)}, u32[]{:S(2)}, u32[]{:S(2)}) collective-permute-start(bf16[1,128,128]{2,1,0:T(8,128)(2,1)S(1)} %slice.41), channel_id=1, source_target_pairs={{0,8},{1,9},{2,10},{3,11},{4,12},{5,13},{6,14},{7,15},{8,0},{9,1},... | collective-permute-start | bytes 98312 | tf_op jit(solution)/shard_map/ppermute | solution.py:34
  47.7 1.9 %collective-permute-start.17 = (f32[136,128]{1,0:T(8,128)S(1)}, f32[136,128]{1,0:T(8,128)S(1)}, u32[]{:S(2)}, u32[]{:S(2)}) collective-permute-start(f32[136,128]{1,0:T(8,128)S(1)} %get-tuple-element.49), channel_id=1, source_target_pairs={{0,1},{1,0},{2,3},{3,2},{4,5},{5,4},{6,7},{7,6},{8,9},{9,8},{10,11... | collective-permute-start | bytes 208904 | tf_op jit(solution)/shard_map/ppermute | solution.py:34
where the time goes:
time: 50.5 us; the launch traced here: 50.3 us
  waiting for transfers between devices  23.5 us (47%)
  starting transfers between devices  19.8 us (39%)
  Pallas kernels  6.23 us (12%)
  between operations  0.72 us (1%)
    ppermute x18, waiting for transfers between devices, swap(): return lax.ppermute(array, 'ctx', [(i, i ^ mask) for i in range(count)])  23.5 us
    ppermute x18, starting transfers between devices, swap(): return lax.ppermute(array, 'ctx', [(i, i ^ mask) for i in range(count)])  19.8 us
    pallas_call x5, Pallas kernels, kernel_call(): pl.pallas_call(kernel, out_shape=tuple(shapes), scratch_shapes=list(scrat...  5.1 us
    pallas_call x1, Pallas kernels, body(): pl.pallas_call(pack_kernel, out_shape=(struct((own_keys + 16, own_keys),...  1.13 us
  transfers between devices with their start and end apart: 18, of which 12 were waited for; matrix products, arithmetic and copies ran while one was open for 0% of the time, Pallas kernels for 8%

commit v1 on v0

--- a/solution.py
+++ b/solution.py
@@ -160,21 +160,24 @@
         )
 
 
-def grad_kernel(key_total, row_parts, places, last, *refs):
+def grad_kernel(key_total, row_parts, places, early_count, *refs):
     count = 1 + max(n for n, _ in places)
     near_ref, far_ref, flat_ref, column_ref = refs[:4]
     exps, indexes = refs[4 : 4 + count], refs[4 + count : 4 + 2 * count]
     refs = refs[4 + 2 * count :]
     blocks, refs = refs[: len(places)], refs[len(places) :]
+    last = early_count > 0
     if last:
         early_dots, early_columns = refs[:2]
-        early_blocks, refs = refs[2 : 2 + len(places)], refs[2 + len(places) :]
-        key_ref, keep_ref, send_ref, dots_ref, total_ref = refs
+        early_blocks, refs = refs[2 : 2 + early_count], refs[2 + early_count :]
+        key_refs, refs = refs[: len(places)], refs[len(places) :]
+        keep_ref, send_ref, dots_ref, total_ref = refs
     else:
-        key_ref, dots_ref, columns_ref, total_ref = refs
+        key_refs, refs = refs[: len(places)], refs[len(places) :]
+        dots_ref, columns_ref, total_ref = refs
     rows, own_rows = total_ref.shape[0], total_ref.shape[0] // row_parts
     index_heads, index_width = column_ref.shape[0], flat_ref.shape[1]
-    head_count, own_keys = exps[0].shape[1], key_ref.shape[1]
+    head_count, own_keys = exps[0].shape[1], key_refs[0].shape[0]
     index_scale = float(index_heads * index_width) ** (-0.5)
     ikeys = jnp.concatenate([b[:own_keys, :] for b in blocks], axis=0)
     flat = flat_ref[...]
@@ -209,8 +212,8 @@
         dots_ref[t * index_heads : (t + 1) * index_heads, :] = grad_dots
     grad_dots = dots_ref[...]
     key_grad = contract(grad_dots, flat, (0, 0))
-    for k in range(len(blocks)):
-        key_ref[k] = key_grad[k * own_keys : (k + 1) * own_keys, :].astype(key_ref.dtype)
+    for k, key_ref in enumerate(key_refs):
+        key_ref[...] = key_grad[k * own_keys : (k + 1) * own_keys, :].astype(key_ref.dtype)
     if not last:
         columns_ref[...] = columns
         return
@@ -224,10 +227,14 @@
         out[at, lines : lines + own_rows, :] = weights[r * own_rows : (r + 1) * own_rows, :]
 
 
-def finish_kernel(key_ref, key_got_ref, row_ref, row_got_ref, query_ref, weight_ref, key_out_ref):
+def finish_kernel(parts, *refs):
+    key_refs, (row_ref, row_got_ref, query_ref, weight_ref, key_out_ref) = refs[:parts], refs[parts:]
     lines = query_ref.shape[0]
     own_rows, index_heads = weight_ref.shape
-    key_out_ref[...] = key_ref[...] + key_got_ref[...].astype(f32)
+    total = key_refs[0][...].astype(f32)
+    for ref in key_refs[1:]:
+        total = total + ref[...].astype(f32)
+    key_out_ref[...] = total
     query_ref[...] = row_ref[:lines, :] + row_got_ref[:lines, :]
     tail = slice(lines, lines + own_rows)
     weight_ref[...] = (row_ref[tail, :] + row_got_ref[tail, :])[:, :index_heads]
@@ -278,7 +285,9 @@
     )(*(pltpu.with_memory_space_constraint(x, pltpu.HBM) for x in sources))
     codes = swap_gather(codes, row_parts, key_parts, count)
     codes[0] = codes_own
-    blocks = swap_gather(key_pack, row_parts, key_parts, count)
+    blocks = [key_pack]
+    for k in range(1, key_parts):
+        blocks.append(swap(key_pack, row_parts * k, count))
     queries = swap_gather(main_raw, 1, row_parts, count)
     queries[0] = main_own
     iqueries = swap_gather(index_own, 1, row_parts, count)
@@ -328,12 +337,10 @@
 
     place = {k: (n, p * own_keys) for n, piece in enumerate(pieces) for p, k in enumerate(piece)}
     teams = [list(range(key_parts))] if key_parts <= step else pieces
-    even, odd, keep, send = [], [], None, None
+    found, keep, send = {}, None, None
     for ids in teams:
-        half = len(ids) // 2
         early = None
-        for part in (1, 0):
-            mine = ids[part::2]
+        for part, mine in enumerate((ids[3:], ids[:3])):
             used = sorted({place[k][0] for k in mine})
             places = tuple((used.index(place[k][0]), place[k][1]) for k in mine)
             operands = (
@@ -344,50 +351,55 @@
                 *(indexes[n] for n in used),
                 *(blocks[k] for k in mine),
             )
-            shapes = (struct((half, own_keys, index_width), bf16 if part else f32),)
-            more = struct((rows * index_heads, half * own_keys), bf16)
+            shapes = tuple(
+                struct((own_keys, index_width), bf16 if k % 2 else f32) for k in mine
+            )
+            more = struct((rows * index_heads, len(mine) * own_keys), bf16)
             scratch = (pltpu.VMEM((rows, head_count), f32),)
-            if part:
+            if part == 0:
                 shapes += (more, struct((index_heads, LANES), f32))
             else:
-                operands += (*early, *(blocks[k] for k in ids[1::2]))
+                operands += (*early, *(blocks[k] for k in ids[3:]))
                 shapes += (struct((row_parts // 2, tall, index_width), f32),) * 2
                 scratch = (pltpu.VMEM(more.shape, bf16), *scratch)
             out = kernel_call(
-                functools.partial(grad_kernel, key_total, row_parts, places, not part),
+                functools.partial(grad_kernel, key_total, row_parts, places, len(ids[3:]) * part),
                 shapes,
                 operands,
                 scratch=scratch,
-                flops=6 * rows * index_heads * index_width * half * own_keys,
+                flops=6 * rows * index_heads * index_width * len(mine) * own_keys,
             )
-            if part:
-                odd.append(out[0])
-                early = out[1:]
+            found.update(zip(mine, out))
+            if part == 0:
+                early = out[len(mine) :]
             else:
-                even.append(out[0])
-                keep = out[1] if keep is None else keep + out[1]
-                send = out[2] if send is None else send + out[2]
-    key_sum = even[0] if len(even) == 1 else jnp.concatenate(even)
-    key_send = odd[0] if len(odd) == 1 else jnp.concatenate(odd)
-
-    key_got = swap(key_send, row_parts, count)
+                keep = out[-2] if keep is None else keep + out[-2]
+                send = out[-1] if send is None else send + out[-1]
+    pick = lambda n: jnp.stack([found[k] for k in range(n, key_parts, 4)]) if key_parts > 4 else found[n]
+    key_got = swap(pick(3), row_parts, count)
+    near_got = swap(pick(1), row_parts, count)
     row_got = swap(send, row_parts // 2, count)
-    bit = 2
+    key_sum = (pick(2) + key_got.astype(f32)).astype(bf16)
+    key_got = swap(key_sum, 2 * row_parts, count)
+    key_sums = (pick(0), near_got, key_got)
+    bit = 4
     while bit < key_parts:
-        key_sum = key_sum + key_got.astype(f32)
+        key_sum = sum(x.astype(f32) for x in key_sums)
         key_got = swap(key_sum[1::2].astype(bf16), row_parts * bit, count)
-        key_sum = key_sum[0::2]
+        key_sums = (key_sum[0::2], key_got)
         bit *= 2
+    if key_parts > 4:
+        key_sums = tuple(x[0] for x in key_sums)
     row_sum = keep + row_got
     row_got = swap(row_sum[1], 1, count)
     grad_query, grad_weight, key_grad = kernel_call(
-        finish_kernel,
+        functools.partial(finish_kernel, len(key_sums)),
         (
             struct((lines, index_width), f32),
             struct((own_rows, index_heads), f32),
             struct((own_keys, index_width), f32),
         ),
-        (key_sum[0], key_got[0], row_sum[0], row_got),
+        (*key_sums, row_sum[0], row_got),
     )
     return grad_query.reshape(own_rows, index_heads, index_width), grad_weight, key_grad
 

time: 50.5 us -> 55.1 us (1.091)
  starting transfers between devices: 19.8 us -> 23 us
  waiting for transfers between devices: 23.5 us -> 24.7 us
    ppermute x18 -> x19, starting transfers between devices: 19.8 us -> 23 us  [swap(): return lax.ppermute(array, 'ctx', [(i, i ^ mask) for i in range(count)])]
    ppermute x18 -> x19, waiting for transfers between devices: 23.5 us -> 24.7 us  [swap(): return lax.ppermute(array, 'ctx', [(i, i ^ mask) for i in range(count)])]
  transfers between devices with their start and end apart: 18 -> 19, of which waited for: 12 -> 11; matrix products, arithmetic and copies ran while one was open for 0% -> 0% of each run, Pallas kernels for 8% -> 5%
where the time goes in v1:
time: 55.1 us; the launch traced here: 54.9 us
  waiting for transfers between devices  24.7 us (45%)
  starting transfers between devices  23 us (42%)
  Pallas kernels  6.33 us (11%)
  between operations  0.73 us (1%)
    ppermute x19, waiting for transfers between devices, swap(): return lax.ppermute(array, 'ctx', [(i, i ^ mask) for i in range(count)])  24.7 us
    ppermute x19, starting transfers between devices, swap(): return lax.ppermute(array, 'ctx', [(i, i ^ mask) for i in range(count)])  23 us
    pallas_call x5, Pallas kernels, kernel_call(): pl.pallas_call(kernel, out_shape=tuple(shapes), scratch_shapes=list(scrat...  5.2 us
    pallas_call x1, Pallas kernels, body(): pl.pallas_call(pack_kernel, out_shape=(struct((own_keys + 16, own_keys),...  1.13 us
  transfers between devices with their start and end apart: 19, of which 11 were waited for; matrix products, arithmetic and copies ran while one was open for 0% of the time, Pallas kernels for 5%

profile of v1, /device:TPU:0, one launch (start us, length us, event | category | flops | bytes accessed | tf_op | source)
XLA Modules:
  0.0 54.9 jit_solution(15567024511749096561)
XLA Ops:
  0.6 3.0 %collective-permute-start.1 = (bf16[2,576,128]{2,1,0:T(8,128)(2,1)}, bf16[2,576,128]{2,1,0:T(8,128)(2,1)S(1)}, u32[]{:S(2)}, u32[]{:S(2)}) collective-permute-start(bf16[2,576,128]{2,1,0:T(8,128)(2,1)} %bitcast.9), channel_id=1, source_target_pairs={{0,2},{1,3},{2,0},{3,1},{4,6},{5,7},{6,4},{7,5},{8,10},{9,11},{10,... | collective-permute-start | bytes 884744 | tf_op jit(solution)/shard_map/ppermute | solution.py:34
  3.7 0.0 collective-permute-start
  3.7 7.2 %collective-permute-done.1.refs_2_ = bf16[2,576,128]{2,1,0:T(8,128)(2,1)S(1)} collective-permute-done((bf16[2,576,128]{2,1,0:T(8,128)(2,1)}, bf16[2,576,128]{2,1,0:T(8,128)(2,1)S(1)}, u32[]{:S(2)}, u32[]{:S(2)}) %collective-permute-start.1) | collective-permute-done | bytes 294944 | tf_op jit(solution)/shard_map/ppermute | solution.py:34
  10.9 0.0 collective-permute-start.2
  10.9 2.8 %collective-permute-start.7 = (bf16[576,128]{1,0:T(8,128)(2,1)}, bf16[576,128]{1,0:T(8,128)(2,1)S(1)}, u32[]{:S(2)}, u32[]{:S(2)}) collective-permute-start(bf16[576,128]{1,0:T(8,128)(2,1)} %bitcast.12), channel_id=1, source_target_pairs={{0,8},{1,9},{2,10},{3,11},{4,12},{5,13},{6,14},{7,15},{8,0},{9,1},... | collective-permute-start | bytes 442376 | tf_op jit(solution)/shard_map/ppermute | solution.py:34
  13.7 1.1 %pack.1 = (bf16[144,128]{1,0:T(8,128)(2,1)S(1)}, bf16[144,128]{1,0:T(8,128)(2,1)S(1)}, bf16[2,576,128]{2,1,0:T(8,128)(2,1)S(1)}, bf16[576,128]{1,0:T(8,128)(2,1)S(1)}) custom-call(s32[4,128]{1,0:T(4,128)} %bitcast.16, bf16[128,128]{1,0:T(8,128)(2,1)} %keys_hbm.1, f32[2,64]{1,0:T(2,128)} %weight_hbm.1, s32[2]{0:T(128)} %pos_hbm.1, ...), custom_call_target="tpu_custom_call" | custom-call | tf_op jit(solution)/shard_map/pack/pallas_call | solution.py:268
  14.9 1.6 %collective-permute-start.8 = (bf16[144,128]{1,0:T(8,128)(2,1)S(1)}, bf16[144,128]{1,0:T(8,128)(2,1)S(1)}, u32[]{:S(2)}, u32[]{:S(2)}) collective-permute-start(bf16[144,128]{1,0:T(8,128)(2,1)S(1)} %get-tuple-element.31.refs_11_.refs_6_), channel_id=1, source_target_pairs={{0,4},{1,5},{2,6},{3,7},{4,0},{5,1},{6,2},{7,3},{8,12},{9,13},{10,... | collective-permute-start | bytes 110600 | tf_op jit(solution)/shard_map/ppermute | solution.py:34
  16.5 0.3 collective-permute-start.9
  16.8 2.1 %collective-permute-done.8.refs_12_.refs_7_ = bf16[144,128]{1,0:T(8,128)(2,1)S(1)} collective-permute-done((bf16[144,128]{1,0:T(8,128)(2,1)S(1)}, bf16[144,128]{1,0:T(8,128)(2,1)S(1)}, u32[]{:S(2)}, u32[]{:S(2)}) %collective-permute-start.8) | collective-permute-done | bytes 36896 | tf_op jit(solution)/shard_map/ppermute | solution.py:34
  18.9 2.5 %collective-permute-start.6 = (bf16[576,128]{1,0:T(8,128)(2,1)}, bf16[576,128]{1,0:T(8,128)(2,1)S(1)}, u32[]{:S(2)}, u32[]{:S(2)}) collective-permute-start(bf16[576,128]{1,0:T(8,128)(2,1)} %bitcast.14), channel_id=1, source_target_pairs={{0,4},{1,5},{2,6},{3,7},{4,0},{5,1},{6,2},{7,3},{8,12},{9,13},{10,... | collective-permute-start | bytes 442376 | tf_op jit(solution)/shard_map/ppermute | solution.py:34
  21.4 1.9 %collective-permute-done.9.refs_13_.refs_8_ = bf16[144,128]{1,0:T(8,128)(2,1)S(1)} collective-permute-done((bf16[144,128]{1,0:T(8,128)(2,1)S(1)}, bf16[144,128]{1,0:T(8,128)(2,1)S(1)}, u32[]{:S(2)}, u32[]{:S(2)}) %collective-permute-start.9) | collective-permute-done | bytes 36896 | tf_op jit(solution)/shard_map/ppermute | solution.py:34
  23.3 1.5 %collective-permute-start.4 = (bf16[144,128]{1,0:T(8,128)(2,1)S(1)}, bf16[144,128]{1,0:T(8,128)(2,1)S(1)}, u32[]{:S(2)}, u32[]{:S(2)}) collective-permute-start(bf16[144,128]{1,0:T(8,128)(2,1)S(1)} %get-tuple-element.29.refs_4_), channel_id=1, source_target_pairs={{0,2},{1,3},{2,0},{3,1},{4,6},{5,7},{6,4},{7,5},{8,10},{9,11},{10,... | collective-permute-start | bytes 110600 | tf_op jit(solution)/shard_map/ppermute | solution.py:34
  24.8 0.0 collective-permute-done.7.refs_10_
  24.8 0.6 %collective-permute-start.10 = (bf16[576,128]{1,0:T(8,128)(2,1)S(1)}, bf16[576,128]{1,0:T(8,128)(2,1)S(1)}, u32[]{:S(2)}, u32[]{:S(2)}) collective-permute-start(bf16[576,128]{1,0:T(8,128)(2,1)S(1)} %collective-permute-done.7.refs_10_), channel_id=1, source_target_pairs={{0,4},{1,5},{2,6},{3,7},{4,0},{5,1},{6,2},{7,3},{8,12},{9,13},{10,... | collective-permute-start | bytes 442376 | tf_op jit(solution)/shard_map/ppermute | solution.py:34
  25.4 1.8 %collective-permute-done.4.refs_6_ = bf16[144,128]{1,0:T(8,128)(2,1)S(1)} collective-permute-done((bf16[144,128]{1,0:T(8,128)(2,1)S(1)}, bf16[144,128]{1,0:T(8,128)(2,1)S(1)}, u32[]{:S(2)}, u32[]{:S(2)}) %collective-permute-start.4) | collective-permute-done | bytes 36896 | tf_op jit(solution)/shard_map/ppermute | solution.py:34
  27.2 0.0 collective-permute-start.3
  27.3 1.2 %collective-permute-done.3.refs_5_ = bf16[144,128]{1,0:T(8,128)(2,1)S(1)} collective-permute-done((bf16[144,128]{1,0:T(8,128)(2,1)S(1)}, bf16[144,128]{1,0:T(8,128)(2,1)S(1)}, u32[]{:S(2)}, u32[]{:S(2)}) %collective-permute-start.3) | collective-permute-done | bytes 36896 | tf_op jit(solution)/shard_map/ppermute | solution.py:34
  28.5 0.2 collective-permute-start.5
  28.6 1.1 %collective-permute-done.5.refs_7_ = bf16[144,128]{1,0:T(8,128)(2,1)S(1)} collective-permute-done((bf16[144,128]{1,0:T(8,128)(2,1)S(1)}, bf16[144,128]{1,0:T(8,128)(2,1)S(1)}, u32[]{:S(2)}, u32[]{:S(2)}) %collective-permute-start.5) | collective-permute-done | bytes 36896 | tf_op jit(solution)/shard_map/ppermute | solution.py:34
  29.7 3.4 %collective-permute-start.11 = (bf16[144,128]{1,0:T(8,128)(2,1)S(1)}, bf16[144,128]{1,0:T(8,128)(2,1)S(1)}, u32[]{:S(2)}, u32[]{:S(2)}) collective-permute-start(bf16[144,128]{1,0:T(8,128)(2,1)S(1)} %get-tuple-element.31.refs_11_.refs_6_), channel_id=1, source_target_pairs={{0,12},{1,13},{2,14},{3,15},{4,8},{5,9},{6,10},{7,11},{8,4},{9,5},... | collective-permute-start | bytes 110600 | tf_op jit(solution)/shard_map/ppermute | solution.py:34
  33.1 0.0 collective-permute-done.6.refs_9_
  33.1 0.0 collective-permute-done.refs_1_
  33.1 0.0 collective-permute-done.2.refs_3_
  33.1 1.6 %shard_map.94 = (f32[8,128,384]{2,1,0:T(8,128)S(1)}, f32[8,384]{1,0:T(8,128)S(1)}, f32[4,4,128]{2,1,0:T(4,128)S(1)}, bf16[1024,576]{1,0:T(8,128)(2,1)S(1)}, bf16...) custom-call(bf16[2,576,128]{2,1,0:T(8,128)(2,1)S(1)} %get-tuple-element.28.refs_0_, ...), custom_call_target="tpu_custom_call" | custom-call | flops 452984832 | bytes 4790272 | tf_op jit(solution)/shard_map/pallas_call | solution.py:20
  34.7 0.7 %collective-permute-done.11.refs_5_.refs_6_.refs_11_ = bf16[144,128]{1,0:T(8,128)(2,1)S(1)} collective-permute-done((bf16[144,128]{1,0:T(8,128)(2,1)S(1)}, bf16[144,128]{1,0:T(8,128)(2,1)S(1)}, u32[]{:S(2)}, u32[]{:S(2)}) %collective-permute-start.11) | collective-permute-done | bytes 36896 | tf_op jit(solution)/shard_map/ppermute | solution.py:34
  35.4 0.0 collective-permute-done.10.refs_4_
  35.4 0.7 %shard_map.95 = (f32[8,128,128]{2,1,0:T(8,128)S(1)}, f32[8,128]{1,0:T(8,128)S(1)}, f32[4,4,128]{2,1,0:T(4,128)S(1)}) custom-call(bf16[1024,576]{1,0:T(8,128)(2,1)S(1)} %get-tuple-element.33.refs_0_, bf16[512,128]{1,0:T(8,128)(2,1)S(1)} %get-tuple-element.34.refs_1_.refs_2_, f32[64,8]{1,0:T(8,128)S(1)} %get-tuple-element.35.refs_2_.refs_3_, ...), custom_call_target="tpu_custom_call" | custom-call | flops 150994944 | bytes 2037760 | tf_op jit(solution)/shard_map/pallas_call | solution.py:20
  36.1 1.6 %collective-permute-start.12 = (f32[4,4,128]{2,1,0:T(4,128)S(1)}, f32[4,4,128]{2,1,0:T(4,128)S(1)}, u32[]{:S(2)}, u32[]{:S(2)}) collective-permute-start(f32[4,4,128]{2,1,0:T(4,128)S(1)} %add.12), channel_id=1, source_target_pairs={{0,2},{1,3},{2,0},{3,1},{4,6},{5,7},{6,4},{7,5},{8,10},{9,11},{10,... | collective-permute-start | bytes 24584 | tf_op jit(solution)/shard_map/ppermute | solution.py:34
  37.7 2.1 %collective-permute-done.12 = f32[4,4,128]{2,1,0:T(4,128)S(1)} collective-permute-done((f32[4,4,128]{2,1,0:T(4,128)S(1)}, f32[4,4,128]{2,1,0:T(4,128)S(1)}, u32[]{:S(2)}, u32[]{:S(2)}) %collective-permute-start.12) | collective-permute-done | bytes 8224 | tf_op jit(solution)/shard_map/ppermute | solution.py:34
  39.9 0.1 collective-permute-start.13
  39.9 1.2 %collective-permute-done.13.refs_1_ = f32[4,4,128]{2,1,0:T(4,128)S(1)} collective-permute-done((f32[4,4,128]{2,1,0:T(4,128)S(1)}, f32[4,4,128]{2,1,0:T(4,128)S(1)}, u32[]{:S(2)}, u32[]{:S(2)}) %collective-permute-start.13) | collective-permute-done | bytes 8224 | tf_op jit(solution)/shard_map/ppermute | solution.py:34
  41.1 1.0 %shard_map.96 = (bf16[128,128]{1,0:T(8,128)(2,1)S(1)}, bf16[512,128]{1,0:T(8,128)(2,1)S(1)}, f32[64,128]{1,0:T(8,128)S(1)}) custom-call(f32[4,4,128]{2,1,0:T(4,128)S(1)} %maximum_add_fusion.refs_0_, f32[4,4,128]{2,1,0:T(4,128)S(1)} %collective-permute-done.13.refs_1_, bf16[512,128]{1,0:T(8,128)(2,1)S(1)} %get-tuple-element.34.refs_1_.refs_2_, ...), custom_call_target="tpu_custom_call" | custom-call | flops 50331648 | bytes 911360 | tf_op jit(solution)/shard_map/pallas_call | solution.py:20
  42.1 1.2 %shard_map.97 = (f32[128,128]{1,0:T(8,128)S(1)}, bf16[128,128]{1,0:T(8,128)(2,1)S(1)}, f32[128,128]{1,0:T(8,128)S(1)}, f32[2,136,128]{2,1,0:T(8,128)S(1)}, f32[2,136,128]{2,1,0:T(8,128)S(1)}) custom-call(f32[4,4,128]{2,1,0:T(4,128)S(1)} %maximum_add_fusion.refs_0_, f32[4,4,128]{2,1,0:T(4,128)S(1)} %collective-permute-done.13.refs_1_, ...), custom_call_target="tpu_custom_call" | custom-call | flops 150994944 | bytes 2488320 | tf_op jit(solution)/shard_map/pallas_call | solution.py:20
  43.4 1.6 %collective-permute-start.17 = (f32[2,136,128]{2,1,0:T(8,128)S(1)}, f32[2,136,128]{2,1,0:T(8,128)S(1)}, u32[]{:S(2)}, u32[]{:S(2)}) collective-permute-start(f32[2,136,128]{2,1,0:T(8,128)S(1)} %get-tuple-element.49), channel_id=1, source_target_pairs={{0,2},{1,3},{2,0},{3,1},{4,6},{5,7},{6,4},{7,5},{8,10},{9,11},{10,... | collective-permute-start | bytes 417800 | tf_op jit(solution)/shard_map/ppermute | solution.py:34
  45.0 0.0 collective-permute-start.15
  45.0 2.0 %collective-permute-start.14 = (bf16[128,128]{1,0:T(8,128)(2,1)S(1)}, bf16[128,128]{1,0:T(8,128)(2,1)S(1)}, u32[]{:S(2)}, u32[]{:S(2)}) collective-permute-start(bf16[128,128]{1,0:T(8,128)(2,1)S(1)} %get-tuple-element.45), channel_id=1, source_target_pairs={{0,4},{1,5},{2,6},{3,7},{4,0},{5,1},{6,2},{7,3},{8,12},{9,13},{10,... | collective-permute-start | bytes 98312 | tf_op jit(solution)/shard_map/ppermute | solution.py:34
  47.0 2.2 %collective-permute-done.17 = f32[2,136,128]{2,1,0:T(8,128)S(1)} collective-permute-done((f32[2,136,128]{2,1,0:T(8,128)S(1)}, f32[2,136,128]{2,1,0:T(8,128)S(1)}, u32[]{:S(2)}, u32[]{:S(2)}) %collective-permute-start.17) | collective-permute-done | bytes 139296 | tf_op jit(solution)/shard_map/ppermute | solution.py:34
  49.2 0.1 collective-permute-start.18
  49.3 0.0 collective-permute-done.15
  49.3 1.6 %collective-permute-start.16 = (bf16[128,128]{1,0:T(8,128)(2,1)S(1)}, bf16[128,128]{1,0:T(8,128)(2,1)S(1)}, u32[]{:S(2)}, u32[]{:S(2)}) collective-permute-start(bf16[128,128]{1,0:T(8,128)(2,1)S(1)} %add_convert_fusion), channel_id=1, source_target_pairs={{0,8},{1,9},{2,10},{3,11},{4,12},{5,13},{6,14},{7,15},{8,0},{9,1},... | collective-permute-start | bytes 98312 | tf_op jit(solution)/shard_map/ppermute | solution.py:34
  50.9 0.0 collective-permute-done.14.refs_1_
  50.9 3.3 %collective-permute-done.16.refs_2_ = bf16[128,128]{1,0:T(8,128)(2,1)S(1)} collective-permute-done((bf16[128,128]{1,0:T(8,128)(2,1)S(1)}, bf16[128,128]{1,0:T(8,128)(2,1)S(1)}, u32[]{:S(2)}, u32[]{:S(2)}) %collective-permute-start.16) | collective-permute-done | bytes 32800 | tf_op jit(solution)/shard_map/ppermute | solution.py:34
  54.2 0.0 collective-permute-done.18.refs_4_
  54.2 0.7 %shard_map.98 = (f32[128,128]{1,0:T(8,128)}, f32[2,64]{1,0:T(2,128)}, f32[128,128]{1,0:T(8,128)}) custom-call(f32[128,128]{1,0:T(8,128)S(1)} %get-tuple-element.44.refs_0_, bf16[128,128]{1,0:T(8,128)(2,1)S(1)} %collective-permute-done.14.refs_1_, bf16[128,128]{1,0:T(8,128)(2,1)S(1)} %collective-permute-done.16.refs_2_, ...), custom_call_target="tpu_custom_call" | custom-call | bytes 401920 | tf_op jit(solution)/shard_map/pallas_call | solution.py:20
  (6 shorter events, 0.1 us)
Async XLA Ops:
  0.6 10.2 %collective-permute-start.1 = (bf16[2,576,128]{2,1,0:T(8,128)(2,1)}, bf16[2,576,128]{2,1,0:T(8,128)(2,1)S(1)}, u32[]{:S(2)}, u32[]{:S(2)}) collective-permute-start(bf16[2,576,128]{2,1,0:T(8,128)(2,1)} %bitcast.9), channel_id=1, source_target_pairs={{0,2},{1,3},{2,0},{3,1},{4,6},{5,7},{6,4},{7,5},{8,10},{9,11},{10,... | collective-permute-start | bytes 884744 | tf_op jit(solution)/shard_map/ppermute | solution.py:34
  3.7 29.5 %collective-permute-start = (bf16[2,576,128]{2,1,0:T(8,128)(2,1)}, bf16[2,576,128]{2,1,0:T(8,128)(2,1)S(1)}, u32[]{:S(2)}, u32[]{:S(2)}) collective-permute-start(bf16[2,576,128]{2,1,0:T(8,128)(2,1)} %bitcast.10), channel_id=1, source_target_pairs={{0,1},{1,0},{2,3},{3,2},{4,5},{5,4},{6,7},{7,6},{8,9},{9,8},{10,11... | collective-permute-start | bytes 884744 | tf_op jit(solution)/shard_map/ppermute | solution.py:34
  10.9 22.2 %collective-permute-start.2 = (bf16[2,576,128]{2,1,0:T(8,128)(2,1)S(1)}, bf16[2,576,128]{2,1,0:T(8,128)(2,1)S(1)}, u32[]{:S(2)}, u32[]{:S(2)}) collective-permute-start(bf16[2,576,128]{2,1,0:T(8,128)(2,1)S(1)} %collective-permute-done.1.refs_2_), channel_id=1, source_target_pairs={{0,1},{1,0},{2,3},{3,2},{4,5},{5,4},{6,7},{7,6},{8,9},{9,8},{10,11... | collective-permute-start | bytes 884744 | tf_op jit(solution)/shard_map/ppermute | solution.py:34
  10.9 14.0 %collective-permute-start.7 = (bf16[576,128]{1,0:T(8,128)(2,1)}, bf16[576,128]{1,0:T(8,128)(2,1)S(1)}, u32[]{:S(2)}, u32[]{:S(2)}) collective-permute-start(bf16[576,128]{1,0:T(8,128)(2,1)} %bitcast.12), channel_id=1, source_target_pairs={{0,8},{1,9},{2,10},{3,11},{4,12},{5,13},{6,14},{7,15},{8,0},{9,1},... | collective-permute-start | bytes 442376 | tf_op jit(solution)/shard_map/ppermute | solution.py:34
  14.9 4.1 %collective-permute-start.8 = (bf16[144,128]{1,0:T(8,128)(2,1)S(1)}, bf16[144,128]{1,0:T(8,128)(2,1)S(1)}, u32[]{:S(2)}, u32[]{:S(2)}) collective-permute-start(bf16[144,128]{1,0:T(8,128)(2,1)S(1)} %get-tuple-element.31.refs_11_.refs_6_), channel_id=1, source_target_pairs={{0,4},{1,5},{2,6},{3,7},{4,0},{5,1},{6,2},{7,3},{8,12},{9,13},{10,... | collective-permute-start | bytes 110600 | tf_op jit(solution)/shard_map/ppermute | solution.py:34
  16.5 6.8 %collective-permute-start.9 = (bf16[144,128]{1,0:T(8,128)(2,1)S(1)}, bf16[144,128]{1,0:T(8,128)(2,1)S(1)}, u32[]{:S(2)}, u32[]{:S(2)}) collective-permute-start(bf16[144,128]{1,0:T(8,128)(2,1)S(1)} %get-tuple-element.31.refs_11_.refs_6_), channel_id=1, source_target_pairs={{0,8},{1,9},{2,10},{3,11},{4,12},{5,13},{6,14},{7,15},{8,0},{9,1},... | collective-permute-start | bytes 110600 | tf_op jit(solution)/shard_map/ppermute | solution.py:34
  18.9 14.2 %collective-permute-start.6 = (bf16[576,128]{1,0:T(8,128)(2,1)}, bf16[576,128]{1,0:T(8,128)(2,1)S(1)}, u32[]{:S(2)}, u32[]{:S(2)}) collective-permute-start(bf16[576,128]{1,0:T(8,128)(2,1)} %bitcast.14), channel_id=1, source_target_pairs={{0,4},{1,5},{2,6},{3,7},{4,0},{5,1},{6,2},{7,3},{8,12},{9,13},{10,... | collective-permute-start | bytes 442376 | tf_op jit(solution)/shard_map/ppermute | solution.py:34
  23.3 4.0 %collective-permute-start.4 = (bf16[144,128]{1,0:T(8,128)(2,1)S(1)}, bf16[144,128]{1,0:T(8,128)(2,1)S(1)}, u32[]{:S(2)}, u32[]{:S(2)}) collective-permute-start(bf16[144,128]{1,0:T(8,128)(2,1)S(1)} %get-tuple-element.29.refs_4_), channel_id=1, source_target_pairs={{0,2},{1,3},{2,0},{3,1},{4,6},{5,7},{6,4},{7,5},{8,10},{9,11},{10,... | collective-permute-start | bytes 110600 | tf_op jit(solution)/shard_map/ppermute | solution.py:34
  24.8 10.6 %collective-permute-start.10 = (bf16[576,128]{1,0:T(8,128)(2,1)S(1)}, bf16[576,128]{1,0:T(8,128)(2,1)S(1)}, u32[]{:S(2)}, u32[]{:S(2)}) collective-permute-start(bf16[576,128]{1,0:T(8,128)(2,1)S(1)} %collective-permute-done.7.refs_10_), channel_id=1, source_target_pairs={{0,4},{1,5},{2,6},{3,7},{4,0},{5,1},{6,2},{7,3},{8,12},{9,13},{10,... | collective-permute-start | bytes 442376 | tf_op jit(solution)/shard_map/ppermute | solution.py:34
  27.2 1.2 %collective-permute-start.3 = (bf16[144,128]{1,0:T(8,128)(2,1)S(1)}, bf16[144,128]{1,0:T(8,128)(2,1)S(1)}, u32[]{:S(2)}, u32[]{:S(2)}) collective-permute-start(bf16[144,128]{1,0:T(8,128)(2,1)S(1)} %get-tuple-element.29.refs_4_), channel_id=1, source_target_pairs={{0,1},{1,0},{2,3},{3,2},{4,5},{5,4},{6,7},{7,6},{8,9},{9,8},{10,11... | collective-permute-start | bytes 110600 | tf_op jit(solution)/shard_map/ppermute | solution.py:34
  28.5 1.2 %collective-permute-start.5 = (bf16[144,128]{1,0:T(8,128)(2,1)S(1)}, bf16[144,128]{1,0:T(8,128)(2,1)S(1)}, u32[]{:S(2)}, u32[]{:S(2)}) collective-permute-start(bf16[144,128]{1,0:T(8,128)(2,1)S(1)} %collective-permute-done.4.refs_6_), channel_id=1, source_target_pairs={{0,1},{1,0},{2,3},{3,2},{4,5},{5,4},{6,7},{7,6},{8,9},{9,8},{10,11... | collective-permute-start | bytes 110600 | tf_op jit(solution)/shard_map/ppermute | solution.py:34
  29.7 5.8 %collective-permute-start.11 = (bf16[144,128]{1,0:T(8,128)(2,1)S(1)}, bf16[144,128]{1,0:T(8,128)(2,1)S(1)}, u32[]{:S(2)}, u32[]{:S(2)}) collective-permute-start(bf16[144,128]{1,0:T(8,128)(2,1)S(1)} %get-tuple-element.31.refs_11_.refs_6_), channel_id=1, source_target_pairs={{0,12},{1,13},{2,14},{3,15},{4,8},{5,9},{6,10},{7,11},{8,4},{9,5},... | collective-permute-start | bytes 110600 | tf_op jit(solution)/shard_map/ppermute | solution.py:34
  36.1 3.7 %collective-permute-start.12 = (f32[4,4,128]{2,1,0:T(4,128)S(1)}, f32[4,4,128]{2,1,0:T(4,128)S(1)}, u32[]{:S(2)}, u32[]{:S(2)}) collective-permute-start(f32[4,4,128]{2,1,0:T(4,128)S(1)} %add.12), channel_id=1, source_target_pairs={{0,2},{1,3},{2,0},{3,1},{4,6},{5,7},{6,4},{7,5},{8,10},{9,11},{10,... | collective-permute-start | bytes 24584 | tf_op jit(solution)/shard_map/ppermute | solution.py:34
  39.9 1.2 %collective-permute-start.13 = (f32[4,4,128]{2,1,0:T(4,128)S(1)}, f32[4,4,128]{2,1,0:T(4,128)S(1)}, u32[]{:S(2)}, u32[]{:S(2)}) collective-permute-start(f32[4,4,128]{2,1,0:T(4,128)S(1)} %maximum_add_fusion.refs_0_), channel_id=1, source_target_pairs={{0,1},{1,0},{2,3},{3,2},{4,5},{5,4},{6,7},{7,6},{8,9},{9,8},{10,11... | collective-permute-start | bytes 24584 | tf_op jit(solution)/shard_map/ppermute | solution.py:34
  43.4 5.8 %collective-permute-start.17 = (f32[2,136,128]{2,1,0:T(8,128)S(1)}, f32[2,136,128]{2,1,0:T(8,128)S(1)}, u32[]{:S(2)}, u32[]{:S(2)}) collective-permute-start(f32[2,136,128]{2,1,0:T(8,128)S(1)} %get-tuple-element.49), channel_id=1, source_target_pairs={{0,2},{1,3},{2,0},{3,1},{4,6},{5,7},{6,4},{7,5},{8,10},{9,11},{10,... | collective-permute-start | bytes 417800 | tf_op jit(solution)/shard_map/ppermute | solution.py:34
  45.0 4.3 %collective-permute-start.15 = (bf16[128,128]{1,0:T(8,128)(2,1)S(1)}, bf16[128,128]{1,0:T(8,128)(2,1)S(1)}, u32[]{:S(2)}, u32[]{:S(2)}) collective-permute-start(bf16[128,128]{1,0:T(8,128)(2,1)S(1)} %get-tuple-element.47), channel_id=1, source_target_pairs={{0,4},{1,5},{2,6},{3,7},{4,0},{5,1},{6,2},{7,3},{8,12},{9,13},{10,... | collective-permute-start | bytes 98312 | tf_op jit(solution)/shard_map/ppermute | solution.py:34
  45.0 5.9 %collective-permute-start.14 = (bf16[128,128]{1,0:T(8,128)(2,1)S(1)}, bf16[128,128]{1,0:T(8,128)(2,1)S(1)}, u32[]{:S(2)}, u32[]{:S(2)}) collective-permute-start(bf16[128,128]{1,0:T(8,128)(2,1)S(1)} %get-tuple-element.45), channel_id=1, source_target_pairs={{0,4},{1,5},{2,6},{3,7},{4,0},{5,1},{6,2},{7,3},{8,12},{9,13},{10,... | collective-permute-start | bytes 98312 | tf_op jit(solution)/shard_map/ppermute | solution.py:34
  49.2 5.0 %collective-permute-start.18 = (f32[136,128]{1,0:T(8,128)S(1)}, f32[136,128]{1,0:T(8,128)S(1)}, u32[]{:S(2)}, u32[]{:S(2)}) collective-permute-start(f32[136,128]{1,0:T(8,128)S(1)} %get-tuple-element.53), channel_id=1, source_target_pairs={{0,1},{1,0},{2,3},{3,2},{4,5},{5,4},{6,7},{7,6},{8,9},{9,8},{10,11... | collective-permute-start | bytes 208904 | tf_op jit(solution)/shard_map/ppermute | solution.py:34
  49.3 4.9 %collective-permute-start.16 = (bf16[128,128]{1,0:T(8,128)(2,1)S(1)}, bf16[128,128]{1,0:T(8,128)(2,1)S(1)}, u32[]{:S(2)}, u32[]{:S(2)}) collective-permute-start(bf16[128,128]{1,0:T(8,128)(2,1)S(1)} %add_convert_fusion), channel_id=1, source_target_pairs={{0,8},{1,9},{2,10},{3,11},{4,12},{5,13},{6,14},{7,15},{8,0},{9,1},... | collective-permute-start | bytes 98312 | tf_op jit(solution)/shard_map/ppermute | solution.py:34

commit v2 on v1

--- a/solution.py
+++ b/solution.py
@@ -221,10 +221,12 @@
     grad_query = contract(grad_dots, ikeys, (1, 0)) + contract(early_dots[...], early_keys, (1, 0))
     weights = jnp.transpose(jnp.concatenate([columns, jnp.zeros_like(columns)], axis=0)[:LANES])
     lines = own_rows * index_heads
+    weights = jnp.concatenate([weights, jnp.zeros((16, LANES), f32)], axis=0)
     for r in range(row_parts):
         out, at = (keep_ref, r) if r < row_parts // 2 else (send_ref, r - row_parts // 2)
-        out[at, :lines, :] = grad_query[r * lines : (r + 1) * lines, :]
-        out[at, lines : lines + own_rows, :] = weights[r * own_rows : (r + 1) * own_rows, :]
+        out[at, :lines, :] = grad_query[r * lines : (r + 1) * lines, :].astype(out.dtype)
+        tail = weights[r * own_rows : r * own_rows + out.shape[1] - lines, :]
+        out[at, lines:, :] = tail.astype(out.dtype)
 
 
 def finish_kernel(parts, *refs):
@@ -250,7 +252,7 @@
     key_total = own_keys * count
     rows = own_rows * row_parts
     lines = own_rows * index_heads
-    tall = lines + 8
+    tall = lines + 16
     struct = jax.ShapeDtypeStruct
 
     codes = key_codes.T
@@ -285,9 +287,7 @@
     )(*(pltpu.with_memory_space_constraint(x, pltpu.HBM) for x in sources))
     codes = swap_gather(codes, row_parts, key_parts, count)
     codes[0] = codes_own
-    blocks = [key_pack]
-    for k in range(1, key_parts):
-        blocks.append(swap(key_pack, row_parts * k, count))
+    blocks = swap_gather(key_pack, row_parts, key_parts, count)
     queries = swap_gather(main_raw, 1, row_parts, count)
     queries[0] = main_own
     iqueries = swap_gather(index_own, 1, row_parts, count)
@@ -360,7 +360,9 @@
                 shapes += (more, struct((index_heads, LANES), f32))
             else:
                 operands += (*early, *(blocks[k] for k in ids[3:]))
-                shapes += (struct((row_parts // 2, tall, index_width), f32),) * 2
+                shapes += tuple(
+                    struct((row_parts // 2, tall, index_width), kind) for kind in (f32, bf16)
+                )
                 scratch = (pltpu.VMEM(more.shape, bf16), *scratch)
             out = kernel_call(
                 functools.partial(grad_kernel, key_total, row_parts, places, len(ids[3:]) * part),
@@ -390,7 +392,7 @@
         bit *= 2
     if key_parts > 4:
         key_sums = tuple(x[0] for x in key_sums)
-    row_sum = keep + row_got
+    row_sum = keep + row_got.astype(f32)
     row_got = swap(row_sum[1], 1, count)
     grad_query, grad_weight, key_grad = kernel_call(
         functools.partial(finish_kernel, len(key_sums)),

time: 55.1 us -> 53.9 us (0.978)
  starting transfers between devices: 23 us -> 21.2 us
  waiting for transfers between devices: 24.7 us -> 25.4 us
    ppermute x19, starting transfers between devices: 23 us -> 21.2 us  [swap(): return lax.ppermute(array, 'ctx', [(i, i ^ mask) for i in range(count)])]
    ppermute x19, waiting for transfers between devices: 24.7 us -> 25.4 us  [swap(): return lax.ppermute(array, 'ctx', [(i, i ^ mask) for i in range(count)])]
where the time goes in v2:
time: 53.9 us; the launch traced here: 53.7 us
  waiting for transfers between devices  25.4 us (47%)
  starting transfers between devices  21.2 us (39%)
  Pallas kernels  6.32 us (12%)
  between operations  0.71 us (1%)
    ppermute x19, waiting for transfers between devices, swap(): return lax.ppermute(array, 'ctx', [(i, i ^ mask) for i in range(count)])  25.4 us
    ppermute x19, starting transfers between devices, swap(): return lax.ppermute(array, 'ctx', [(i, i ^ mask) for i in range(count)])  21.2 us
    pallas_call x5, Pallas kernels, kernel_call(): pl.pallas_call(kernel, out_shape=tuple(shapes), scratch_shapes=list(scrat...  5.19 us
    pallas_call x1, Pallas kernels, body(): pl.pallas_call(pack_kernel, out_shape=(struct((own_keys + 16, own_keys),...  1.13 us
  transfers between devices with their start and end apart: 19, of which 11 were waited for; matrix products, arithmetic and copies ran while one was open for 0% of the time, Pallas kernels for 5%

profile of v2, /device:TPU:0, one launch (start us, length us, event | category | flops | bytes accessed | tf_op | source)
XLA Modules:
  0.0 53.7 jit_solution(9852345951540850000)
XLA Ops:
  0.6 3.0 %collective-permute-start.1 = (bf16[2,576,128]{2,1,0:T(8,128)(2,1)}, bf16[2,576,128]{2,1,0:T(8,128)(2,1)S(1)}, u32[]{:S(2)}, u32[]{:S(2)}) collective-permute-start(bf16[2,576,128]{2,1,0:T(8,128)(2,1)} %bitcast.9), channel_id=1, source_target_pairs={{0,2},{1,3},{2,0},{3,1},{4,6},{5,7},{6,4},{7,5},{8,10},{9,11},{10,... | collective-permute-start | bytes 884744 | tf_op jit(solution)/shard_map/ppermute | solution.py:34
  3.7 0.0 collective-permute-start
  3.7 7.2 %collective-permute-done.1.refs_2_ = bf16[2,576,128]{2,1,0:T(8,128)(2,1)S(1)} collective-permute-done((bf16[2,576,128]{2,1,0:T(8,128)(2,1)}, bf16[2,576,128]{2,1,0:T(8,128)(2,1)S(1)}, u32[]{:S(2)}, u32[]{:S(2)}) %collective-permute-start.1) | collective-permute-done | bytes 294944 | tf_op jit(solution)/shard_map/ppermute | solution.py:34
  10.9 0.0 collective-permute-start.2
  10.9 2.8 %collective-permute-start.7 = (bf16[576,128]{1,0:T(8,128)(2,1)}, bf16[576,128]{1,0:T(8,128)(2,1)S(1)}, u32[]{:S(2)}, u32[]{:S(2)}) collective-permute-start(bf16[576,128]{1,0:T(8,128)(2,1)} %bitcast.12), channel_id=1, source_target_pairs={{0,8},{1,9},{2,10},{3,11},{4,12},{5,13},{6,14},{7,15},{8,0},{9,1},... | collective-permute-start | bytes 442376 | tf_op jit(solution)/shard_map/ppermute | solution.py:34
  13.7 1.1 %pack.1 = (bf16[144,128]{1,0:T(8,128)(2,1)S(1)}, bf16[144,128]{1,0:T(8,128)(2,1)S(1)}, bf16[2,576,128]{2,1,0:T(8,128)(2,1)S(1)}, bf16[576,128]{1,0:T(8,128)(2,1)S(1)}) custom-call(s32[4,128]{1,0:T(4,128)} %bitcast.16, bf16[128,128]{1,0:T(8,128)(2,1)} %keys_hbm.1, f32[2,64]{1,0:T(2,128)} %weight_hbm.1, s32[2]{0:T(128)} %pos_hbm.1, ...), custom_call_target="tpu_custom_call" | custom-call | tf_op jit(solution)/shard_map/pack/pallas_call | solution.py:270
  14.9 0.2 collective-permute-start.9
  15.0 1.8 %collective-permute-start.8 = (bf16[144,128]{1,0:T(8,128)(2,1)S(1)}, bf16[144,128]{1,0:T(8,128)(2,1)S(1)}, u32[]{:S(2)}, u32[]{:S(2)}) collective-permute-start(bf16[144,128]{1,0:T(8,128)(2,1)S(1)} %get-tuple-element.31.refs_11_.refs_6_), channel_id=1, source_target_pairs={{0,4},{1,5},{2,6},{3,7},{4,0},{5,1},{6,2},{7,3},{8,12},{9,13},{10,... | collective-permute-start | bytes 110600 | tf_op jit(solution)/shard_map/ppermute | solution.py:34
  16.8 6.4 %collective-permute-done.9.refs_13_.refs_8_ = bf16[144,128]{1,0:T(8,128)(2,1)S(1)} collective-permute-done((bf16[144,128]{1,0:T(8,128)(2,1)S(1)}, bf16[144,128]{1,0:T(8,128)(2,1)S(1)}, u32[]{:S(2)}, u32[]{:S(2)}) %collective-permute-start.9) | collective-permute-done | bytes 36896 | tf_op jit(solution)/shard_map/ppermute | solution.py:34
  23.2 0.7 %collective-permute-start.6 = (bf16[576,128]{1,0:T(8,128)(2,1)}, bf16[576,128]{1,0:T(8,128)(2,1)S(1)}, u32[]{:S(2)}, u32[]{:S(2)}) collective-permute-start(bf16[576,128]{1,0:T(8,128)(2,1)} %bitcast.14), channel_id=1, source_target_pairs={{0,4},{1,5},{2,6},{3,7},{4,0},{5,1},{6,2},{7,3},{8,12},{9,13},{10,... | collective-permute-start | bytes 442376 | tf_op jit(solution)/shard_map/ppermute | solution.py:34
  23.9 0.0 collective-permute-done.8.refs_12_.refs_7_
  23.9 1.5 %collective-permute-start.4 = (bf16[144,128]{1,0:T(8,128)(2,1)S(1)}, bf16[144,128]{1,0:T(8,128)(2,1)S(1)}, u32[]{:S(2)}, u32[]{:S(2)}) collective-permute-start(bf16[144,128]{1,0:T(8,128)(2,1)S(1)} %get-tuple-element.29.refs_4_), channel_id=1, source_target_pairs={{0,2},{1,3},{2,0},{3,1},{4,6},{5,7},{6,4},{7,5},{8,10},{9,11},{10,... | collective-permute-start | bytes 110600 | tf_op jit(solution)/shard_map/ppermute | solution.py:34
  25.4 0.0 collective-permute-done.7.refs_10_
  25.4 1.3 %collective-permute-start.10 = (bf16[576,128]{1,0:T(8,128)(2,1)S(1)}, bf16[576,128]{1,0:T(8,128)(2,1)S(1)}, u32[]{:S(2)}, u32[]{:S(2)}) collective-permute-start(bf16[576,128]{1,0:T(8,128)(2,1)S(1)} %collective-permute-done.7.refs_10_), channel_id=1, source_target_pairs={{0,4},{1,5},{2,6},{3,7},{4,0},{5,1},{6,2},{7,3},{8,12},{9,13},{10,... | collective-permute-start | bytes 442376 | tf_op jit(solution)/shard_map/ppermute | solution.py:34
  26.8 1.1 %collective-permute-done.4.refs_6_ = bf16[144,128]{1,0:T(8,128)(2,1)S(1)} collective-permute-done((bf16[144,128]{1,0:T(8,128)(2,1)S(1)}, bf16[144,128]{1,0:T(8,128)(2,1)S(1)}, u32[]{:S(2)}, u32[]{:S(2)}) %collective-permute-start.4) | collective-permute-done | bytes 36896 | tf_op jit(solution)/shard_map/ppermute | solution.py:34
  27.9 0.0 collective-permute-start.3
  27.9 1.2 %collective-permute-done.3.refs_5_ = bf16[144,128]{1,0:T(8,128)(2,1)S(1)} collective-permute-done((bf16[144,128]{1,0:T(8,128)(2,1)S(1)}, bf16[144,128]{1,0:T(8,128)(2,1)S(1)}, u32[]{:S(2)}, u32[]{:S(2)}) %collective-permute-start.3) | collective-permute-done | bytes 36896 | tf_op jit(solution)/shard_map/ppermute | solution.py:34
  29.1 0.2 collective-permute-start.5
  29.3 1.1 %collective-permute-done.5.refs_7_ = bf16[144,128]{1,0:T(8,128)(2,1)S(1)} collective-permute-done((bf16[144,128]{1,0:T(8,128)(2,1)S(1)}, bf16[144,128]{1,0:T(8,128)(2,1)S(1)}, u32[]{:S(2)}, u32[]{:S(2)}) %collective-permute-start.5) | collective-permute-done | bytes 36896 | tf_op jit(solution)/shard_map/ppermute | solution.py:34
  30.3 1.3 %collective-permute-start.11 = (bf16[144,128]{1,0:T(8,128)(2,1)S(1)}, bf16[144,128]{1,0:T(8,128)(2,1)S(1)}, u32[]{:S(2)}, u32[]{:S(2)}) collective-permute-start(bf16[144,128]{1,0:T(8,128)(2,1)S(1)} %collective-permute-done.9.refs_13_.refs_8_), channel_id=1, source_target_pairs={{0,4},{1,5},{2,6},{3,7},{4,0},{5,1},{6,2},{7,3},{8,12},{9,13},{10,... | collective-permute-start | bytes 110600 | tf_op jit(solution)/shard_map/ppermute | solution.py:34
  31.6 0.0 collective-permute-done.6.refs_9_
  31.6 0.0 collective-permute-done.refs_1_
  31.6 0.0 collective-permute-done.2.refs_3_
  31.6 1.6 %shard_map.94 = (f32[8,128,384]{2,1,0:T(8,128)S(1)}, f32[8,384]{1,0:T(8,128)S(1)}, f32[4,4,128]{2,1,0:T(4,128)S(1)}, bf16[1024,576]{1,0:T(8,128)(2,1)S(1)}, bf16...) custom-call(bf16[2,576,128]{2,1,0:T(8,128)(2,1)S(1)} %get-tuple-element.28.refs_0_, ...), custom_call_target="tpu_custom_call" | custom-call | flops 452984832 | bytes 4790272 | tf_op jit(solution)/shard_map/pallas_call | solution.py:20
  33.2 1.1 %collective-permute-done.11.refs_5_.refs_6_.refs_11_ = bf16[144,128]{1,0:T(8,128)(2,1)S(1)} collective-permute-done((bf16[144,128]{1,0:T(8,128)(2,1)S(1)}, bf16[144,128]{1,0:T(8,128)(2,1)S(1)}, u32[]{:S(2)}, u32[]{:S(2)}) %collective-permute-start.11) | collective-permute-done | bytes 36896 | tf_op jit(solution)/shard_map/ppermute | solution.py:34
  34.3 0.0 collective-permute-done.10.refs_4_
  34.3 0.7 %shard_map.95 = (f32[8,128,128]{2,1,0:T(8,128)S(1)}, f32[8,128]{1,0:T(8,128)S(1)}, f32[4,4,128]{2,1,0:T(4,128)S(1)}) custom-call(bf16[1024,576]{1,0:T(8,128)(2,1)S(1)} %get-tuple-element.33.refs_0_, bf16[512,128]{1,0:T(8,128)(2,1)S(1)} %get-tuple-element.34.refs_1_.refs_2_, f32[64,8]{1,0:T(8,128)S(1)} %get-tuple-element.35.refs_2_.refs_3_, ...), custom_call_target="tpu_custom_call" | custom-call | flops 150994944 | bytes 2037760 | tf_op jit(solution)/shard_map/pallas_call | solution.py:20
  35.0 1.6 %collective-permute-start.12 = (f32[4,4,128]{2,1,0:T(4,128)S(1)}, f32[4,4,128]{2,1,0:T(4,128)S(1)}, u32[]{:S(2)}, u32[]{:S(2)}) collective-permute-start(f32[4,4,128]{2,1,0:T(4,128)S(1)} %add.12), channel_id=1, source_target_pairs={{0,2},{1,3},{2,0},{3,1},{4,6},{5,7},{6,4},{7,5},{8,10},{9,11},{10,... | collective-permute-start | bytes 24584 | tf_op jit(solution)/shard_map/ppermute | solution.py:34
  36.5 2.2 %collective-permute-done.12 = f32[4,4,128]{2,1,0:T(4,128)S(1)} collective-permute-done((f32[4,4,128]{2,1,0:T(4,128)S(1)}, f32[4,4,128]{2,1,0:T(4,128)S(1)}, u32[]{:S(2)}, u32[]{:S(2)}) %collective-permute-start.12) | collective-permute-done | bytes 8224 | tf_op jit(solution)/shard_map/ppermute | solution.py:34
  38.7 0.1 collective-permute-start.13
  38.8 1.2 %collective-permute-done.13.refs_1_ = f32[4,4,128]{2,1,0:T(4,128)S(1)} collective-permute-done((f32[4,4,128]{2,1,0:T(4,128)S(1)}, f32[4,4,128]{2,1,0:T(4,128)S(1)}, u32[]{:S(2)}, u32[]{:S(2)}) %collective-permute-start.13) | collective-permute-done | bytes 8224 | tf_op jit(solution)/shard_map/ppermute | solution.py:34
  40.0 1.0 %shard_map.96 = (bf16[128,128]{1,0:T(8,128)(2,1)S(1)}, bf16[512,128]{1,0:T(8,128)(2,1)S(1)}, f32[64,128]{1,0:T(8,128)S(1)}) custom-call(f32[4,4,128]{2,1,0:T(4,128)S(1)} %maximum_add_fusion.refs_0_, f32[4,4,128]{2,1,0:T(4,128)S(1)} %collective-permute-done.13.refs_1_, bf16[512,128]{1,0:T(8,128)(2,1)S(1)} %get-tuple-element.34.refs_1_.refs_2_, ...), custom_call_target="tpu_custom_call" | custom-call | flops 50331648 | bytes 911360 | tf_op jit(solution)/shard_map/pallas_call | solution.py:20
  41.0 1.2 %shard_map.97 = (f32[128,128]{1,0:T(8,128)S(1)}, bf16[128,128]{1,0:T(8,128)(2,1)S(1)}, f32[128,128]{1,0:T(8,128)S(1)}, f32[2,144,128]{2,1,0:T(8,128)S(1)}, bf16[2,144,128]{2,1,0:T(8,128)(2,1)S(1)}) custom-call(f32[4,4,128]{2,1,0:T(4,128)S(1)} %maximum_add_fusion.refs_0_, f32[4,4,128]{2,1,0:T(4,128)S(1)} %collective-permute-done.13.refs_1_, ...), custom_call_target="tpu_custom_call" | custom-call | flops 150994944 | bytes 2430976 | tf_op jit(solution)/shard_map/pallas_call | solution.py:20
  42.2 1.6 %collective-permute-start.17 = (bf16[2,144,128]{2,1,0:T(8,128)(2,1)S(1)}, bf16[2,144,128]{2,1,0:T(8,128)(2,1)S(1)}, u32[]{:S(2)}, u32[]{:S(2)}) collective-permute-start(bf16[2,144,128]{2,1,0:T(8,128)(2,1)S(1)} %get-tuple-element.49), channel_id=1, source_target_pairs={{0,2},{1,3},{2,0},{3,1},{4,6},{5,7},{6,4},{7,5},{8,10},{9,11},{10,... | collective-permute-start | bytes 221192 | tf_op jit(solution)/shard_map/ppermute | solution.py:34
  43.8 1.3 %collective-permute-start.15 = (bf16[128,128]{1,0:T(8,128)(2,1)S(1)}, bf16[128,128]{1,0:T(8,128)(2,1)S(1)}, u32[]{:S(2)}, u32[]{:S(2)}) collective-permute-start(bf16[128,128]{1,0:T(8,128)(2,1)S(1)} %get-tuple-element.47), channel_id=1, source_target_pairs={{0,4},{1,5},{2,6},{3,7},{4,0},{5,1},{6,2},{7,3},{8,12},{9,13},{10,... | collective-permute-start | bytes 98312 | tf_op jit(solution)/shard_map/ppermute | solution.py:34
  45.1 0.7 %collective-permute-start.14 = (bf16[128,128]{1,0:T(8,128)(2,1)S(1)}, bf16[128,128]{1,0:T(8,128)(2,1)S(1)}, u32[]{:S(2)}, u32[]{:S(2)}) collective-permute-start(bf16[128,128]{1,0:T(8,128)(2,1)S(1)} %get-tuple-element.45), channel_id=1, source_target_pairs={{0,4},{1,5},{2,6},{3,7},{4,0},{5,1},{6,2},{7,3},{8,12},{9,13},{10,... | collective-permute-start | bytes 98312 | tf_op jit(solution)/shard_map/ppermute | solution.py:34
  45.8 0.8 %collective-permute-done.17 = bf16[2,144,128]{2,1,0:T(8,128)(2,1)S(1)} collective-permute-done((bf16[2,144,128]{2,1,0:T(8,128)(2,1)S(1)}, bf16[2,144,128]{2,1,0:T(8,128)(2,1)S(1)}, u32[]{:S(2)}, u32[]{:S(2)}) %collective-permute-start.17) | collective-permute-done | bytes 73760 | tf_op jit(solution)/shard_map/ppermute | solution.py:34
  46.7 0.1 collective-permute-start.18
  46.8 1.3 %collective-permute-done.15 = bf16[128,128]{1,0:T(8,128)(2,1)S(1)} collective-permute-done((bf16[128,128]{1,0:T(8,128)(2,1)S(1)}, bf16[128,128]{1,0:T(8,128)(2,1)S(1)}, u32[]{:S(2)}, u32[]{:S(2)}) %collective-permute-start.15) | collective-permute-done | bytes 32800 | tf_op jit(solution)/shard_map/ppermute | solution.py:34
  48.0 3.1 %collective-permute-start.16 = (bf16[128,128]{1,0:T(8,128)(2,1)S(1)}, bf16[128,128]{1,0:T(8,128)(2,1)S(1)}, u32[]{:S(2)}, u32[]{:S(2)}) collective-permute-start(bf16[128,128]{1,0:T(8,128)(2,1)S(1)} %add_convert_fusion), channel_id=1, source_target_pairs={{0,8},{1,9},{2,10},{3,11},{4,12},{5,13},{6,14},{7,15},{8,0},{9,1},... | collective-permute-start | bytes 98312 | tf_op jit(solution)/shard_map/ppermute | solution.py:34
  51.1 0.0 collective-permute-done.14.refs_1_
  51.1 1.9 %collective-permute-done.16.refs_2_ = bf16[128,128]{1,0:T(8,128)(2,1)S(1)} collective-permute-done((bf16[128,128]{1,0:T(8,128)(2,1)S(1)}, bf16[128,128]{1,0:T(8,128)(2,1)S(1)}, u32[]{:S(2)}, u32[]{:S(2)}) %collective-permute-start.16) | collective-permute-done | bytes 32800 | tf_op jit(solution)/shard_map/ppermute | solution.py:34
  53.0 0.0 collective-permute-done.18.refs_4_
  53.0 0.7 %shard_map.98 = (f32[128,128]{1,0:T(8,128)}, f32[2,64]{1,0:T(2,128)}, f32[128,128]{1,0:T(8,128)}) custom-call(f32[128,128]{1,0:T(8,128)S(1)} %get-tuple-element.44.refs_0_, bf16[128,128]{1,0:T(8,128)(2,1)S(1)} %collective-permute-done.14.refs_1_, bf16[128,128]{1,0:T(8,128)(2,1)S(1)} %collective-permute-done.16.refs_2_, ...), custom_call_target="tpu_custom_call" | custom-call | bytes 410112 | tf_op jit(solution)/shard_map/pallas_call | solution.py:20
  (6 shorter events, 0.1 us)
Async XLA Ops:
  0.6 10.2 %collective-permute-start.1 = (bf16[2,576,128]{2,1,0:T(8,128)(2,1)}, bf16[2,576,128]{2,1,0:T(8,128)(2,1)S(1)}, u32[]{:S(2)}, u32[]{:S(2)}) collective-permute-start(bf16[2,576,128]{2,1,0:T(8,128)(2,1)} %bitcast.9), channel_id=1, source_target_pairs={{0,2},{1,3},{2,0},{3,1},{4,6},{5,7},{6,4},{7,5},{8,10},{9,11},{10,... | collective-permute-start | bytes 884744 | tf_op jit(solution)/shard_map/ppermute | solution.py:34
  3.7 28.0 %collective-permute-start = (bf16[2,576,128]{2,1,0:T(8,128)(2,1)}, bf16[2,576,128]{2,1,0:T(8,128)(2,1)S(1)}, u32[]{:S(2)}, u32[]{:S(2)}) collective-permute-start(bf16[2,576,128]{2,1,0:T(8,128)(2,1)} %bitcast.10), channel_id=1, source_target_pairs={{0,1},{1,0},{2,3},{3,2},{4,5},{5,4},{6,7},{7,6},{8,9},{9,8},{10,11... | collective-permute-start | bytes 884744 | tf_op jit(solution)/shard_map/ppermute | solution.py:34
  10.9 20.7 %collective-permute-start.2 = (bf16[2,576,128]{2,1,0:T(8,128)(2,1)S(1)}, bf16[2,576,128]{2,1,0:T(8,128)(2,1)S(1)}, u32[]{:S(2)}, u32[]{:S(2)}) collective-permute-start(bf16[2,576,128]{2,1,0:T(8,128)(2,1)S(1)} %collective-permute-done.1.refs_2_), channel_id=1, source_target_pairs={{0,1},{1,0},{2,3},{3,2},{4,5},{5,4},{6,7},{7,6},{8,9},{9,8},{10,11... | collective-permute-start | bytes 884744 | tf_op jit(solution)/shard_map/ppermute | solution.py:34
  10.9 14.6 %collective-permute-start.7 = (bf16[576,128]{1,0:T(8,128)(2,1)}, bf16[576,128]{1,0:T(8,128)(2,1)S(1)}, u32[]{:S(2)}, u32[]{:S(2)}) collective-permute-start(bf16[576,128]{1,0:T(8,128)(2,1)} %bitcast.12), channel_id=1, source_target_pairs={{0,8},{1,9},{2,10},{3,11},{4,12},{5,13},{6,14},{7,15},{8,0},{9,1},... | collective-permute-start | bytes 442376 | tf_op jit(solution)/shard_map/ppermute | solution.py:34
  14.9 8.3 %collective-permute-start.9 = (bf16[144,128]{1,0:T(8,128)(2,1)S(1)}, bf16[144,128]{1,0:T(8,128)(2,1)S(1)}, u32[]{:S(2)}, u32[]{:S(2)}) collective-permute-start(bf16[144,128]{1,0:T(8,128)(2,1)S(1)} %get-tuple-element.31.refs_11_.refs_6_), channel_id=1, source_target_pairs={{0,8},{1,9},{2,10},{3,11},{4,12},{5,13},{6,14},{7,15},{8,0},{9,1},... | collective-permute-start | bytes 110600 | tf_op jit(solution)/shard_map/ppermute | solution.py:34
  15.0 8.9 %collective-permute-start.8 = (bf16[144,128]{1,0:T(8,128)(2,1)S(1)}, bf16[144,128]{1,0:T(8,128)(2,1)S(1)}, u32[]{:S(2)}, u32[]{:S(2)}) collective-permute-start(bf16[144,128]{1,0:T(8,128)(2,1)S(1)} %get-tuple-element.31.refs_11_.refs_6_), channel_id=1, source_target_pairs={{0,4},{1,5},{2,6},{3,7},{4,0},{5,1},{6,2},{7,3},{8,12},{9,13},{10,... | collective-permute-start | bytes 110600 | tf_op jit(solution)/shard_map/ppermute | solution.py:34
  23.2 8.4 %collective-permute-start.6 = (bf16[576,128]{1,0:T(8,128)(2,1)}, bf16[576,128]{1,0:T(8,128)(2,1)S(1)}, u32[]{:S(2)}, u32[]{:S(2)}) collective-permute-start(bf16[576,128]{1,0:T(8,128)(2,1)} %bitcast.14), channel_id=1, source_target_pairs={{0,4},{1,5},{2,6},{3,7},{4,0},{5,1},{6,2},{7,3},{8,12},{9,13},{10,... | collective-permute-start | bytes 442376 | tf_op jit(solution)/shard_map/ppermute | solution.py:34
  23.9 4.0 %collective-permute-start.4 = (bf16[144,128]{1,0:T(8,128)(2,1)S(1)}, bf16[144,128]{1,0:T(8,128)(2,1)S(1)}, u32[]{:S(2)}, u32[]{:S(2)}) collective-permute-start(bf16[144,128]{1,0:T(8,128)(2,1)S(1)} %get-tuple-element.29.refs_4_), channel_id=1, source_target_pairs={{0,2},{1,3},{2,0},{3,1},{4,6},{5,7},{6,4},{7,5},{8,10},{9,11},{10,... | collective-permute-start | bytes 110600 | tf_op jit(solution)/shard_map/ppermute | solution.py:34
  25.4 8.9 %collective-permute-start.10 = (bf16[576,128]{1,0:T(8,128)(2,1)S(1)}, bf16[576,128]{1,0:T(8,128)(2,1)S(1)}, u32[]{:S(2)}, u32[]{:S(2)}) collective-permute-start(bf16[576,128]{1,0:T(8,128)(2,1)S(1)} %collective-permute-done.7.refs_10_), channel_id=1, source_target_pairs={{0,4},{1,5},{2,6},{3,7},{4,0},{5,1},{6,2},{7,3},{8,12},{9,13},{10,... | collective-permute-start | bytes 442376 | tf_op jit(solution)/shard_map/ppermute | solution.py:34
  27.9 1.2 %collective-permute-start.3 = (bf16[144,128]{1,0:T(8,128)(2,1)S(1)}, bf16[144,128]{1,0:T(8,128)(2,1)S(1)}, u32[]{:S(2)}, u32[]{:S(2)}) collective-permute-start(bf16[144,128]{1,0:T(8,128)(2,1)S(1)} %get-tuple-element.29.refs_4_), channel_id=1, source_target_pairs={{0,1},{1,0},{2,3},{3,2},{4,5},{5,4},{6,7},{7,6},{8,9},{9,8},{10,11... | collective-permute-start | bytes 110600 | tf_op jit(solution)/shard_map/ppermute | solution.py:34
  29.1 1.2 %collective-permute-start.5 = (bf16[144,128]{1,0:T(8,128)(2,1)S(1)}, bf16[144,128]{1,0:T(8,128)(2,1)S(1)}, u32[]{:S(2)}, u32[]{:S(2)}) collective-permute-start(bf16[144,128]{1,0:T(8,128)(2,1)S(1)} %collective-permute-done.4.refs_6_), channel_id=1, source_target_pairs={{0,1},{1,0},{2,3},{3,2},{4,5},{5,4},{6,7},{7,6},{8,9},{9,8},{10,11... | collective-permute-start | bytes 110600 | tf_op jit(solution)/shard_map/ppermute | solution.py:34
  30.3 4.0 %collective-permute-start.11 = (bf16[144,128]{1,0:T(8,128)(2,1)S(1)}, bf16[144,128]{1,0:T(8,128)(2,1)S(1)}, u32[]{:S(2)}, u32[]{:S(2)}) collective-permute-start(bf16[144,128]{1,0:T(8,128)(2,1)S(1)} %collective-permute-done.9.refs_13_.refs_8_), channel_id=1, source_target_pairs={{0,4},{1,5},{2,6},{3,7},{4,0},{5,1},{6,2},{7,3},{8,12},{9,13},{10,... | collective-permute-start | bytes 110600 | tf_op jit(solution)/shard_map/ppermute | solution.py:34
  35.0 3.7 %collective-permute-start.12 = (f32[4,4,128]{2,1,0:T(4,128)S(1)}, f32[4,4,128]{2,1,0:T(4,128)S(1)}, u32[]{:S(2)}, u32[]{:S(2)}) collective-permute-start(f32[4,4,128]{2,1,0:T(4,128)S(1)} %add.12), channel_id=1, source_target_pairs={{0,2},{1,3},{2,0},{3,1},{4,6},{5,7},{6,4},{7,5},{8,10},{9,11},{10,... | collective-permute-start | bytes 24584 | tf_op jit(solution)/shard_map/ppermute | solution.py:34
  38.7 1.2 %collective-permute-start.13 = (f32[4,4,128]{2,1,0:T(4,128)S(1)}, f32[4,4,128]{2,1,0:T(4,128)S(1)}, u32[]{:S(2)}, u32[]{:S(2)}) collective-permute-start(f32[4,4,128]{2,1,0:T(4,128)S(1)} %maximum_add_fusion.refs_0_), channel_id=1, source_target_pairs={{0,1},{1,0},{2,3},{3,2},{4,5},{5,4},{6,7},{7,6},{8,9},{9,8},{10,11... | collective-permute-start | bytes 24584 | tf_op jit(solution)/shard_map/ppermute | solution.py:34
  42.2 4.4 %collective-permute-start.17 = (bf16[2,144,128]{2,1,0:T(8,128)(2,1)S(1)}, bf16[2,144,128]{2,1,0:T(8,128)(2,1)S(1)}, u32[]{:S(2)}, u32[]{:S(2)}) collective-permute-start(bf16[2,144,128]{2,1,0:T(8,128)(2,1)S(1)} %get-tuple-element.49), channel_id=1, source_target_pairs={{0,2},{1,3},{2,0},{3,1},{4,6},{5,7},{6,4},{7,5},{8,10},{9,11},{10,... | collective-permute-start | bytes 221192 | tf_op jit(solution)/shard_map/ppermute | solution.py:34
  43.8 4.2 %collective-permute-start.15 = (bf16[128,128]{1,0:T(8,128)(2,1)S(1)}, bf16[128,128]{1,0:T(8,128)(2,1)S(1)}, u32[]{:S(2)}, u32[]{:S(2)}) collective-permute-start(bf16[128,128]{1,0:T(8,128)(2,1)S(1)} %get-tuple-element.47), channel_id=1, source_target_pairs={{0,4},{1,5},{2,6},{3,7},{4,0},{5,1},{6,2},{7,3},{8,12},{9,13},{10,... | collective-permute-start | bytes 98312 | tf_op jit(solution)/shard_map/ppermute | solution.py:34
  45.1 6.0 %collective-permute-start.14 = (bf16[128,128]{1,0:T(8,128)(2,1)S(1)}, bf16[128,128]{1,0:T(8,128)(2,1)S(1)}, u32[]{:S(2)}, u32[]{:S(2)}) collective-permute-start(bf16[128,128]{1,0:T(8,128)(2,1)S(1)} %get-tuple-element.45), channel_id=1, source_target_pairs={{0,4},{1,5},{2,6},{3,7},{4,0},{5,1},{6,2},{7,3},{8,12},{9,13},{10,... | collective-permute-start | bytes 98312 | tf_op jit(solution)/shard_map/ppermute | solution.py:34
  46.7 6.4 %collective-permute-start.18 = (f32[144,128]{1,0:T(8,128)S(1)}, f32[144,128]{1,0:T(8,128)S(1)}, u32[]{:S(2)}, u32[]{:S(2)}) collective-permute-start(f32[144,128]{1,0:T(8,128)S(1)} %get-tuple-element.53), channel_id=1, source_target_pairs={{0,1},{1,0},{2,3},{3,2},{4,5},{5,4},{6,7},{7,6},{8,9},{9,8},{10,11... | collective-permute-start | bytes 221192 | tf_op jit(solution)/shard_map/ppermute | solution.py:34
  48.0 5.0 %collective-permute-start.16 = (bf16[128,128]{1,0:T(8,128)(2,1)S(1)}, bf16[128,128]{1,0:T(8,128)(2,1)S(1)}, u32[]{:S(2)}, u32[]{:S(2)}) collective-permute-start(bf16[128,128]{1,0:T(8,128)(2,1)S(1)} %add_convert_fusion), channel_id=1, source_target_pairs={{0,8},{1,9},{2,10},{3,11},{4,12},{5,13},{6,14},{7,15},{8,0},{9,1},... | collective-permute-start | bytes 98312 | tf_op jit(solution)/shard_map/ppermute | solution.py:34

commit v3 on v0

--- a/solution.py
+++ b/solution.py
@@ -160,31 +160,28 @@
         )
 
 
-def grad_kernel(key_total, row_parts, places, last, *refs):
-    count = 1 + max(n for n, _ in places)
-    near_ref, far_ref, flat_ref, column_ref = refs[:4]
-    exps, indexes = refs[4 : 4 + count], refs[4 + count : 4 + 2 * count]
-    refs = refs[4 + 2 * count :]
-    blocks, refs = refs[: len(places)], refs[len(places) :]
-    if last:
-        early_dots, early_columns = refs[:2]
-        early_blocks, refs = refs[2 : 2 + len(places)], refs[2 + len(places) :]
-        key_ref, keep_ref, send_ref, dots_ref, total_ref = refs
-    else:
-        key_ref, dots_ref, columns_ref, total_ref = refs
-    rows, own_rows = total_ref.shape[0], total_ref.shape[0] // row_parts
-    index_heads, index_width = column_ref.shape[0], flat_ref.shape[1]
-    head_count, own_keys = exps[0].shape[1], key_ref.shape[1]
-    index_scale = float(index_heads * index_width) ** (-0.5)
+def prepare_kernel(flat_ref, column_ref, *refs):
+    blocks, (heads_ref, masked_ref) = refs[:-2], refs[-2:]
+    index_heads, rows = column_ref.shape
+    own_keys = heads_ref.shape[1] // len(blocks)
+    index_scale = float(index_heads * flat_ref.shape[1]) ** (-0.5)
     ikeys = jnp.concatenate([b[:own_keys, :] for b in blocks], axis=0)
-    flat = flat_ref[...]
-    dots = contract(flat, ikeys, (1, 1))
+    dots = contract(flat_ref[...], ikeys, (1, 1))
+    heads_ref[...] = jnp.maximum(dots, 0.0)
+    for t in range(rows):
+        lines = slice(t * index_heads, (t + 1) * index_heads)
+        weight = index_scale * column_ref[:, t : t + 1]
+        masked_ref[lines, :] = jnp.where(dots[lines, :] > 0, weight, 0.0)
+
+
+def gradient_of(key_total, row_parts, places, near_ref, far_ref, total_ref, exps, indexes, own_keys):
+    rows, head_count = total_ref.shape
+    own_rows = rows // row_parts
     for r in range(row_parts):
         lines = slice(0, own_rows)
         total_ref[r * own_rows : (r + 1) * own_rows, :] = near_ref[r, lines, :] + far_ref[r ^ 1, lines, :]
     shares = jnp.transpose(1.0 / total_ref[...])
-    lane = lax.broadcasted_iota(jnp.int32, (index_heads, LANES), 1)
-    columns = early_columns[...] if last else jnp.zeros((index_heads, LANES), f32)
+    gradients = []
     for t in range(rows):
         r, i = divmod(t, own_rows)
         share = shares[:, t : t + 1]
@@ -200,20 +197,64 @@
         index_exp = jnp.concatenate(
             [indexes[n][t : t + 1, p : p + own_keys] for n, p in places], axis=1
         )
-        gradient = key_total * (index_exp / index_total - target / head_count)
-        heads = dots[t * index_heads : (t + 1) * index_heads, :]
-        column = index_scale * jnp.sum(gradient * jnp.maximum(heads, 0.0), axis=1, keepdims=True)
-        columns = jnp.where(lane == t, columns + column, columns)
+        gradients.append(key_total * (index_exp / index_total - target / head_count))
+    return gradients
+
+
+def first_grad_kernel(key_total, row_parts, places, *refs):
+    count = 1 + max(n for n, _ in places)
+    near_ref, far_ref, flat_ref, masked_ref = refs[:4]
+    exps, indexes = refs[4 : 4 + count], refs[4 + count : 4 + 2 * count]
+    key_ref, dots_ref, gradient_ref, total_ref = refs[4 + 2 * count :]
+    own_keys = key_ref.shape[1]
+    gradients = gradient_of(
+        key_total, row_parts, places, near_ref, far_ref, total_ref, exps, indexes, own_keys
+    )
+    index_heads = flat_ref.shape[0] // len(gradients)
+    for t, gradient in enumerate(gradients):
+        lines = slice(t * index_heads, (t + 1) * index_heads)
+        gradient_ref[t : t + 1, :] = gradient
+        dots_ref[lines, :] = (gradient * masked_ref[lines, :]).astype(bf16)
+    key_grad = contract(dots_ref[...], flat_ref[...], (0, 0))
+    for k in range(len(places)):
+        key_ref[k] = key_grad[k * own_keys : (k + 1) * own_keys, :].astype(key_ref.dtype)
+
+
+def grad_kernel(key_total, row_parts, places, *refs):
+    count = 1 + max(n for n, _ in places)
+    near_ref, far_ref, flat_ref, column_ref = refs[:4]
+    exps, indexes = refs[4 : 4 + count], refs[4 + count : 4 + 2 * count]
+    refs = refs[4 + 2 * count :]
+    blocks, refs = refs[: len(places)], refs[len(places) :]
+    early_dots, early_gradient, early_heads = refs[:3]
+    early_blocks, refs = refs[3 : 3 + len(places)], refs[3 + len(places) :]
+    key_ref, keep_ref, send_ref, dots_ref, total_ref = refs
+    own_rows = total_ref.shape[0] // row_parts
+    index_heads, index_width = column_ref.shape[0], flat_ref.shape[1]
+    own_keys = key_ref.shape[1]
+    index_scale = float(index_heads * index_width) ** (-0.5)
+    ikeys = jnp.concatenate([b[:own_keys, :] for b in blocks], axis=0)
+    flat = flat_ref[...]
+    dots = contract(flat, ikeys, (1, 1))
+    gradients = gradient_of(
+        key_total, row_parts, places, near_ref, far_ref, total_ref, exps, indexes, own_keys
+    )
+    lane = lax.broadcasted_iota(jnp.int32, (index_heads, LANES), 1)
+    columns = jnp.zeros((index_heads, LANES), f32)
+    for t, gradient in enumerate(gradients):
+        lines = slice(t * index_heads, (t + 1) * index_heads)
+        heads = dots[lines, :]
+        terms = gradient * jnp.maximum(heads, 0.0)
+        terms = terms + early_gradient[t : t + 1, :] * early_heads[lines, :]
+        column = index_scale * jnp.sum(terms, axis=1, keepdims=True)
+        columns = jnp.where(lane == t, column, columns)
         weight = column_ref[:, t : t + 1]
         grad_dots = jnp.where(heads > 0, index_scale * gradient * weight, 0.0).astype(bf16)
-        dots_ref[t * index_heads : (t + 1) * index_heads, :] = grad_dots
+        dots_ref[lines, :] = grad_dots
     grad_dots = dots_ref[...]
     key_grad = contract(grad_dots, flat, (0, 0))
     for k in range(len(blocks)):
         key_ref[k] = key_grad[k * own_keys : (k + 1) * own_keys, :].astype(key_ref.dtype)
-    if not last:
-        columns_ref[...] = columns
-        return
     early_keys = jnp.concatenate([b[:own_keys, :] for b in early_blocks], axis=0)
     grad_query = contract(grad_dots, ikeys, (1, 0)) + contract(early_dots[...], early_keys, (1, 0))
     weights = jnp.transpose(jnp.concatenate([columns, jnp.zeros_like(columns)], axis=0)[:LANES])
@@ -331,34 +372,39 @@
     even, odd, keep, send = [], [], None, None
     for ids in teams:
         half = len(ids) // 2
+        more = struct((rows * index_heads, half * own_keys), bf16)
+        wide = struct(more.shape, f32)
+        grads_flops = 4 * rows * index_heads * index_width * half * own_keys
+        heads, masked = kernel_call(
+            prepare_kernel,
+            (wide, wide),
+            (*laid[1:3], *(blocks[k] for k in ids[1::2])),
+            flops=grads_flops,
+        )
         early = None
         for part in (1, 0):
             mine = ids[part::2]
             used = sorted({place[k][0] for k in mine})
             places = tuple((used.index(place[k][0]), place[k][1]) for k in mine)
-            operands = (
-                sums,
-                got,
-                *laid[1:3],
-                *(exps[n] for n in used),
-                *(indexes[n] for n in used),
-                *(blocks[k] for k in mine),
-            )
+            stored = (*(exps[n] for n in used), *(indexes[n] for n in used))
             shapes = (struct((half, own_keys, index_width), bf16 if part else f32),)
-            more = struct((rows * index_heads, half * own_keys), bf16)
             scratch = (pltpu.VMEM((rows, head_count), f32),)
             if part:
-                shapes += (more, struct((index_heads, LANES), f32))
+                kernel = first_grad_kernel
+                operands = (sums, got, laid[1], masked, *stored)
+                shapes += (more, struct((rows, half * own_keys), f32))
             else:
-                operands += (*early, *(blocks[k] for k in ids[1::2]))
+                kernel = grad_kernel
+                operands = (sums, got, *laid[1:3], *stored, *(blocks[k] for k in mine))
+                operands += (*early, heads, *(blocks[k] for k in ids[1::2]))
                 shapes += (struct((row_parts // 2, tall, index_width), f32),) * 2
                 scratch = (pltpu.VMEM(more.shape, bf16), *scratch)
             out = kernel_call(
-                functools.partial(grad_kernel, key_total, row_parts, places, not part),
+                functools.partial(kernel, key_total, row_parts, places),
                 shapes,
                 operands,
                 scratch=scratch,
-                flops=6 * rows * index_heads * index_width * half * own_keys,
+                flops=grads_flops,
             )
             if part:
                 odd.append(out[0])

time: 50.5 us -> 52.2 us (1.034)
  waiting for transfers between devices: 23.5 us -> 28.9 us
  starting transfers between devices: 19.8 us -> 16.3 us
    ppermute x18, waiting for transfers between devices: 23.5 us -> 28.9 us  [swap(): return lax.ppermute(array, 'ctx', [(i, i ^ mask) for i in range(count)])]
    ppermute x18, starting transfers between devices: 19.8 us -> 16.3 us  [swap(): return lax.ppermute(array, 'ctx', [(i, i ^ mask) for i in range(count)])]
    pallas_call x5 -> x6, Pallas kernels: 5.1 us -> 4.88 us  [kernel_call(): pl.pallas_call(kernel, out_shape=tuple(shapes), scratch_shapes=list(scrat...]
where the time goes in v3:
time: 52.2 us; the launch traced here: 52 us
  waiting for transfers between devices  28.9 us (55%)
  starting transfers between devices  16.3 us (31%)
  Pallas kernels  6.01 us (12%)
  between operations  0.73 us (1%)
    ppermute x18, waiting for transfers between devices, swap(): return lax.ppermute(array, 'ctx', [(i, i ^ mask) for i in range(count)])  28.9 us
    ppermute x18, starting transfers between devices, swap(): return lax.ppermute(array, 'ctx', [(i, i ^ mask) for i in range(count)])  16.3 us
    pallas_call x6, Pallas kernels, kernel_call(): pl.pallas_call(kernel, out_shape=tuple(shapes), scratch_shapes=list(scrat...  4.88 us
    pallas_call x1, Pallas kernels, body(): pl.pallas_call(pack_kernel, out_shape=(struct((own_keys + 16, own_keys),...  1.13 us
  transfers between devices with their start and end apart: 18, of which 12 were waited for; matrix products, arithmetic and copies ran while one was open for 0% of the time, Pallas kernels for 8%

profile of v3, /device:TPU:0, one launch (start us, length us, event | category | flops | bytes accessed | tf_op | source)
XLA Modules:
  0.0 52.0 jit_solution(1581852299073621680)
XLA Ops:
  0.6 3.0 %collective-permute-start.1 = (bf16[2,576,128]{2,1,0:T(8,128)(2,1)}, bf16[2,576,128]{2,1,0:T(8,128)(2,1)S(1)}, u32[]{:S(2)}, u32[]{:S(2)}) collective-permute-start(bf16[2,576,128]{2,1,0:T(8,128)(2,1)} %bitcast.13), channel_id=1, source_target_pairs={{0,2},{1,3},{2,0},{3,1},{4,6},{5,7},{6,4},{7,5},{8,10},{9,11},{10,... | collective-permute-start | bytes 884744 | tf_op jit(solution)/shard_map/ppermute | solution.py:34
  3.7 0.0 collective-permute-start
  3.7 7.2 %collective-permute-done.1.refs_2_ = bf16[2,576,128]{2,1,0:T(8,128)(2,1)S(1)} collective-permute-done((bf16[2,576,128]{2,1,0:T(8,128)(2,1)}, bf16[2,576,128]{2,1,0:T(8,128)(2,1)S(1)}, u32[]{:S(2)}, u32[]{:S(2)}) %collective-permute-start.1) | collective-permute-done | bytes 294944 | tf_op jit(solution)/shard_map/ppermute | solution.py:34
  10.9 0.0 collective-permute-start.2
  10.9 2.8 %collective-permute-start.7 = (bf16[576,128]{1,0:T(8,128)(2,1)}, bf16[576,128]{1,0:T(8,128)(2,1)S(1)}, u32[]{:S(2)}, u32[]{:S(2)}) collective-permute-start(bf16[576,128]{1,0:T(8,128)(2,1)} %bitcast.16), channel_id=1, source_target_pairs={{0,8},{1,9},{2,10},{3,11},{4,12},{5,13},{6,14},{7,15},{8,0},{9,1},... | collective-permute-start | bytes 442376 | tf_op jit(solution)/shard_map/ppermute | solution.py:34
  13.7 1.1 %pack.1 = (bf16[144,128]{1,0:T(8,128)(2,1)S(1)}, bf16[144,128]{1,0:T(8,128)(2,1)S(1)}, bf16[2,576,128]{2,1,0:T(8,128)(2,1)S(1)}, bf16[576,128]{1,0:T(8,128)(2,1)S(1)}) custom-call(s32[4,128]{1,0:T(4,128)} %bitcast.20, bf16[128,128]{1,0:T(8,128)(2,1)} %keys_hbm.1, f32[2,64]{1,0:T(2,128)} %weight_hbm.1, s32[2]{0:T(128)} %pos_hbm.1, ...), custom_call_target="tpu_custom_call" | custom-call | tf_op jit(solution)/shard_map/pack/pallas_call | solution.py:302
  14.9 0.3 collective-permute-start.3
  15.2 1.5 %collective-permute-start.4 = (bf16[144,128]{1,0:T(8,128)(2,1)S(1)}, bf16[144,128]{1,0:T(8,128)(2,1)S(1)}, u32[]{:S(2)}, u32[]{:S(2)}) collective-permute-start(bf16[144,128]{1,0:T(8,128)(2,1)S(1)} %get-tuple-element.29.refs_4_), channel_id=1, source_target_pairs={{0,2},{1,3},{2,0},{3,1},{4,6},{5,7},{6,4},{7,5},{8,10},{9,11},{10,... | collective-permute-start | bytes 110600 | tf_op jit(solution)/shard_map/ppermute | solution.py:34
  16.6 0.0 collective-permute-done.3.refs_5_
  16.7 1.6 %collective-permute-start.6 = (bf16[576,128]{1,0:T(8,128)(2,1)}, bf16[576,128]{1,0:T(8,128)(2,1)S(1)}, u32[]{:S(2)}, u32[]{:S(2)}) collective-permute-start(bf16[576,128]{1,0:T(8,128)(2,1)} %bitcast.18), channel_id=1, source_target_pairs={{0,4},{1,5},{2,6},{3,7},{4,0},{5,1},{6,2},{7,3},{8,12},{9,13},{10,... | collective-permute-start | bytes 442376 | tf_op jit(solution)/shard_map/ppermute | solution.py:34
  18.2 0.9 %collective-permute-done.4.refs_6_ = bf16[144,128]{1,0:T(8,128)(2,1)S(1)} collective-permute-done((bf16[144,128]{1,0:T(8,128)(2,1)S(1)}, bf16[144,128]{1,0:T(8,128)(2,1)S(1)}, u32[]{:S(2)}, u32[]{:S(2)}) %collective-permute-start.4) | collective-permute-done | bytes 36896 | tf_op jit(solution)/shard_map/ppermute | solution.py:34
  19.1 1.6 %collective-permute-start.8 = (bf16[144,128]{1,0:T(8,128)(2,1)S(1)}, bf16[144,128]{1,0:T(8,128)(2,1)S(1)}, u32[]{:S(2)}, u32[]{:S(2)}) collective-permute-start(bf16[144,128]{1,0:T(8,128)(2,1)S(1)} %get-tuple-element.31.refs_11_.refs_6_), channel_id=1, source_target_pairs={{0,4},{1,5},{2,6},{3,7},{4,0},{5,1},{6,2},{7,3},{8,12},{9,13},{10,... | collective-permute-start | bytes 110600 | tf_op jit(solution)/shard_map/ppermute | solution.py:34
  20.7 1.0 %collective-permute-done.7.refs_10_ = bf16[576,128]{1,0:T(8,128)(2,1)S(1)} collective-permute-done((bf16[576,128]{1,0:T(8,128)(2,1)}, bf16[576,128]{1,0:T(8,128)(2,1)S(1)}, u32[]{:S(2)}, u32[]{:S(2)}) %collective-permute-start.7) | collective-permute-done | bytes 147488 | tf_op jit(solution)/shard_map/ppermute | solution.py:34
  21.7 0.8 %collective-permute-start.10 = (bf16[576,128]{1,0:T(8,128)(2,1)S(1)}, bf16[576,128]{1,0:T(8,128)(2,1)S(1)}, u32[]{:S(2)}, u32[]{:S(2)}) collective-permute-start(bf16[576,128]{1,0:T(8,128)(2,1)S(1)} %collective-permute-done.7.refs_10_), channel_id=1, source_target_pairs={{0,4},{1,5},{2,6},{3,7},{4,0},{5,1},{6,2},{7,3},{8,12},{9,13},{10,... | collective-permute-start | bytes 442376 | tf_op jit(solution)/shard_map/ppermute | solution.py:34
  22.5 3.2 %collective-permute-done.8.refs_12_.refs_0_.refs_11_ = bf16[144,128]{1,0:T(8,128)(2,1)S(1)} collective-permute-done((bf16[144,128]{1,0:T(8,128)(2,1)S(1)}, bf16[144,128]{1,0:T(8,128)(2,1)S(1)}, u32[]{:S(2)}, u32[]{:S(2)}) %collective-permute-start.8) | collective-permute-done | bytes 36896 | tf_op jit(solution)/shard_map/ppermute | solution.py:34
  25.7 0.2 collective-permute-start.9
  25.9 4.6 %collective-permute-done.9.refs_13_.refs_7_ = bf16[144,128]{1,0:T(8,128)(2,1)S(1)} collective-permute-done((bf16[144,128]{1,0:T(8,128)(2,1)S(1)}, bf16[144,128]{1,0:T(8,128)(2,1)S(1)}, u32[]{:S(2)}, u32[]{:S(2)}) %collective-permute-start.9) | collective-permute-done | bytes 36896 | tf_op jit(solution)/shard_map/ppermute | solution.py:34
  30.5 0.0 collective-permute-start.5
  30.5 1.2 %collective-permute-done.5.refs_7_ = bf16[144,128]{1,0:T(8,128)(2,1)S(1)} collective-permute-done((bf16[144,128]{1,0:T(8,128)(2,1)S(1)}, bf16[144,128]{1,0:T(8,128)(2,1)S(1)}, u32[]{:S(2)}, u32[]{:S(2)}) %collective-permute-start.5) | collective-permute-done | bytes 36896 | tf_op jit(solution)/shard_map/ppermute | solution.py:34
  31.7 0.1 collective-permute-start.11
  31.9 0.0 collective-permute-done.6.refs_9_
  31.9 0.0 collective-permute-done.refs_1_
  31.9 0.0 collective-permute-done.2.refs_3_
  31.9 1.6 %shard_map.94 = (f32[8,128,384]{2,1,0:T(8,128)S(1)}, f32[8,384]{1,0:T(8,128)S(1)}, f32[4,4,128]{2,1,0:T(4,128)S(1)}, bf16[1024,576]{1,0:T(8,128)(2,1)S(1)}, bf16...) custom-call(bf16[2,576,128]{2,1,0:T(8,128)(2,1)S(1)} %get-tuple-element.28.refs_0_, ...), custom_call_target="tpu_custom_call" | custom-call | flops 452984832 | bytes 4790272 | tf_op jit(solution)/shard_map/pallas_call | solution.py:20
  33.5 2.2 %collective-permute-done.11.refs_5_.refs_1_.refs_12_ = bf16[144,128]{1,0:T(8,128)(2,1)S(1)} collective-permute-done((bf16[144,128]{1,0:T(8,128)(2,1)S(1)}, bf16[144,128]{1,0:T(8,128)(2,1)S(1)}, u32[]{:S(2)}, u32[]{:S(2)}) %collective-permute-start.11) | collective-permute-done | bytes 36896 | tf_op jit(solution)/shard_map/ppermute | solution.py:34
  35.7 0.0 collective-permute-done.10.refs_4_
  35.7 0.7 %shard_map.95 = (f32[8,128,128]{2,1,0:T(8,128)S(1)}, f32[8,128]{1,0:T(8,128)S(1)}, f32[4,4,128]{2,1,0:T(4,128)S(1)}) custom-call(bf16[1024,576]{1,0:T(8,128)(2,1)S(1)} %get-tuple-element.33.refs_0_, bf16[512,128]{1,0:T(8,128)(2,1)S(1)} %get-tuple-element.34.refs_1_.flat_ref.refs_2_, f32[64,8]{1,0:T(8,128)S(1)} %get-tuple-element.35.refs_2_.column_ref.refs_3_, ...), custom_call_target="tpu_custom_call" | custom-call | flops 150994944 | bytes 2037760 | tf_op jit(solution)/shard_map/pallas_call | solution.py:20
  36.4 1.5 %collective-permute-start.12 = (f32[4,4,128]{2,1,0:T(4,128)S(1)}, f32[4,4,128]{2,1,0:T(4,128)S(1)}, u32[]{:S(2)}, u32[]{:S(2)}) collective-permute-start(f32[4,4,128]{2,1,0:T(4,128)S(1)} %add.12), channel_id=1, source_target_pairs={{0,2},{1,3},{2,0},{3,1},{4,6},{5,7},{6,4},{7,5},{8,10},{9,11},{10,... | collective-permute-start | bytes 24584 | tf_op jit(solution)/shard_map/ppermute | solution.py:34
  37.9 2.2 %collective-permute-done.12 = f32[4,4,128]{2,1,0:T(4,128)S(1)} collective-permute-done((f32[4,4,128]{2,1,0:T(4,128)S(1)}, f32[4,4,128]{2,1,0:T(4,128)S(1)}, u32[]{:S(2)}, u32[]{:S(2)}) %collective-permute-start.12) | collective-permute-done | bytes 8224 | tf_op jit(solution)/shard_map/ppermute | solution.py:34
  40.1 0.1 collective-permute-start.13
  40.2 0.2 shard_map.96
  40.4 0.9 %collective-permute-done.13.refs_1_ = f32[4,4,128]{2,1,0:T(4,128)S(1)} collective-permute-done((f32[4,4,128]{2,1,0:T(4,128)S(1)}, f32[4,4,128]{2,1,0:T(4,128)S(1)}, u32[]{:S(2)}, u32[]{:S(2)}) %collective-permute-start.13) | collective-permute-done | bytes 8224 | tf_op jit(solution)/shard_map/ppermute | solution.py:34
  41.4 0.7 %shard_map.97 = (bf16[2,128,128]{2,1,0:T(8,128)(2,1)S(1)}, bf16[512,256]{1,0:T(8,128)(2,1)S(1)}, f32[8,256]{1,0:T(8,128)S(1)}) custom-call(f32[4,4,128]{2,1,0:T(4,128)S(1)} %maximum_add_fusion.refs_0_, f32[4,4,128]{2,1,0:T(4,128)S(1)} %collective-permute-done.13.refs_1_, bf16[512,128]{1,0:T(8,128)(2,1)S(1)} %get-tuple-element.34.refs_1_.flat_ref.refs_2_, ...), custom_call_target="tpu_custom_call" | custom-call | flops 67108864 | bytes 3121152 | tf_op jit(solution)/shard_map/pallas_call | solution.py:20
  42.1 0.2 collective-permute-start.14
  42.2 1.0 %shard_map.98 = (f32[2,128,128]{2,1,0:T(8,128)S(1)}, f32[2,136,128]{2,1,0:T(8,128)S(1)}, f32[2,136,128]{2,1,0:T(8,128)S(1)}) custom-call(f32[4,4,128]{2,1,0:T(4,128)S(1)} %maximum_add_fusion.refs_0_, f32[4,4,128]{2,1,0:T(4,128)S(1)} %collective-permute-done.13.refs_1_, bf16[512,128]{1,0:T(8,128)(2,1)S(1)} %get-tuple-element.34.refs_1_.flat_ref.refs_2_, ...), custom_call_target="tpu_custom_call" | custom-call | flops 67108864 | bytes 3086336 | tf_op jit(solution)/shard_map/pallas_call | solution.py:20
  43.2 1.6 %collective-permute-start.16 = (f32[2,136,128]{2,1,0:T(8,128)S(1)}, f32[2,136,128]{2,1,0:T(8,128)S(1)}, u32[]{:S(2)}, u32[]{:S(2)}) collective-permute-start(f32[2,136,128]{2,1,0:T(8,128)S(1)} %get-tuple-element.49), channel_id=1, source_target_pairs={{0,2},{1,3},{2,0},{3,1},{4,6},{5,7},{6,4},{7,5},{8,10},{9,11},{10,... | collective-permute-start | bytes 417800 | tf_op jit(solution)/shard_map/ppermute | solution.py:34
  44.8 1.6 %collective-permute-done.14 = bf16[2,128,128]{2,1,0:T(8,128)(2,1)S(1)} collective-permute-done((bf16[2,128,128]{2,1,0:T(8,128)(2,1)S(1)}, bf16[2,128,128]{2,1,0:T(8,128)(2,1)S(1)}, u32[]{:S(2)}, u32[]{:S(2)}) %collective-permute-start.14) | collective-permute-done | bytes 65568 | tf_op jit(solution)/shard_map/ppermute | solution.py:34
  46.4 0.9 %collective-permute-start.15 = (bf16[1,128,128]{2,1,0:T(8,128)(2,1)S(1)}, bf16[1,128,128]{2,1,0:T(8,128)(2,1)S(1)}, u32[]{:S(2)}, u32[]{:S(2)}) collective-permute-start(bf16[1,128,128]{2,1,0:T(8,128)(2,1)S(1)} %slice.41), channel_id=1, source_target_pairs={{0,8},{1,9},{2,10},{3,11},{4,12},{5,13},{6,14},{7,15},{8,0},{9,1},... | collective-permute-start | bytes 98312 | tf_op jit(solution)/shard_map/ppermute | solution.py:34
  47.4 1.6 %collective-permute-done.16 = f32[2,136,128]{2,1,0:T(8,128)S(1)} collective-permute-done((f32[2,136,128]{2,1,0:T(8,128)S(1)}, f32[2,136,128]{2,1,0:T(8,128)S(1)}, u32[]{:S(2)}, u32[]{:S(2)}) %collective-permute-start.16) | collective-permute-done | bytes 139296 | tf_op jit(solution)/shard_map/ppermute | solution.py:34
  49.0 0.1 collective-permute-start.17
  49.1 2.3 %collective-permute-done.15 = bf16[1,128,128]{2,1,0:T(8,128)(2,1)S(1)} collective-permute-done((bf16[1,128,128]{2,1,0:T(8,128)(2,1)S(1)}, bf16[1,128,128]{2,1,0:T(8,128)(2,1)S(1)}, u32[]{:S(2)}, u32[]{:S(2)}) %collective-permute-start.15) | collective-permute-done | bytes 32800 | tf_op jit(solution)/shard_map/ppermute | solution.py:34
  51.3 0.0 collective-permute-done.17.row_got_ref
  51.4 0.7 %shard_map.99 = (f32[128,128]{1,0:T(8,128)}, f32[2,64]{1,0:T(2,128)}, f32[128,128]{1,0:T(8,128)}) custom-call(f32[128,128]{1,0:T(8,128)S(1)} %slice_bitcast_fusion.2.key_ref, bf16[128,128]{1,0:T(8,128)(2,1)S(1)} %bitcast.12, f32[136,128]{1,0:T(8,128)S(1)} %get-tuple-element.54.row_ref, f32[136,128]{1,0:T(8,128)S(1)} %collective-permute-done.17.row_got_ref), custom_call_target="tpu_custom_call" | custom-call | bytes 369152 | tf_op jit(solution)/shard_map/pallas_call | solution.py:20
  (8 shorter events, 0.1 us)
Async XLA Ops:
  0.6 10.2 %collective-permute-start.1 = (bf16[2,576,128]{2,1,0:T(8,128)(2,1)}, bf16[2,576,128]{2,1,0:T(8,128)(2,1)S(1)}, u32[]{:S(2)}, u32[]{:S(2)}) collective-permute-start(bf16[2,576,128]{2,1,0:T(8,128)(2,1)} %bitcast.13), channel_id=1, source_target_pairs={{0,2},{1,3},{2,0},{3,1},{4,6},{5,7},{6,4},{7,5},{8,10},{9,11},{10,... | collective-permute-start | bytes 884744 | tf_op jit(solution)/shard_map/ppermute | solution.py:34
  3.7 28.2 %collective-permute-start = (bf16[2,576,128]{2,1,0:T(8,128)(2,1)}, bf16[2,576,128]{2,1,0:T(8,128)(2,1)S(1)}, u32[]{:S(2)}, u32[]{:S(2)}) collective-permute-start(bf16[2,576,128]{2,1,0:T(8,128)(2,1)} %bitcast.14), channel_id=1, source_target_pairs={{0,1},{1,0},{2,3},{3,2},{4,5},{5,4},{6,7},{7,6},{8,9},{9,8},{10,11... | collective-permute-start | bytes 884744 | tf_op jit(solution)/shard_map/ppermute | solution.py:34
  10.9 21.0 %collective-permute-start.2 = (bf16[2,576,128]{2,1,0:T(8,128)(2,1)S(1)}, bf16[2,576,128]{2,1,0:T(8,128)(2,1)S(1)}, u32[]{:S(2)}, u32[]{:S(2)}) collective-permute-start(bf16[2,576,128]{2,1,0:T(8,128)(2,1)S(1)} %collective-permute-done.1.refs_2_), channel_id=1, source_target_pairs={{0,1},{1,0},{2,3},{3,2},{4,5},{5,4},{6,7},{7,6},{8,9},{9,8},{10,11... | collective-permute-start | bytes 884744 | tf_op jit(solution)/shard_map/ppermute | solution.py:34
  10.9 10.8 %collective-permute-start.7 = (bf16[576,128]{1,0:T(8,128)(2,1)}, bf16[576,128]{1,0:T(8,128)(2,1)S(1)}, u32[]{:S(2)}, u32[]{:S(2)}) collective-permute-start(bf16[576,128]{1,0:T(8,128)(2,1)} %bitcast.16), channel_id=1, source_target_pairs={{0,8},{1,9},{2,10},{3,11},{4,12},{5,13},{6,14},{7,15},{8,0},{9,1},... | collective-permute-start | bytes 442376 | tf_op jit(solution)/shard_map/ppermute | solution.py:34
  14.9 1.8 %collective-permute-start.3 = (bf16[144,128]{1,0:T(8,128)(2,1)S(1)}, bf16[144,128]{1,0:T(8,128)(2,1)S(1)}, u32[]{:S(2)}, u32[]{:S(2)}) collective-permute-start(bf16[144,128]{1,0:T(8,128)(2,1)S(1)} %get-tuple-element.29.refs_4_), channel_id=1, source_target_pairs={{0,1},{1,0},{2,3},{3,2},{4,5},{5,4},{6,7},{7,6},{8,9},{9,8},{10,11... | collective-permute-start | bytes 110600 | tf_op jit(solution)/shard_map/ppermute | solution.py:34
  15.2 4.0 %collective-permute-start.4 = (bf16[144,128]{1,0:T(8,128)(2,1)S(1)}, bf16[144,128]{1,0:T(8,128)(2,1)S(1)}, u32[]{:S(2)}, u32[]{:S(2)}) collective-permute-start(bf16[144,128]{1,0:T(8,128)(2,1)S(1)} %get-tuple-element.29.refs_4_), channel_id=1, source_target_pairs={{0,2},{1,3},{2,0},{3,1},{4,6},{5,7},{6,4},{7,5},{8,10},{9,11},{10,... | collective-permute-start | bytes 110600 | tf_op jit(solution)/shard_map/ppermute | solution.py:34
  16.7 15.2 %collective-permute-start.6 = (bf16[576,128]{1,0:T(8,128)(2,1)}, bf16[576,128]{1,0:T(8,128)(2,1)S(1)}, u32[]{:S(2)}, u32[]{:S(2)}) collective-permute-start(bf16[576,128]{1,0:T(8,128)(2,1)} %bitcast.18), channel_id=1, source_target_pairs={{0,4},{1,5},{2,6},{3,7},{4,0},{5,1},{6,2},{7,3},{8,12},{9,13},{10,... | collective-permute-start | bytes 442376 | tf_op jit(solution)/shard_map/ppermute | solution.py:34
  19.1 6.5 %collective-permute-start.8 = (bf16[144,128]{1,0:T(8,128)(2,1)S(1)}, bf16[144,128]{1,0:T(8,128)(2,1)S(1)}, u32[]{:S(2)}, u32[]{:S(2)}) collective-permute-start(bf16[144,128]{1,0:T(8,128)(2,1)S(1)} %get-tuple-element.31.refs_11_.refs_6_), channel_id=1, source_target_pairs={{0,4},{1,5},{2,6},{3,7},{4,0},{5,1},{6,2},{7,3},{8,12},{9,13},{10,... | collective-permute-start | bytes 110600 | tf_op jit(solution)/shard_map/ppermute | solution.py:34
  21.7 14.0 %collective-permute-start.10 = (bf16[576,128]{1,0:T(8,128)(2,1)S(1)}, bf16[576,128]{1,0:T(8,128)(2,1)S(1)}, u32[]{:S(2)}, u32[]{:S(2)}) collective-permute-start(bf16[576,128]{1,0:T(8,128)(2,1)S(1)} %collective-permute-done.7.refs_10_), channel_id=1, source_target_pairs={{0,4},{1,5},{2,6},{3,7},{4,0},{5,1},{6,2},{7,3},{8,12},{9,13},{10,... | collective-permute-start | bytes 442376 | tf_op jit(solution)/shard_map/ppermute | solution.py:34
  25.7 4.9 %collective-permute-start.9 = (bf16[144,128]{1,0:T(8,128)(2,1)S(1)}, bf16[144,128]{1,0:T(8,128)(2,1)S(1)}, u32[]{:S(2)}, u32[]{:S(2)}) collective-permute-start(bf16[144,128]{1,0:T(8,128)(2,1)S(1)} %get-tuple-element.31.refs_11_.refs_6_), channel_id=1, source_target_pairs={{0,8},{1,9},{2,10},{3,11},{4,12},{5,13},{6,14},{7,15},{8,0},{9,1},... | collective-permute-start | bytes 110600 | tf_op jit(solution)/shard_map/ppermute | solution.py:34
  30.5 1.2 %collective-permute-start.5 = (bf16[144,128]{1,0:T(8,128)(2,1)S(1)}, bf16[144,128]{1,0:T(8,128)(2,1)S(1)}, u32[]{:S(2)}, u32[]{:S(2)}) collective-permute-start(bf16[144,128]{1,0:T(8,128)(2,1)S(1)} %collective-permute-done.4.refs_6_), channel_id=1, source_target_pairs={{0,1},{1,0},{2,3},{3,2},{4,5},{5,4},{6,7},{7,6},{8,9},{9,8},{10,11... | collective-permute-start | bytes 110600 | tf_op jit(solution)/shard_map/ppermute | solution.py:34
  31.7 4.0 %collective-permute-start.11 = (bf16[144,128]{1,0:T(8,128)(2,1)S(1)}, bf16[144,128]{1,0:T(8,128)(2,1)S(1)}, u32[]{:S(2)}, u32[]{:S(2)}) collective-permute-start(bf16[144,128]{1,0:T(8,128)(2,1)S(1)} %collective-permute-done.9.refs_13_.refs_7_), channel_id=1, source_target_pairs={{0,4},{1,5},{2,6},{3,7},{4,0},{5,1},{6,2},{7,3},{8,12},{9,13},{10,... | collective-permute-start | bytes 110600 | tf_op jit(solution)/shard_map/ppermute | solution.py:34
  36.4 3.7 %collective-permute-start.12 = (f32[4,4,128]{2,1,0:T(4,128)S(1)}, f32[4,4,128]{2,1,0:T(4,128)S(1)}, u32[]{:S(2)}, u32[]{:S(2)}) collective-permute-start(f32[4,4,128]{2,1,0:T(4,128)S(1)} %add.12), channel_id=1, source_target_pairs={{0,2},{1,3},{2,0},{3,1},{4,6},{5,7},{6,4},{7,5},{8,10},{9,11},{10,... | collective-permute-start | bytes 24584 | tf_op jit(solution)/shard_map/ppermute | solution.py:34
  40.1 1.2 %collective-permute-start.13 = (f32[4,4,128]{2,1,0:T(4,128)S(1)}, f32[4,4,128]{2,1,0:T(4,128)S(1)}, u32[]{:S(2)}, u32[]{:S(2)}) collective-permute-start(f32[4,4,128]{2,1,0:T(4,128)S(1)} %maximum_add_fusion.refs_0_), channel_id=1, source_target_pairs={{0,1},{1,0},{2,3},{3,2},{4,5},{5,4},{6,7},{7,6},{8,9},{9,8},{10,11... | collective-permute-start | bytes 24584 | tf_op jit(solution)/shard_map/ppermute | solution.py:34
  42.1 4.3 %collective-permute-start.14 = (bf16[2,128,128]{2,1,0:T(8,128)(2,1)S(1)}, bf16[2,128,128]{2,1,0:T(8,128)(2,1)S(1)}, u32[]{:S(2)}, u32[]{:S(2)}) collective-permute-start(bf16[2,128,128]{2,1,0:T(8,128)(2,1)S(1)} %get-tuple-element.47), channel_id=1, source_target_pairs={{0,4},{1,5},{2,6},{3,7},{4,0},{5,1},{6,2},{7,3},{8,12},{9,13},{10,... | collective-permute-start | bytes 196616 | tf_op jit(solution)/shard_map/ppermute | solution.py:34
  43.2 5.7 %collective-permute-start.16 = (f32[2,136,128]{2,1,0:T(8,128)S(1)}, f32[2,136,128]{2,1,0:T(8,128)S(1)}, u32[]{:S(2)}, u32[]{:S(2)}) collective-permute-start(f32[2,136,128]{2,1,0:T(8,128)S(1)} %get-tuple-element.49), channel_id=1, source_target_pairs={{0,2},{1,3},{2,0},{3,1},{4,6},{5,7},{6,4},{7,5},{8,10},{9,11},{10,... | collective-permute-start | bytes 417800 | tf_op jit(solution)/shard_map/ppermute | solution.py:34
  46.4 4.9 %collective-permute-start.15 = (bf16[1,128,128]{2,1,0:T(8,128)(2,1)S(1)}, bf16[1,128,128]{2,1,0:T(8,128)(2,1)S(1)}, u32[]{:S(2)}, u32[]{:S(2)}) collective-permute-start(bf16[1,128,128]{2,1,0:T(8,128)(2,1)S(1)} %slice.41), channel_id=1, source_target_pairs={{0,8},{1,9},{2,10},{3,11},{4,12},{5,13},{6,14},{7,15},{8,0},{9,1},... | collective-permute-start | bytes 98312 | tf_op jit(solution)/shard_map/ppermute | solution.py:34
  49.0 2.4 %collective-permute-start.17 = (f32[136,128]{1,0:T(8,128)S(1)}, f32[136,128]{1,0:T(8,128)S(1)}, u32[]{:S(2)}, u32[]{:S(2)}) collective-permute-start(f32[136,128]{1,0:T(8,128)S(1)} %get-tuple-element.53), channel_id=1, source_target_pairs={{0,1},{1,0},{2,3},{3,2},{4,5},{5,4},{6,7},{7,6},{8,9},{9,8},{10,11... | collective-permute-start | bytes 208904 | tf_op jit(solution)/shard_map/ppermute | solution.py:34

commit v4 on v3

--- a/solution.py
+++ b/solution.py
@@ -174,19 +174,21 @@
         masked_ref[lines, :] = jnp.where(dots[lines, :] > 0, weight, 0.0)
 
 
-def gradient_of(key_total, row_parts, places, near_ref, far_ref, total_ref, exps, indexes, own_keys):
+def gradient_of(key_total, row_parts, places, sums, total_ref, exps, indexes, own_keys):
     rows, head_count = total_ref.shape
     own_rows = rows // row_parts
     for r in range(row_parts):
         lines = slice(0, own_rows)
-        total_ref[r * own_rows : (r + 1) * own_rows, :] = near_ref[r, lines, :] + far_ref[r ^ 1, lines, :]
+        total_ref[r * own_rows : (r + 1) * own_rows, :] = sum(
+            s[r ^ m, lines, :] for m, s in enumerate(sums)
+        )
     shares = jnp.transpose(1.0 / total_ref[...])
     gradients = []
     for t in range(rows):
         r, i = divmod(t, own_rows)
         share = shares[:, t : t + 1]
         at = own_rows + i
-        index_total = near_ref[r, at : at + 1, :1] + far_ref[r ^ 1, at : at + 1, :1]
+        index_total = sum(s[r ^ m, at : at + 1, :1] for m, s in enumerate(sums))
         target = jnp.concatenate(
             [
                 jnp.sum(exps[n][t, :, p : p + own_keys] * share, axis=0, keepdims=True)
@@ -203,12 +205,13 @@
 
 def first_grad_kernel(key_total, row_parts, places, *refs):
     count = 1 + max(n for n, _ in places)
-    near_ref, far_ref, flat_ref, masked_ref = refs[:4]
+    sums, refs = refs[:row_parts], refs[row_parts - 2 :]
+    flat_ref, masked_ref = refs[2:4]
     exps, indexes = refs[4 : 4 + count], refs[4 + count : 4 + 2 * count]
     key_ref, dots_ref, gradient_ref, total_ref = refs[4 + 2 * count :]
     own_keys = key_ref.shape[1]
     gradients = gradient_of(
-        key_total, row_parts, places, near_ref, far_ref, total_ref, exps, indexes, own_keys
+        key_total, row_parts, places, sums, total_ref, exps, indexes, own_keys
     )
     index_heads = flat_ref.shape[0] // len(gradients)
     for t, gradient in enumerate(gradients):
@@ -222,7 +225,8 @@
 
 def grad_kernel(key_total, row_parts, places, *refs):
     count = 1 + max(n for n, _ in places)
-    near_ref, far_ref, flat_ref, column_ref = refs[:4]
+    sums, refs = refs[:row_parts], refs[row_parts - 2 :]
+    flat_ref, column_ref = refs[2:4]
     exps, indexes = refs[4 : 4 + count], refs[4 + count : 4 + 2 * count]
     refs = refs[4 + 2 * count :]
     blocks, refs = refs[: len(places)], refs[len(places) :]
@@ -237,7 +241,7 @@
     flat = flat_ref[...]
     dots = contract(flat, ikeys, (1, 1))
     gradients = gradient_of(
-        key_total, row_parts, places, near_ref, far_ref, total_ref, exps, indexes, own_keys
+        key_total, row_parts, places, sums, total_ref, exps, indexes, own_keys
     )
     lane = lax.broadcasted_iota(jnp.int32, (index_heads, LANES), 1)
     columns = jnp.zeros((index_heads, LANES), f32)
@@ -360,12 +364,10 @@
         indexes.append(out[1])
         sums = out[2] if sums is None else sums + out[2]
 
-    bit = row_parts // 2
-    while bit > 1:
-        got = swap(sums, bit, count)
-        sums = sums + jnp.stack([got[r ^ bit] for r in range(row_parts)])
-        bit //= 2
-    got = swap(sums, 1, count)
+    sums = [sums]
+    for mask in (2, 3, 1):
+        sums.append(swap(sums[0], mask, count))
+    sums = [sums[0], sums[3], sums[1], sums[2]]
 
     place = {k: (n, p * own_keys) for n, piece in enumerate(pieces) for p, k in enumerate(piece)}
     teams = [list(range(key_parts))] if key_parts <= step else pieces
@@ -391,11 +393,11 @@
             scratch = (pltpu.VMEM((rows, head_count), f32),)
             if part:
                 kernel = first_grad_kernel
-                operands = (sums, got, laid[1], masked, *stored)
+                operands = (*sums, laid[1], masked, *stored)
                 shapes += (more, struct((rows, half * own_keys), f32))
             else:
                 kernel = grad_kernel
-                operands = (sums, got, *laid[1:3], *stored, *(blocks[k] for k in mine))
+                operands = (*sums, *laid[1:3], *stored, *(blocks[k] for k in mine))
                 operands += (*early, heads, *(blocks[k] for k in ids[1::2]))
                 shapes += (struct((row_parts // 2, tall, index_width), f32),) * 2
                 scratch = (pltpu.VMEM(more.shape, bf16), *scratch)

time: 52.2 us -> 51.9 us (level)
  starting transfers between devices: 16.3 us -> 15.6 us
    ppermute x18 -> x19, starting transfers between devices: 16.3 us -> 15.6 us  [swap(): return lax.ppermute(array, 'ctx', [(i, i ^ mask) for i in range(count)])]
    ppermute x18 -> x19, waiting for transfers between devices: 28.9 us -> 29.3 us  [swap(): return lax.ppermute(array, 'ctx', [(i, i ^ mask) for i in range(count)])]
  transfers between devices with their start and end apart: 18 -> 19, of which waited for: 12 -> 12; matrix products, arithmetic and copies ran while one was open for 0% -> 0% of each run, Pallas kernels for 8% -> 8%
where the time goes in v4:
time: 51.9 us; the launch traced here: 51.7 us
  waiting for transfers between devices  29.3 us (56%)
  starting transfers between devices  15.6 us (30%)
  Pallas kernels  6.03 us (12%)
  between operations  0.74 us (1%)
    ppermute x19, waiting for transfers between devices, swap(): return lax.ppermute(array, 'ctx', [(i, i ^ mask) for i in range(count)])  29.3 us
    ppermute x19, starting transfers between devices, swap(): return lax.ppermute(array, 'ctx', [(i, i ^ mask) for i in range(count)])  15.6 us
    pallas_call x6, Pallas kernels, kernel_call(): pl.pallas_call(kernel, out_shape=tuple(shapes), scratch_shapes=list(scrat...  4.9 us
    pallas_call x1, Pallas kernels, body(): pl.pallas_call(pack_kernel, out_shape=(struct((own_keys + 16, own_keys),...  1.13 us
  transfers between devices with their start and end apart: 19, of which 12 were waited for; matrix products, arithmetic and copies ran while one was open for 0% of the time, Pallas kernels for 8%

profile of v4, /device:TPU:0, one launch (start us, length us, event | category | flops | bytes accessed | tf_op | source)
XLA Modules:
  0.0 51.7 jit_solution(10599264254813876945)
XLA Ops:
  0.6 3.0 %collective-permute-start.1 = (bf16[2,576,128]{2,1,0:T(8,128)(2,1)}, bf16[2,576,128]{2,1,0:T(8,128)(2,1)S(1)}, u32[]{:S(2)}, u32[]{:S(2)}) collective-permute-start(bf16[2,576,128]{2,1,0:T(8,128)(2,1)} %bitcast.13), channel_id=1, source_target_pairs={{0,2},{1,3},{2,0},{3,1},{4,6},{5,7},{6,4},{7,5},{8,10},{9,11},{10,... | collective-permute-start | bytes 884744 | tf_op jit(solution)/shard_map/ppermute | solution.py:34
  3.7 0.0 collective-permute-start
  3.7 7.2 %collective-permute-done.1.refs_2_ = bf16[2,576,128]{2,1,0:T(8,128)(2,1)S(1)} collective-permute-done((bf16[2,576,128]{2,1,0:T(8,128)(2,1)}, bf16[2,576,128]{2,1,0:T(8,128)(2,1)S(1)}, u32[]{:S(2)}, u32[]{:S(2)}) %collective-permute-start.1) | collective-permute-done | bytes 294944 | tf_op jit(solution)/shard_map/ppermute | solution.py:34
  10.9 0.0 collective-permute-start.2
  10.9 2.8 %collective-permute-start.7 = (bf16[576,128]{1,0:T(8,128)(2,1)}, bf16[576,128]{1,0:T(8,128)(2,1)S(1)}, u32[]{:S(2)}, u32[]{:S(2)}) collective-permute-start(bf16[576,128]{1,0:T(8,128)(2,1)} %bitcast.16), channel_id=1, source_target_pairs={{0,8},{1,9},{2,10},{3,11},{4,12},{5,13},{6,14},{7,15},{8,0},{9,1},... | collective-permute-start | bytes 442376 | tf_op jit(solution)/shard_map/ppermute | solution.py:34
  13.7 1.1 %pack.1 = (bf16[144,128]{1,0:T(8,128)(2,1)S(1)}, bf16[144,128]{1,0:T(8,128)(2,1)S(1)}, bf16[2,576,128]{2,1,0:T(8,128)(2,1)S(1)}, bf16[576,128]{1,0:T(8,128)(2,1)S(1)}) custom-call(s32[4,128]{1,0:T(4,128)} %bitcast.20, bf16[128,128]{1,0:T(8,128)(2,1)} %keys_hbm.1, f32[2,64]{1,0:T(2,128)} %weight_hbm.1, s32[2]{0:T(128)} %pos_hbm.1, ...), custom_call_target="tpu_custom_call" | custom-call | tf_op jit(solution)/shard_map/pack/pallas_call | solution.py:306
  14.9 0.3 collective-permute-start.3
  15.2 1.5 %collective-permute-start.4 = (bf16[144,128]{1,0:T(8,128)(2,1)S(1)}, bf16[144,128]{1,0:T(8,128)(2,1)S(1)}, u32[]{:S(2)}, u32[]{:S(2)}) collective-permute-start(bf16[144,128]{1,0:T(8,128)(2,1)S(1)} %get-tuple-element.29.refs_4_), channel_id=1, source_target_pairs={{0,2},{1,3},{2,0},{3,1},{4,6},{5,7},{6,4},{7,5},{8,10},{9,11},{10,... | collective-permute-start | bytes 110600 | tf_op jit(solution)/shard_map/ppermute | solution.py:34
  16.6 0.0 collective-permute-done.3.refs_5_
  16.7 1.6 %collective-permute-start.6 = (bf16[576,128]{1,0:T(8,128)(2,1)}, bf16[576,128]{1,0:T(8,128)(2,1)S(1)}, u32[]{:S(2)}, u32[]{:S(2)}) collective-permute-start(bf16[576,128]{1,0:T(8,128)(2,1)} %bitcast.18), channel_id=1, source_target_pairs={{0,4},{1,5},{2,6},{3,7},{4,0},{5,1},{6,2},{7,3},{8,12},{9,13},{10,... | collective-permute-start | bytes 442376 | tf_op jit(solution)/shard_map/ppermute | solution.py:34
  18.2 0.9 %collective-permute-done.4.refs_6_ = bf16[144,128]{1,0:T(8,128)(2,1)S(1)} collective-permute-done((bf16[144,128]{1,0:T(8,128)(2,1)S(1)}, bf16[144,128]{1,0:T(8,128)(2,1)S(1)}, u32[]{:S(2)}, u32[]{:S(2)}) %collective-permute-start.4) | collective-permute-done | bytes 36896 | tf_op jit(solution)/shard_map/ppermute | solution.py:34
  19.1 1.6 %collective-permute-start.8 = (bf16[144,128]{1,0:T(8,128)(2,1)S(1)}, bf16[144,128]{1,0:T(8,128)(2,1)S(1)}, u32[]{:S(2)}, u32[]{:S(2)}) collective-permute-start(bf16[144,128]{1,0:T(8,128)(2,1)S(1)} %get-tuple-element.31.refs_11_.refs_8_), channel_id=1, source_target_pairs={{0,4},{1,5},{2,6},{3,7},{4,0},{5,1},{6,2},{7,3},{8,12},{9,13},{10,... | collective-permute-start | bytes 110600 | tf_op jit(solution)/shard_map/ppermute | solution.py:34
  20.7 1.0 %collective-permute-done.7.refs_10_ = bf16[576,128]{1,0:T(8,128)(2,1)S(1)} collective-permute-done((bf16[576,128]{1,0:T(8,128)(2,1)}, bf16[576,128]{1,0:T(8,128)(2,1)S(1)}, u32[]{:S(2)}, u32[]{:S(2)}) %collective-permute-start.7) | collective-permute-done | bytes 147488 | tf_op jit(solution)/shard_map/ppermute | solution.py:34
  21.7 0.8 %collective-permute-start.10 = (bf16[576,128]{1,0:T(8,128)(2,1)S(1)}, bf16[576,128]{1,0:T(8,128)(2,1)S(1)}, u32[]{:S(2)}, u32[]{:S(2)}) collective-permute-start(bf16[576,128]{1,0:T(8,128)(2,1)S(1)} %collective-permute-done.7.refs_10_), channel_id=1, source_target_pairs={{0,4},{1,5},{2,6},{3,7},{4,0},{5,1},{6,2},{7,3},{8,12},{9,13},{10,... | collective-permute-start | bytes 442376 | tf_op jit(solution)/shard_map/ppermute | solution.py:34
  22.5 3.2 %collective-permute-done.8.refs_12_.refs_0_.refs_13_ = bf16[144,128]{1,0:T(8,128)(2,1)S(1)} collective-permute-done((bf16[144,128]{1,0:T(8,128)(2,1)S(1)}, bf16[144,128]{1,0:T(8,128)(2,1)S(1)}, u32[]{:S(2)}, u32[]{:S(2)}) %collective-permute-start.8) | collective-permute-done | bytes 36896 | tf_op jit(solution)/shard_map/ppermute | solution.py:34
  25.7 0.2 collective-permute-start.9
  25.9 4.6 %collective-permute-done.9.refs_13_.refs_9_ = bf16[144,128]{1,0:T(8,128)(2,1)S(1)} collective-permute-done((bf16[144,128]{1,0:T(8,128)(2,1)S(1)}, bf16[144,128]{1,0:T(8,128)(2,1)S(1)}, u32[]{:S(2)}, u32[]{:S(2)}) %collective-permute-start.9) | collective-permute-done | bytes 36896 | tf_op jit(solution)/shard_map/ppermute | solution.py:34
  30.5 0.0 collective-permute-start.5
  30.5 1.2 %collective-permute-done.5.refs_7_ = bf16[144,128]{1,0:T(8,128)(2,1)S(1)} collective-permute-done((bf16[144,128]{1,0:T(8,128)(2,1)S(1)}, bf16[144,128]{1,0:T(8,128)(2,1)S(1)}, u32[]{:S(2)}, u32[]{:S(2)}) %collective-permute-start.5) | collective-permute-done | bytes 36896 | tf_op jit(solution)/shard_map/ppermute | solution.py:34
  31.7 0.1 collective-permute-start.11
  31.9 0.0 collective-permute-done.6.refs_9_
  31.9 0.0 collective-permute-done.refs_1_
  31.9 0.0 collective-permute-done.2.refs_3_
  31.9 1.6 %shard_map.94 = (f32[8,128,384]{2,1,0:T(8,128)S(1)}, f32[8,384]{1,0:T(8,128)S(1)}, f32[4,4,128]{2,1,0:T(4,128)S(1)}, bf16[1024,576]{1,0:T(8,128)(2,1)S(1)}, bf16...) custom-call(bf16[2,576,128]{2,1,0:T(8,128)(2,1)S(1)} %get-tuple-element.28.refs_0_, ...), custom_call_target="tpu_custom_call" | custom-call | flops 452984832 | bytes 4790272 | tf_op jit(solution)/shard_map/pallas_call | solution.py:20
  33.5 2.2 %collective-permute-done.11.refs_5_.refs_1_.refs_14_ = bf16[144,128]{1,0:T(8,128)(2,1)S(1)} collective-permute-done((bf16[144,128]{1,0:T(8,128)(2,1)S(1)}, bf16[144,128]{1,0:T(8,128)(2,1)S(1)}, u32[]{:S(2)}, u32[]{:S(2)}) %collective-permute-start.11) | collective-permute-done | bytes 36896 | tf_op jit(solution)/shard_map/ppermute | solution.py:34
  35.7 0.0 collective-permute-done.10.refs_4_
  35.7 0.7 %shard_map.95 = (f32[8,128,128]{2,1,0:T(8,128)S(1)}, f32[8,128]{1,0:T(8,128)S(1)}, f32[4,4,128]{2,1,0:T(4,128)S(1)}) custom-call(bf16[1024,576]{1,0:T(8,128)(2,1)S(1)} %get-tuple-element.33.refs_0_, bf16[512,128]{1,0:T(8,128)(2,1)S(1)} %get-tuple-element.34.refs_1_.flat_ref.refs_4_, f32[64,8]{1,0:T(8,128)S(1)} %get-tuple-element.35.refs_2_.column_ref.refs_5_, ...), custom_call_target="tpu_custom_call" | custom-call | flops 150994944 | bytes 2037760 | tf_op jit(solution)/shard_map/pallas_call | solution.py:20
  36.4 0.1 collective-permute-start.12
  36.5 1.5 %collective-permute-start.13 = (f32[4,4,128]{2,1,0:T(4,128)S(1)}, f32[4,4,128]{2,1,0:T(4,128)S(1)}, u32[]{:S(2)}, u32[]{:S(2)}) collective-permute-start(f32[4,4,128]{2,1,0:T(4,128)S(1)} %add.9.refs_0_), channel_id=1, source_target_pairs={{0,2},{1,3},{2,0},{3,1},{4,6},{5,7},{6,4},{7,5},{8,10},{9,11},{10,... | collective-permute-start | bytes 24584 | tf_op jit(solution)/shard_map/ppermute | solution.py:34
  38.0 0.3 collective-permute-start.14
  38.3 0.2 shard_map.96
  38.6 0.0 collective-permute-done.12.refs_1_
  38.6 1.6 %collective-permute-done.13.refs_2_ = f32[4,4,128]{2,1,0:T(4,128)S(1)} collective-permute-done((f32[4,4,128]{2,1,0:T(4,128)S(1)}, f32[4,4,128]{2,1,0:T(4,128)S(1)}, u32[]{:S(2)}, u32[]{:S(2)}) %collective-permute-start.13) | collective-permute-done | bytes 8224 | tf_op jit(solution)/shard_map/ppermute | solution.py:34
  40.2 0.9 %collective-permute-done.14.refs_3_ = f32[4,4,128]{2,1,0:T(4,128)S(1)} collective-permute-done((f32[4,4,128]{2,1,0:T(4,128)S(1)}, f32[4,4,128]{2,1,0:T(4,128)S(1)}, u32[]{:S(2)}, u32[]{:S(2)}) %collective-permute-start.14) | collective-permute-done | bytes 8224 | tf_op jit(solution)/shard_map/ppermute | solution.py:34
  41.1 0.7 %shard_map.97 = (bf16[2,128,128]{2,1,0:T(8,128)(2,1)S(1)}, bf16[512,256]{1,0:T(8,128)(2,1)S(1)}, f32[8,256]{1,0:T(8,128)S(1)}) custom-call(f32[4,4,128]{2,1,0:T(4,128)S(1)} %add.9.refs_0_, f32[4,4,128]{2,1,0:T(4,128)S(1)} %collective-permute-done.12.refs_1_, f32[4,4,128]{2,1,0:T(4,128)S(1)} %collective-permute-done.13.refs_2_, ...), custom_call_target="tpu_custom_call" | custom-call | flops 67108864 | bytes 3137536 | tf_op jit(solution)/shard_map/pallas_call | solution.py:20
  41.8 0.2 collective-permute-start.15
  42.0 1.0 %shard_map.98 = (f32[2,128,128]{2,1,0:T(8,128)S(1)}, f32[2,136,128]{2,1,0:T(8,128)S(1)}, f32[2,136,128]{2,1,0:T(8,128)S(1)}) custom-call(f32[4,4,128]{2,1,0:T(4,128)S(1)} %add.9.refs_0_, f32[4,4,128]{2,1,0:T(4,128)S(1)} %collective-permute-done.12.refs_1_, f32[4,4,128]{2,1,0:T(4,128)S(1)} %collective-permute-done.13.refs_2_, ...), custom_call_target="tpu_custom_call" | custom-call | flops 67108864 | bytes 3102720 | tf_op jit(solution)/shard_map/pallas_call | solution.py:20
  43.0 0.7 %collective-permute-start.17 = (f32[2,136,128]{2,1,0:T(8,128)S(1)}, f32[2,136,128]{2,1,0:T(8,128)S(1)}, u32[]{:S(2)}, u32[]{:S(2)}) collective-permute-start(f32[2,136,128]{2,1,0:T(8,128)S(1)} %get-tuple-element.49), channel_id=1, source_target_pairs={{0,2},{1,3},{2,0},{3,1},{4,6},{5,7},{6,4},{7,5},{8,10},{9,11},{10,... | collective-permute-start | bytes 417800 | tf_op jit(solution)/shard_map/ppermute | solution.py:34
  43.7 2.4 %collective-permute-done.15 = bf16[2,128,128]{2,1,0:T(8,128)(2,1)S(1)} collective-permute-done((bf16[2,128,128]{2,1,0:T(8,128)(2,1)S(1)}, bf16[2,128,128]{2,1,0:T(8,128)(2,1)S(1)}, u32[]{:S(2)}, u32[]{:S(2)}) %collective-permute-start.15) | collective-permute-done | bytes 65568 | tf_op jit(solution)/shard_map/ppermute | solution.py:34
  46.1 0.7 %collective-permute-start.16 = (bf16[1,128,128]{2,1,0:T(8,128)(2,1)S(1)}, bf16[1,128,128]{2,1,0:T(8,128)(2,1)S(1)}, u32[]{:S(2)}, u32[]{:S(2)}) collective-permute-start(bf16[1,128,128]{2,1,0:T(8,128)(2,1)S(1)} %slice.27), channel_id=1, source_target_pairs={{0,8},{1,9},{2,10},{3,11},{4,12},{5,13},{6,14},{7,15},{8,0},{9,1},... | collective-permute-start | bytes 98312 | tf_op jit(solution)/shard_map/ppermute | solution.py:34
  46.8 1.8 %collective-permute-done.17 = f32[2,136,128]{2,1,0:T(8,128)S(1)} collective-permute-done((f32[2,136,128]{2,1,0:T(8,128)S(1)}, f32[2,136,128]{2,1,0:T(8,128)S(1)}, u32[]{:S(2)}, u32[]{:S(2)}) %collective-permute-start.17) | collective-permute-done | bytes 139296 | tf_op jit(solution)/shard_map/ppermute | solution.py:34
  48.7 0.1 collective-permute-start.18
  48.8 2.2 %collective-permute-done.16 = bf16[1,128,128]{2,1,0:T(8,128)(2,1)S(1)} collective-permute-done((bf16[1,128,128]{2,1,0:T(8,128)(2,1)S(1)}, bf16[1,128,128]{2,1,0:T(8,128)(2,1)S(1)}, u32[]{:S(2)}, u32[]{:S(2)}) %collective-permute-start.16) | collective-permute-done | bytes 32800 | tf_op jit(solution)/shard_map/ppermute | solution.py:34
  51.0 0.0 collective-permute-done.18.row_got_ref
  51.0 0.7 %shard_map.99 = (f32[128,128]{1,0:T(8,128)}, f32[2,64]{1,0:T(2,128)}, f32[128,128]{1,0:T(8,128)}) custom-call(f32[128,128]{1,0:T(8,128)S(1)} %slice_bitcast_fusion.2.key_ref, bf16[128,128]{1,0:T(8,128)(2,1)S(1)} %bitcast.12, f32[136,128]{1,0:T(8,128)S(1)} %get-tuple-element.54.row_ref, f32[136,128]{1,0:T(8,128)S(1)} %collective-permute-done.18.row_got_ref), custom_call_target="tpu_custom_call" | custom-call | bytes 369152 | tf_op jit(solution)/shard_map/pallas_call | solution.py:20
  (6 shorter events, 0.1 us)
Async XLA Ops:
  0.6 10.2 %collective-permute-start.1 = (bf16[2,576,128]{2,1,0:T(8,128)(2,1)}, bf16[2,576,128]{2,1,0:T(8,128)(2,1)S(1)}, u32[]{:S(2)}, u32[]{:S(2)}) collective-permute-start(bf16[2,576,128]{2,1,0:T(8,128)(2,1)} %bitcast.13), channel_id=1, source_target_pairs={{0,2},{1,3},{2,0},{3,1},{4,6},{5,7},{6,4},{7,5},{8,10},{9,11},{10,... | collective-permute-start | bytes 884744 | tf_op jit(solution)/shard_map/ppermute | solution.py:34
  3.7 28.2 %collective-permute-start = (bf16[2,576,128]{2,1,0:T(8,128)(2,1)}, bf16[2,576,128]{2,1,0:T(8,128)(2,1)S(1)}, u32[]{:S(2)}, u32[]{:S(2)}) collective-permute-start(bf16[2,576,128]{2,1,0:T(8,128)(2,1)} %bitcast.14), channel_id=1, source_target_pairs={{0,1},{1,0},{2,3},{3,2},{4,5},{5,4},{6,7},{7,6},{8,9},{9,8},{10,11... | collective-permute-start | bytes 884744 | tf_op jit(solution)/shard_map/ppermute | solution.py:34
  10.9 21.0 %collective-permute-start.2 = (bf16[2,576,128]{2,1,0:T(8,128)(2,1)S(1)}, bf16[2,576,128]{2,1,0:T(8,128)(2,1)S(1)}, u32[]{:S(2)}, u32[]{:S(2)}) collective-permute-start(bf16[2,576,128]{2,1,0:T(8,128)(2,1)S(1)} %collective-permute-done.1.refs_2_), channel_id=1, source_target_pairs={{0,1},{1,0},{2,3},{3,2},{4,5},{5,4},{6,7},{7,6},{8,9},{9,8},{10,11... | collective-permute-start | bytes 884744 | tf_op jit(solution)/shard_map/ppermute | solution.py:34
  10.9 10.8 %collective-permute-start.7 = (bf16[576,128]{1,0:T(8,128)(2,1)}, bf16[576,128]{1,0:T(8,128)(2,1)S(1)}, u32[]{:S(2)}, u32[]{:S(2)}) collective-permute-start(bf16[576,128]{1,0:T(8,128)(2,1)} %bitcast.16), channel_id=1, source_target_pairs={{0,8},{1,9},{2,10},{3,11},{4,12},{5,13},{6,14},{7,15},{8,0},{9,1},... | collective-permute-start | bytes 442376 | tf_op jit(solution)/shard_map/ppermute | solution.py:34
  14.9 1.8 %collective-permute-start.3 = (bf16[144,128]{1,0:T(8,128)(2,1)S(1)}, bf16[144,128]{1,0:T(8,128)(2,1)S(1)}, u32[]{:S(2)}, u32[]{:S(2)}) collective-permute-start(bf16[144,128]{1,0:T(8,128)(2,1)S(1)} %get-tuple-element.29.refs_4_), channel_id=1, source_target_pairs={{0,1},{1,0},{2,3},{3,2},{4,5},{5,4},{6,7},{7,6},{8,9},{9,8},{10,11... | collective-permute-start | bytes 110600 | tf_op jit(solution)/shard_map/ppermute | solution.py:34
  15.2 4.0 %collective-permute-start.4 = (bf16[144,128]{1,0:T(8,128)(2,1)S(1)}, bf16[144,128]{1,0:T(8,128)(2,1)S(1)}, u32[]{:S(2)}, u32[]{:S(2)}) collective-permute-start(bf16[144,128]{1,0:T(8,128)(2,1)S(1)} %get-tuple-element.29.refs_4_), channel_id=1, source_target_pairs={{0,2},{1,3},{2,0},{3,1},{4,6},{5,7},{6,4},{7,5},{8,10},{9,11},{10,... | collective-permute-start | bytes 110600 | tf_op jit(solution)/shard_map/ppermute | solution.py:34
  16.7 15.2 %collective-permute-start.6 = (bf16[576,128]{1,0:T(8,128)(2,1)}, bf16[576,128]{1,0:T(8,128)(2,1)S(1)}, u32[]{:S(2)}, u32[]{:S(2)}) collective-permute-start(bf16[576,128]{1,0:T(8,128)(2,1)} %bitcast.18), channel_id=1, source_target_pairs={{0,4},{1,5},{2,6},{3,7},{4,0},{5,1},{6,2},{7,3},{8,12},{9,13},{10,... | collective-permute-start | bytes 442376 | tf_op jit(solution)/shard_map/ppermute | solution.py:34
  19.1 6.5 %collective-permute-start.8 = (bf16[144,128]{1,0:T(8,128)(2,1)S(1)}, bf16[144,128]{1,0:T(8,128)(2,1)S(1)}, u32[]{:S(2)}, u32[]{:S(2)}) collective-permute-start(bf16[144,128]{1,0:T(8,128)(2,1)S(1)} %get-tuple-element.31.refs_11_.refs_8_), channel_id=1, source_target_pairs={{0,4},{1,5},{2,6},{3,7},{4,0},{5,1},{6,2},{7,3},{8,12},{9,13},{10,... | collective-permute-start | bytes 110600 | tf_op jit(solution)/shard_map/ppermute | solution.py:34
  21.7 14.0 %collective-permute-start.10 = (bf16[576,128]{1,0:T(8,128)(2,1)S(1)}, bf16[576,128]{1,0:T(8,128)(2,1)S(1)}, u32[]{:S(2)}, u32[]{:S(2)}) collective-permute-start(bf16[576,128]{1,0:T(8,128)(2,1)S(1)} %collective-permute-done.7.refs_10_), channel_id=1, source_target_pairs={{0,4},{1,5},{2,6},{3,7},{4,0},{5,1},{6,2},{7,3},{8,12},{9,13},{10,... | collective-permute-start | bytes 442376 | tf_op jit(solution)/shard_map/ppermute | solution.py:34
  25.7 4.9 %collective-permute-start.9 = (bf16[144,128]{1,0:T(8,128)(2,1)S(1)}, bf16[144,128]{1,0:T(8,128)(2,1)S(1)}, u32[]{:S(2)}, u32[]{:S(2)}) collective-permute-start(bf16[144,128]{1,0:T(8,128)(2,1)S(1)} %get-tuple-element.31.refs_11_.refs_8_), channel_id=1, source_target_pairs={{0,8},{1,9},{2,10},{3,11},{4,12},{5,13},{6,14},{7,15},{8,0},{9,1},... | collective-permute-start | bytes 110600 | tf_op jit(solution)/shard_map/ppermute | solution.py:34
  30.5 1.2 %collective-permute-start.5 = (bf16[144,128]{1,0:T(8,128)(2,1)S(1)}, bf16[144,128]{1,0:T(8,128)(2,1)S(1)}, u32[]{:S(2)}, u32[]{:S(2)}) collective-permute-start(bf16[144,128]{1,0:T(8,128)(2,1)S(1)} %collective-permute-done.4.refs_6_), channel_id=1, source_target_pairs={{0,1},{1,0},{2,3},{3,2},{4,5},{5,4},{6,7},{7,6},{8,9},{9,8},{10,11... | collective-permute-start | bytes 110600 | tf_op jit(solution)/shard_map/ppermute | solution.py:34
  31.7 4.0 %collective-permute-start.11 = (bf16[144,128]{1,0:T(8,128)(2,1)S(1)}, bf16[144,128]{1,0:T(8,128)(2,1)S(1)}, u32[]{:S(2)}, u32[]{:S(2)}) collective-permute-start(bf16[144,128]{1,0:T(8,128)(2,1)S(1)} %collective-permute-done.9.refs_13_.refs_9_), channel_id=1, source_target_pairs={{0,4},{1,5},{2,6},{3,7},{4,0},{5,1},{6,2},{7,3},{8,12},{9,13},{10,... | collective-permute-start | bytes 110600 | tf_op jit(solution)/shard_map/ppermute | solution.py:34
  36.4 2.2 %collective-permute-start.12 = (f32[4,4,128]{2,1,0:T(4,128)S(1)}, f32[4,4,128]{2,1,0:T(4,128)S(1)}, u32[]{:S(2)}, u32[]{:S(2)}) collective-permute-start(f32[4,4,128]{2,1,0:T(4,128)S(1)} %add.9.refs_0_), channel_id=1, source_target_pairs={{0,1},{1,0},{2,3},{3,2},{4,5},{5,4},{6,7},{7,6},{8,9},{9,8},{10,11... | collective-permute-start | bytes 24584 | tf_op jit(solution)/shard_map/ppermute | solution.py:34
  36.5 3.7 %collective-permute-start.13 = (f32[4,4,128]{2,1,0:T(4,128)S(1)}, f32[4,4,128]{2,1,0:T(4,128)S(1)}, u32[]{:S(2)}, u32[]{:S(2)}) collective-permute-start(f32[4,4,128]{2,1,0:T(4,128)S(1)} %add.9.refs_0_), channel_id=1, source_target_pairs={{0,2},{1,3},{2,0},{3,1},{4,6},{5,7},{6,4},{7,5},{8,10},{9,11},{10,... | collective-permute-start | bytes 24584 | tf_op jit(solution)/shard_map/ppermute | solution.py:34
  38.0 3.1 %collective-permute-start.14 = (f32[4,4,128]{2,1,0:T(4,128)S(1)}, f32[4,4,128]{2,1,0:T(4,128)S(1)}, u32[]{:S(2)}, u32[]{:S(2)}) collective-permute-start(f32[4,4,128]{2,1,0:T(4,128)S(1)} %add.9.refs_0_), channel_id=1, source_target_pairs={{0,3},{1,2},{2,1},{3,0},{4,7},{5,6},{6,5},{7,4},{8,11},{9,10},{10,... | collective-permute-start | bytes 24584 | tf_op jit(solution)/shard_map/ppermute | solution.py:34
  41.8 4.3 %collective-permute-start.15 = (bf16[2,128,128]{2,1,0:T(8,128)(2,1)S(1)}, bf16[2,128,128]{2,1,0:T(8,128)(2,1)S(1)}, u32[]{:S(2)}, u32[]{:S(2)}) collective-permute-start(bf16[2,128,128]{2,1,0:T(8,128)(2,1)S(1)} %get-tuple-element.47), channel_id=1, source_target_pairs={{0,4},{1,5},{2,6},{3,7},{4,0},{5,1},{6,2},{7,3},{8,12},{9,13},{10,... | collective-permute-start | bytes 196616 | tf_op jit(solution)/shard_map/ppermute | solution.py:34
  43.0 5.7 %collective-permute-start.17 = (f32[2,136,128]{2,1,0:T(8,128)S(1)}, f32[2,136,128]{2,1,0:T(8,128)S(1)}, u32[]{:S(2)}, u32[]{:S(2)}) collective-permute-start(f32[2,136,128]{2,1,0:T(8,128)S(1)} %get-tuple-element.49), channel_id=1, source_target_pairs={{0,2},{1,3},{2,0},{3,1},{4,6},{5,7},{6,4},{7,5},{8,10},{9,11},{10,... | collective-permute-start | bytes 417800 | tf_op jit(solution)/shard_map/ppermute | solution.py:34
  46.1 4.9 %collective-permute-start.16 = (bf16[1,128,128]{2,1,0:T(8,128)(2,1)S(1)}, bf16[1,128,128]{2,1,0:T(8,128)(2,1)S(1)}, u32[]{:S(2)}, u32[]{:S(2)}) collective-permute-start(bf16[1,128,128]{2,1,0:T(8,128)(2,1)S(1)} %slice.27), channel_id=1, source_target_pairs={{0,8},{1,9},{2,10},{3,11},{4,12},{5,13},{6,14},{7,15},{8,0},{9,1},... | collective-permute-start | bytes 98312 | tf_op jit(solution)/shard_map/ppermute | solution.py:34
  48.7 2.3 %collective-permute-start.18 = (f32[136,128]{1,0:T(8,128)S(1)}, f32[136,128]{1,0:T(8,128)S(1)}, u32[]{:S(2)}, u32[]{:S(2)}) collective-permute-start(f32[136,128]{1,0:T(8,128)S(1)} %get-tuple-element.53), channel_id=1, source_target_pairs={{0,1},{1,0},{2,3},{3,2},{4,5},{5,4},{6,7},{7,6},{8,9},{9,8},{10,11... | collective-permute-start | bytes 208904 | tf_op jit(solution)/shard_map/ppermute | solution.py:34

commit v5 on v4

--- a/solution.py
+++ b/solution.py
@@ -97,14 +97,23 @@
     return jnp.concatenate([*latent, codes_ref[groups * group_width :, :]], axis=0)
 
 
+def lay_kernel(*refs):
+    queries, main_ref = refs[:-1], refs[-1]
+    own_rows, _, head_count = queries[0].shape
+    for r, query in enumerate(queries):
+        for i in range(own_rows):
+            t = r * own_rows + i
+            main_ref[t * head_count : (t + 1) * head_count, :] = jnp.transpose(query[i])
+
+
 def score_kernel(offsets, row_parts, groups, first, *refs):
     parts = len(offsets)
     if first:
-        queries, iqueries = refs[:row_parts], refs[row_parts : 2 * row_parts]
-        refs = refs[2 * row_parts :]
+        early_ref, query, iqueries = refs[0], refs[1], refs[2 : 2 + row_parts]
+        refs = refs[2 + row_parts :]
         codes, blocks, refs = refs[:parts], refs[parts : 2 * parts], refs[2 * parts :]
         exp_ref, index_ref, sums_ref, main_ref, flat_ref, column_ref, pos_ref, side_ref = refs
-        own_rows, head_count = queries[0].shape[0], queries[0].shape[2]
+        own_rows, head_count = query.shape[0], query.shape[2]
         lines = flat_ref.shape[0] // row_parts
         index_heads = lines // own_rows
         for r in range(row_parts):
@@ -113,22 +122,22 @@
             side = side + tail[2 * own_rows : 3 * own_rows]
             side_ref[r * own_rows : (r + 1) * own_rows, :] = side
             flat_ref[r * lines : (r + 1) * lines, :] = iqueries[r][:lines, :]
-            for i in range(own_rows):
-                t = r * own_rows + i
-                main_ref[t * head_count : (t + 1) * head_count, :] = jnp.transpose(queries[r][i])
+        for i in range(own_rows):
+            main_ref[i * head_count : (i + 1) * head_count, :] = jnp.transpose(query[i])
         side = side_ref[...]
         columns = jnp.transpose(side)
         column_ref[...] = columns[:index_heads, :]
         pos_ref[...] = jnp.broadcast_to(side[:, index_heads : index_heads + 1], pos_ref.shape)
     else:
-        main_ref, flat_ref, column_ref, pos_ref = refs[:4]
-        codes, blocks = refs[4 : 4 + parts], refs[4 + parts : 4 + 2 * parts]
-        exp_ref, index_ref, sums_ref = refs[4 + 2 * parts :]
+        early_ref, main_ref, flat_ref, column_ref, pos_ref = refs[:5]
+        codes, blocks = refs[5 : 5 + parts], refs[5 + parts : 5 + 2 * parts]
+        exp_ref, index_ref, sums_ref = refs[5 + 2 * parts :]
     rows = pos_ref.shape[0]
     own_rows = rows // row_parts
     index_heads = column_ref.shape[0]
     index_width = flat_ref.shape[1]
-    head_count = main_ref.shape[0] // rows
+    early_rows = early_ref.shape[0]
+    head_count = (early_rows + main_ref.shape[0]) // rows
     own_keys = blocks[0].shape[1]
     index_scale = float(index_heads * index_width) ** (-0.5)
     me = lax.axis_index("ctx")
@@ -138,7 +147,9 @@
     latent = jnp.concatenate([latent_of(c, b, groups) for c, b in zip(codes, blocks)], axis=1)
     ikeys = jnp.concatenate([b[:own_keys, :] for b in blocks], axis=0)
     dots = contract(flat_ref[...], ikeys, (1, 1))
-    scores = contract(main_ref[...], latent, (1, 0))
+    scores = jnp.concatenate(
+        [contract(early_ref[...], latent, (1, 0)), contract(main_ref[...], latent, (1, 0))], axis=0
+    )
     sums_ref[...] = jnp.zeros_like(sums_ref)
     for t in range(rows):
         r, i = divmod(t, own_rows)
@@ -208,8 +219,8 @@
     sums, refs = refs[:row_parts], refs[row_parts - 2 :]
     flat_ref, masked_ref = refs[2:4]
     exps, indexes = refs[4 : 4 + count], refs[4 + count : 4 + 2 * count]
-    key_ref, dots_ref, gradient_ref, total_ref = refs[4 + 2 * count :]
-    own_keys = key_ref.shape[1]
+    *key_refs, dots_ref, gradient_ref, total_ref = refs[4 + 2 * count :]
+    own_keys = key_refs[0].shape[0]
     gradients = gradient_of(
         key_total, row_parts, places, sums, total_ref, exps, indexes, own_keys
     )
@@ -219,8 +230,8 @@
         gradient_ref[t : t + 1, :] = gradient
         dots_ref[lines, :] = (gradient * masked_ref[lines, :]).astype(bf16)
     key_grad = contract(dots_ref[...], flat_ref[...], (0, 0))
-    for k in range(len(places)):
-        key_ref[k] = key_grad[k * own_keys : (k + 1) * own_keys, :].astype(key_ref.dtype)
+    for k, key_ref in enumerate(key_refs):
+        key_ref[...] = key_grad[k * own_keys : (k + 1) * own_keys, :].astype(key_ref.dtype)
 
 
 def grad_kernel(key_total, row_parts, places, *refs):
@@ -232,10 +243,10 @@
     blocks, refs = refs[: len(places)], refs[len(places) :]
     early_dots, early_gradient, early_heads = refs[:3]
     early_blocks, refs = refs[3 : 3 + len(places)], refs[3 + len(places) :]
-    key_ref, keep_ref, send_ref, dots_ref, total_ref = refs
+    *key_refs, keep_ref, send_ref, dots_ref, total_ref = refs
     own_rows = total_ref.shape[0] // row_parts
     index_heads, index_width = column_ref.shape[0], flat_ref.shape[1]
-    own_keys = key_ref.shape[1]
+    own_keys = key_refs[0].shape[0]
     index_scale = float(index_heads * index_width) ** (-0.5)
     ikeys = jnp.concatenate([b[:own_keys, :] for b in blocks], axis=0)
     flat = flat_ref[...]
@@ -257,8 +268,8 @@
         dots_ref[lines, :] = grad_dots
     grad_dots = dots_ref[...]
     key_grad = contract(grad_dots, flat, (0, 0))
-    for k in range(len(blocks)):
-        key_ref[k] = key_grad[k * own_keys : (k + 1) * own_keys, :].astype(key_ref.dtype)
+    for k, key_ref in enumerate(key_refs):
+        key_ref[...] = key_grad[k * own_keys : (k + 1) * own_keys, :].astype(key_ref.dtype)
     early_keys = jnp.concatenate([b[:own_keys, :] for b in early_blocks], axis=0)
     grad_query = contract(grad_dots, ikeys, (1, 0)) + contract(early_dots[...], early_keys, (1, 0))
     weights = jnp.transpose(jnp.concatenate([columns, jnp.zeros_like(columns)], axis=0)[:LANES])
@@ -269,10 +280,11 @@
         out[at, lines : lines + own_rows, :] = weights[r * own_rows : (r + 1) * own_rows, :]
 
 
-def finish_kernel(key_ref, key_got_ref, row_ref, row_got_ref, query_ref, weight_ref, key_out_ref):
+def finish_kernel(parts, *refs):
+    key_refs, (row_ref, row_got_ref, query_ref, weight_ref, key_out_ref) = refs[:parts], refs[parts:]
     lines = query_ref.shape[0]
     own_rows, index_heads = weight_ref.shape
-    key_out_ref[...] = key_ref[...] + key_got_ref[...].astype(f32)
+    key_out_ref[...] = sum(ref[...].astype(f32) for ref in key_refs)
     query_ref[...] = row_ref[:lines, :] + row_got_ref[:lines, :]
     tail = slice(lines, lines + own_rows)
     weight_ref[...] = (row_ref[tail, :] + row_got_ref[tail, :])[:, :index_heads]
@@ -333,6 +345,9 @@
         pieces = [list(range(key_parts - 1)), [key_parts - 1]]
     else:
         pieces = [list(range(k, k + step)) for k in range(0, key_parts, step)]
+    (main_early,) = kernel_call(
+        lay_kernel, (struct(((rows - own_rows) * head_count, latent_width), bf16),), queries[:-1]
+    )
     exps, indexes, sums, laid = [], [], None, None
     for n, piece in enumerate(pieces):
         wide = len(piece) * own_keys
@@ -343,7 +358,7 @@
         )
         if n == 0:
             shapes += (
-                struct((rows * head_count, latent_width), bf16),
+                struct((own_rows * head_count, latent_width), bf16),
                 struct((rows * index_heads, index_width), bf16),
                 struct((index_heads, rows), f32),
                 struct((rows, LANES), f32),
@@ -352,14 +367,14 @@
             functools.partial(score_kernel, tuple(piece), row_parts, groups, n == 0),
             shapes,
             (
-                *(laid or (*queries, *iqueries)),
+                *(laid or (main_early, queries[-1], *iqueries)),
                 *(codes[k] for k in piece),
                 *(blocks[k] for k in piece),
             ),
             scratch=(pltpu.VMEM((rows, LANES), f32),) if n == 0 else (),
             flops=2 * rows * head_count * latent_width * wide,
         )
-        laid = laid or out[3:]
+        laid = laid or (main_early, *out[3:])
         exps.append(out[0])
         indexes.append(out[1])
         sums = out[2] if sums is None else sums + out[2]
@@ -371,7 +386,7 @@
 
     place = {k: (n, p * own_keys) for n, piece in enumerate(pieces) for p, k in enumerate(piece)}
     teams = [list(range(key_parts))] if key_parts <= step else pieces
-    even, odd, keep, send = [], [], None, None
+    found, keep, send = {}, None, None
     for ids in teams:
         half = len(ids) // 2
         more = struct((rows * index_heads, half * own_keys), bf16)
@@ -380,7 +395,7 @@
         heads, masked = kernel_call(
             prepare_kernel,
             (wide, wide),
-            (*laid[1:3], *(blocks[k] for k in ids[1::2])),
+            (*laid[2:4], *(blocks[k] for k in ids[1::2])),
             flops=grads_flops,
         )
         early = None
@@ -389,15 +404,15 @@
             used = sorted({place[k][0] for k in mine})
             places = tuple((used.index(place[k][0]), place[k][1]) for k in mine)
             stored = (*(exps[n] for n in used), *(indexes[n] for n in used))
-            shapes = (struct((half, own_keys, index_width), bf16 if part else f32),)
+            shapes = (struct((own_keys, index_width), bf16 if part else f32),) * half
             scratch = (pltpu.VMEM((rows, head_count), f32),)
             if part:
                 kernel = first_grad_kernel
-                operands = (*sums, laid[1], masked, *stored)
+                operands = (*sums, laid[2], masked, *stored)
                 shapes += (more, struct((rows, half * own_keys), f32))
             else:
                 kernel = grad_kernel
-                operands = (*sums, *laid[1:3], *stored, *(blocks[k] for k in mine))
+                operands = (*sums, *laid[2:4], *stored, *(blocks[k] for k in mine))
                 operands += (*early, heads, *(blocks[k] for k in ids[1::2]))
                 shapes += (struct((row_parts // 2, tall, index_width), f32),) * 2
                 scratch = (pltpu.VMEM(more.shape, bf16), *scratch)
@@ -408,34 +423,40 @@
                 scratch=scratch,
                 flops=grads_flops,
             )
+            found.update(zip(mine, out))
             if part:
-                odd.append(out[0])
-                early = out[1:]
+                early = out[half:]
             else:
-                even.append(out[0])
-                keep = out[1] if keep is None else keep + out[1]
-                send = out[2] if send is None else send + out[2]
-    key_sum = even[0] if len(even) == 1 else jnp.concatenate(even)
-    key_send = odd[0] if len(odd) == 1 else jnp.concatenate(odd)
-
-    key_got = swap(key_send, row_parts, count)
+                keep = out[-2] if keep is None else keep + out[-2]
+                send = out[-1] if send is None else send + out[-1]
+
+    def pick(n):
+        return found[n] if len(teams) == 1 else jnp.stack([found[k] for k in range(n, key_parts, 4)])
+
+    key_got = swap(pick(3), row_parts, count)
+    near_got = swap(pick(1), row_parts, count)
     row_got = swap(send, row_parts // 2, count)
-    bit = 2
+    key_sum = (pick(2) + key_got.astype(f32)).astype(bf16)
+    key_got = swap(key_sum, 2 * row_parts, count)
+    key_sums = (pick(0), near_got, key_got)
+    bit = 4
     while bit < key_parts:
-        key_sum = key_sum + key_got.astype(f32)
+        key_sum = sum(x.astype(f32) for x in key_sums)
         key_got = swap(key_sum[1::2].astype(bf16), row_parts * bit, count)
-        key_sum = key_sum[0::2]
+        key_sums = (key_sum[0::2], key_got)
         bit *= 2
+    if len(teams) > 1:
+        key_sums = tuple(x[0] for x in key_sums)
     row_sum = keep + row_got
     row_got = swap(row_sum[1], 1, count)
     grad_query, grad_weight, key_grad = kernel_call(
-        finish_kernel,
+        functools.partial(finish_kernel, len(key_sums)),
         (
             struct((lines, index_width), f32),
             struct((own_rows, index_heads), f32),
             struct((own_keys, index_width), f32),
         ),
-        (key_sum[0], key_got[0], row_sum[0], row_got),
+        (*key_sums, row_sum[0], row_got),
     )
     return grad_query.reshape(own_rows, index_heads, index_width), grad_weight, key_grad
 

time: 51.9 us -> 55.9 us (1.077)
  starting transfers between devices: 15.6 us -> 23.1 us
  waiting for transfers between devices: 29.3 us -> 25.8 us
    ppermute x19 -> x20, starting transfers between devices: 15.6 us -> 23.1 us  [swap(): return lax.ppermute(array, 'ctx', [(i, i ^ mask) for i in range(count)])]
    ppermute x19 -> x20, waiting for transfers between devices: 29.3 us -> 25.8 us  [swap(): return lax.ppermute(array, 'ctx', [(i, i ^ mask) for i in range(count)])]
    pallas_call x6 -> x7, Pallas kernels: 4.9 us -> 4.91 us  [kernel_call(): pl.pallas_call(kernel, out_shape=tuple(shapes), scratch_shapes=list(scrat...]
  transfers between devices with their start and end apart: 19 -> 20, of which waited for: 12 -> 10; matrix products, arithmetic and copies ran while one was open for 0% -> 0% of each run, Pallas kernels for 8% -> 5%
where the time goes in v5:
time: 55.9 us; the launch traced here: 55.7 us
  waiting for transfers between devices  25.8 us (46%)
  starting transfers between devices  23.1 us (41%)
  Pallas kernels  6.04 us (11%)
  between operations  0.73 us (1%)
    ppermute x20, waiting for transfers between devices, swap(): return lax.ppermute(array, 'ctx', [(i, i ^ mask) for i in range(count)])  25.8 us
    ppermute x20, starting transfers between devices, swap(): return lax.ppermute(array, 'ctx', [(i, i ^ mask) for i in range(count)])  23.1 us
    pallas_call x7, Pallas kernels, kernel_call(): pl.pallas_call(kernel, out_shape=tuple(shapes), scratch_shapes=list(scrat...  4.91 us
    pallas_call x1, Pallas kernels, body(): pl.pallas_call(pack_kernel, out_shape=(struct((own_keys + 16, own_keys),...  1.13 us
  transfers between devices with their start and end apart: 20, of which 10 were waited for; matrix products, arithmetic and copies ran while one was open for 0% of the time, Pallas kernels for 5%

profile of v5, /device:TPU:0, one launch (start us, length us, event | category | flops | bytes accessed | tf_op | source)
XLA Modules:
  0.0 55.7 jit_solution(4922806811468319618)
XLA Ops:
  0.6 3.0 %collective-permute-start.1 = (bf16[2,576,128]{2,1,0:T(8,128)(2,1)}, bf16[2,576,128]{2,1,0:T(8,128)(2,1)S(1)}, u32[]{:S(2)}, u32[]{:S(2)}) collective-permute-start(bf16[2,576,128]{2,1,0:T(8,128)(2,1)} %bitcast.9), channel_id=1, source_target_pairs={{0,2},{1,3},{2,0},{3,1},{4,6},{5,7},{6,4},{7,5},{8,10},{9,11},{10,... | collective-permute-start | bytes 884744 | tf_op jit(solution)/shard_map/ppermute | solution.py:34
  3.7 0.0 collective-permute-start
  3.7 7.2 %collective-permute-done.1.refs_2_ = bf16[2,576,128]{2,1,0:T(8,128)(2,1)S(1)} collective-permute-done((bf16[2,576,128]{2,1,0:T(8,128)(2,1)}, bf16[2,576,128]{2,1,0:T(8,128)(2,1)S(1)}, u32[]{:S(2)}, u32[]{:S(2)}) %collective-permute-start.1) | collective-permute-done | bytes 294944 | tf_op jit(solution)/shard_map/ppermute | solution.py:34
  10.9 0.0 collective-permute-start.2
  10.9 2.8 %collective-permute-start.7 = (bf16[576,128]{1,0:T(8,128)(2,1)}, bf16[576,128]{1,0:T(8,128)(2,1)S(1)}, u32[]{:S(2)}, u32[]{:S(2)}) collective-permute-start(bf16[576,128]{1,0:T(8,128)(2,1)} %bitcast.12), channel_id=1, source_target_pairs={{0,8},{1,9},{2,10},{3,11},{4,12},{5,13},{6,14},{7,15},{8,0},{9,1},... | collective-permute-start | bytes 442376 | tf_op jit(solution)/shard_map/ppermute | solution.py:34
  13.7 1.1 %pack.1 = (bf16[144,128]{1,0:T(8,128)(2,1)S(1)}, bf16[144,128]{1,0:T(8,128)(2,1)S(1)}, bf16[2,576,128]{2,1,0:T(8,128)(2,1)S(1)}, bf16[576,128]{1,0:T(8,128)(2,1)S(1)}) custom-call(s32[4,128]{1,0:T(4,128)} %bitcast.16, bf16[128,128]{1,0:T(8,128)(2,1)} %keys_hbm.1, f32[2,64]{1,0:T(2,128)} %weight_hbm.1, s32[2]{0:T(128)} %pos_hbm.1, ...), custom_call_target="tpu_custom_call" | custom-call | tf_op jit(solution)/shard_map/pack/pallas_call | solution.py:318
  14.9 0.3 collective-permute-start.3
  15.2 1.6 %collective-permute-start.6 = (bf16[576,128]{1,0:T(8,128)(2,1)}, bf16[576,128]{1,0:T(8,128)(2,1)S(1)}, u32[]{:S(2)}, u32[]{:S(2)}) collective-permute-start(bf16[576,128]{1,0:T(8,128)(2,1)} %bitcast.14), channel_id=1, source_target_pairs={{0,4},{1,5},{2,6},{3,7},{4,0},{5,1},{6,2},{7,3},{8,12},{9,13},{10,... | collective-permute-start | bytes 442376 | tf_op jit(solution)/shard_map/ppermute | solution.py:34
  16.7 0.0 collective-permute-done.3.refs_3_
  16.7 1.5 %collective-permute-start.4 = (bf16[144,128]{1,0:T(8,128)(2,1)S(1)}, bf16[144,128]{1,0:T(8,128)(2,1)S(1)}, u32[]{:S(2)}, u32[]{:S(2)}) collective-permute-start(bf16[144,128]{1,0:T(8,128)(2,1)S(1)} %get-tuple-element.31.refs_2_), channel_id=1, source_target_pairs={{0,2},{1,3},{2,0},{3,1},{4,6},{5,7},{6,4},{7,5},{8,10},{9,11},{10,... | collective-permute-start | bytes 110600 | tf_op jit(solution)/shard_map/ppermute | solution.py:34
  18.2 3.5 %collective-permute-done.7.refs_8_ = bf16[576,128]{1,0:T(8,128)(2,1)S(1)} collective-permute-done((bf16[576,128]{1,0:T(8,128)(2,1)}, bf16[576,128]{1,0:T(8,128)(2,1)S(1)}, u32[]{:S(2)}, u32[]{:S(2)}) %collective-permute-start.7) | collective-permute-done | bytes 147488 | tf_op jit(solution)/shard_map/ppermute | solution.py:34
  21.7 0.8 %collective-permute-start.10 = (bf16[576,128]{1,0:T(8,128)(2,1)S(1)}, bf16[576,128]{1,0:T(8,128)(2,1)S(1)}, u32[]{:S(2)}, u32[]{:S(2)}) collective-permute-start(bf16[576,128]{1,0:T(8,128)(2,1)S(1)} %collective-permute-done.7.refs_8_), channel_id=1, source_target_pairs={{0,4},{1,5},{2,6},{3,7},{4,0},{5,1},{6,2},{7,3},{8,12},{9,13},{10,... | collective-permute-start | bytes 442376 | tf_op jit(solution)/shard_map/ppermute | solution.py:34
  22.5 0.0 collective-permute-done.4.refs_4_
  22.5 1.3 %collective-permute-start.8 = (bf16[144,128]{1,0:T(8,128)(2,1)S(1)}, bf16[144,128]{1,0:T(8,128)(2,1)S(1)}, u32[]{:S(2)}, u32[]{:S(2)}) collective-permute-start(bf16[144,128]{1,0:T(8,128)(2,1)S(1)} %get-tuple-element.33.refs_9_.refs_8_), channel_id=1, source_target_pairs={{0,4},{1,5},{2,6},{3,7},{4,0},{5,1},{6,2},{7,3},{8,12},{9,13},{10,... | collective-permute-start | bytes 110600 | tf_op jit(solution)/shard_map/ppermute | solution.py:34
  23.7 4.3 %collective-permute-done.8.refs_10_.refs_0_.refs_13_ = bf16[144,128]{1,0:T(8,128)(2,1)S(1)} collective-permute-done((bf16[144,128]{1,0:T(8,128)(2,1)S(1)}, bf16[144,128]{1,0:T(8,128)(2,1)S(1)}, u32[]{:S(2)}, u32[]{:S(2)}) %collective-permute-start.8) | collective-permute-done | bytes 36896 | tf_op jit(solution)/shard_map/ppermute | solution.py:34
  28.1 2.6 %collective-permute-start.9 = (bf16[144,128]{1,0:T(8,128)(2,1)S(1)}, bf16[144,128]{1,0:T(8,128)(2,1)S(1)}, u32[]{:S(2)}, u32[]{:S(2)}) collective-permute-start(bf16[144,128]{1,0:T(8,128)(2,1)S(1)} %get-tuple-element.33.refs_9_.refs_8_), channel_id=1, source_target_pairs={{0,8},{1,9},{2,10},{3,11},{4,12},{5,13},{6,14},{7,15},{8,0},{9,1},... | collective-permute-start | bytes 110600 | tf_op jit(solution)/shard_map/ppermute | solution.py:34
  30.6 0.0 collective-permute-done.refs_1_
  30.6 0.0 collective-permute-start.5
  30.6 0.3 shard_map.94.refs_0_
  31.0 1.9 %collective-permute-done.9.refs_11_.refs_9_ = bf16[144,128]{1,0:T(8,128)(2,1)S(1)} collective-permute-done((bf16[144,128]{1,0:T(8,128)(2,1)S(1)}, bf16[144,128]{1,0:T(8,128)(2,1)S(1)}, u32[]{:S(2)}, u32[]{:S(2)}) %collective-permute-start.9) | collective-permute-done | bytes 36896 | tf_op jit(solution)/shard_map/ppermute | solution.py:34
  32.9 1.4 %collective-permute-start.11 = (bf16[144,128]{1,0:T(8,128)(2,1)S(1)}, bf16[144,128]{1,0:T(8,128)(2,1)S(1)}, u32[]{:S(2)}, u32[]{:S(2)}) collective-permute-start(bf16[144,128]{1,0:T(8,128)(2,1)S(1)} %collective-permute-done.9.refs_11_.refs_9_), channel_id=1, source_target_pairs={{0,4},{1,5},{2,6},{3,7},{4,0},{5,1},{6,2},{7,3},{8,12},{9,13},{10,... | collective-permute-start | bytes 110600 | tf_op jit(solution)/shard_map/ppermute | solution.py:34
  34.3 0.0 collective-permute-done.5.refs_5_
  34.3 0.0 collective-permute-done.6.refs_7_
  34.3 0.0 collective-permute-done.2.refs_1_
  34.3 1.3 %shard_map.95 = (f32[8,128,384]{2,1,0:T(8,128)S(1)}, f32[8,384]{1,0:T(8,128)S(1)}, f32[4,4,128]{2,1,0:T(4,128)S(1)}, bf16[256,576]{1,0:T(8,128)(2,1)S(1)}, bf16[...) custom-call(bf16[768,576]{1,0:T(8,128)(2,1)S(1)} %shard_map.94.refs_0_, ...), custom_call_target="tpu_custom_call" | custom-call | flops 452984832 | bytes 3905536 | tf_op jit(solution)/shard_map/pallas_call | solution.py:20
  35.6 1.3 %collective-permute-done.11.refs_6_.refs_1_.refs_14_ = bf16[144,128]{1,0:T(8,128)(2,1)S(1)} collective-permute-done((bf16[144,128]{1,0:T(8,128)(2,1)S(1)}, bf16[144,128]{1,0:T(8,128)(2,1)S(1)}, u32[]{:S(2)}, u32[]{:S(2)}) %collective-permute-start.11) | collective-permute-done | bytes 36896 | tf_op jit(solution)/shard_map/ppermute | solution.py:34
  36.9 0.0 collective-permute-done.10.refs_5_
  36.9 0.7 %shard_map.96 = (f32[8,128,128]{2,1,0:T(8,128)S(1)}, f32[8,128]{1,0:T(8,128)S(1)}, f32[4,4,128]{2,1,0:T(4,128)S(1)}) custom-call(bf16[768,576]{1,0:T(8,128)(2,1)S(1)} %shard_map.94.refs_0_, bf16[256,576]{1,0:T(8,128)(2,1)S(1)} %get-tuple-element.35.refs_1_, bf16[512,128]{1,0:T(8,128)(2,1)S(1)} %get-tuple-element.36.refs_2_.flat_ref.refs_4_, ...), custom_call_target="tpu_custom_call" | custom-call | flops 150994944 | bytes 2037760 | tf_op jit(solution)/shard_map/pallas_call | solution.py:20
  37.6 0.1 collective-permute-start.12
  37.7 1.4 %collective-permute-start.13 = (f32[4,4,128]{2,1,0:T(4,128)S(1)}, f32[4,4,128]{2,1,0:T(4,128)S(1)}, u32[]{:S(2)}, u32[]{:S(2)}) collective-permute-start(f32[4,4,128]{2,1,0:T(4,128)S(1)} %add.9.refs_0_), channel_id=1, source_target_pairs={{0,2},{1,3},{2,0},{3,1},{4,6},{5,7},{6,4},{7,5},{8,10},{9,11},{10,... | collective-permute-start | bytes 24584 | tf_op jit(solution)/shard_map/ppermute | solution.py:34
  39.1 0.4 collective-permute-start.14
  39.5 0.2 shard_map.97
  39.8 0.0 collective-permute-done.12.refs_1_
  39.8 1.6 %collective-permute-done.13.refs_2_ = f32[4,4,128]{2,1,0:T(4,128)S(1)} collective-permute-done((f32[4,4,128]{2,1,0:T(4,128)S(1)}, f32[4,4,128]{2,1,0:T(4,128)S(1)}, u32[]{:S(2)}, u32[]{:S(2)}) %collective-permute-start.13) | collective-permute-done | bytes 8224 | tf_op jit(solution)/shard_map/ppermute | solution.py:34
  41.4 0.8 %collective-permute-done.14.refs_3_ = f32[4,4,128]{2,1,0:T(4,128)S(1)} collective-permute-done((f32[4,4,128]{2,1,0:T(4,128)S(1)}, f32[4,4,128]{2,1,0:T(4,128)S(1)}, u32[]{:S(2)}, u32[]{:S(2)}) %collective-permute-start.14) | collective-permute-done | bytes 8224 | tf_op jit(solution)/shard_map/ppermute | solution.py:34
  42.2 0.7 %shard_map.98 = (bf16[128,128]{1,0:T(8,128)(2,1)S(1)}, bf16[128,128]{1,0:T(8,128)(2,1)S(1)}, bf16[512,256]{1,0:T(8,128)(2,1)S(1)}, f32[8,256]{1,0:T(8,128)S(1)}) custom-call(f32[4,4,128]{2,1,0:T(4,128)S(1)} %add.9.refs_0_, f32[4,4,128]{2,1,0:T(4,128)S(1)} %collective-permute-done.12.refs_1_, f32[4,4,128]{2,1,0:T(4,128)S(1)} %collective-permute-done.13.refs_2_, ...), custom_call_target="tpu_custom_call" | custom-call | flops 67108864 | bytes 3137536 | tf_op jit(solution)/shard_map/pallas_call | solution.py:20
  42.9 1.0 %shard_map.99 = (f32[128,128]{1,0:T(8,128)S(1)}, f32[128,128]{1,0:T(8,128)S(1)}, f32[2,136,128]{2,1,0:T(8,128)S(1)}, f32[2,136,128]{2,1,0:T(8,128)S(1)}) custom-call(f32[4,4,128]{2,1,0:T(4,128)S(1)} %add.9.refs_0_, f32[4,4,128]{2,1,0:T(4,128)S(1)} %collective-permute-done.12.refs_1_, f32[4,4,128]{2,1,0:T(4,128)S(1)} %collective-permute-done.13.refs_2_, ...), custom_call_target="tpu_custom_call" | custom-call | flops 67108864 | bytes 3102720 | tf_op jit(solution)/shard_map/pallas_call | solution.py:20
  43.9 0.8 %collective-permute-start.18 = (f32[2,136,128]{2,1,0:T(8,128)S(1)}, f32[2,136,128]{2,1,0:T(8,128)S(1)}, u32[]{:S(2)}, u32[]{:S(2)}) collective-permute-start(f32[2,136,128]{2,1,0:T(8,128)S(1)} %get-tuple-element.53), channel_id=1, source_target_pairs={{0,2},{1,3},{2,0},{3,1},{4,6},{5,7},{6,4},{7,5},{8,10},{9,11},{10,... | collective-permute-start | bytes 417800 | tf_op jit(solution)/shard_map/ppermute | solution.py:34
  44.6 1.5 %collective-permute-start.15 = (bf16[128,128]{1,0:T(8,128)(2,1)S(1)}, bf16[128,128]{1,0:T(8,128)(2,1)S(1)}, u32[]{:S(2)}, u32[]{:S(2)}) collective-permute-start(bf16[128,128]{1,0:T(8,128)(2,1)S(1)} %get-tuple-element.49), channel_id=1, source_target_pairs={{0,4},{1,5},{2,6},{3,7},{4,0},{5,1},{6,2},{7,3},{8,12},{9,13},{10,... | collective-permute-start | bytes 98312 | tf_op jit(solution)/shard_map/ppermute | solution.py:34
  46.1 0.5 collective-permute-start.16
  46.7 3.0 %collective-permute-done.18 = f32[2,136,128]{2,1,0:T(8,128)S(1)} collective-permute-done((f32[2,136,128]{2,1,0:T(8,128)S(1)}, f32[2,136,128]{2,1,0:T(8,128)S(1)}, u32[]{:S(2)}, u32[]{:S(2)}) %collective-permute-start.18) | collective-permute-done | bytes 139296 | tf_op jit(solution)/shard_map/ppermute | solution.py:34
  49.7 0.1 collective-permute-start.19
  49.8 0.2 collective-permute-done.16
  50.0 3.1 %collective-permute-start.17 = (bf16[128,128]{1,0:T(8,128)(2,1)S(1)}, bf16[128,128]{1,0:T(8,128)(2,1)S(1)}, u32[]{:S(2)}, u32[]{:S(2)}) collective-permute-start(bf16[128,128]{1,0:T(8,128)(2,1)S(1)} %add_convert_fusion), channel_id=1, source_target_pairs={{0,8},{1,9},{2,10},{3,11},{4,12},{5,13},{6,14},{7,15},{8,0},{9,1},... | collective-permute-start | bytes 98312 | tf_op jit(solution)/shard_map/ppermute | solution.py:34
  53.2 0.0 collective-permute-done.15.refs_1_
  53.2 1.9 %collective-permute-done.17.refs_2_ = bf16[128,128]{1,0:T(8,128)(2,1)S(1)} collective-permute-done((bf16[128,128]{1,0:T(8,128)(2,1)S(1)}, bf16[128,128]{1,0:T(8,128)(2,1)S(1)}, u32[]{:S(2)}, u32[]{:S(2)}) %collective-permute-start.17) | collective-permute-done | bytes 32800 | tf_op jit(solution)/shard_map/ppermute | solution.py:34
  55.0 0.0 collective-permute-done.19.refs_4_
  55.0 0.7 %shard_map.100 = (f32[128,128]{1,0:T(8,128)}, f32[2,64]{1,0:T(2,128)}, f32[128,128]{1,0:T(8,128)}) custom-call(f32[128,128]{1,0:T(8,128)S(1)} %get-tuple-element.48.refs_0_, bf16[128,128]{1,0:T(8,128)(2,1)S(1)} %collective-permute-done.15.refs_1_, bf16[128,128]{1,0:T(8,128)(2,1)S(1)} %collective-permute-done.17.refs_2_, ...), custom_call_target="tpu_custom_call" | custom-call | bytes 401920 | tf_op jit(solution)/shard_map/pallas_call | solution.py:20
  (4 shorter events, 0.0 us)
Async XLA Ops:
  0.6 10.2 %collective-permute-start.1 = (bf16[2,576,128]{2,1,0:T(8,128)(2,1)}, bf16[2,576,128]{2,1,0:T(8,128)(2,1)S(1)}, u32[]{:S(2)}, u32[]{:S(2)}) collective-permute-start(bf16[2,576,128]{2,1,0:T(8,128)(2,1)} %bitcast.9), channel_id=1, source_target_pairs={{0,2},{1,3},{2,0},{3,1},{4,6},{5,7},{6,4},{7,5},{8,10},{9,11},{10,... | collective-permute-start | bytes 884744 | tf_op jit(solution)/shard_map/ppermute | solution.py:34
  3.7 27.0 %collective-permute-start = (bf16[2,576,128]{2,1,0:T(8,128)(2,1)}, bf16[2,576,128]{2,1,0:T(8,128)(2,1)S(1)}, u32[]{:S(2)}, u32[]{:S(2)}) collective-permute-start(bf16[2,576,128]{2,1,0:T(8,128)(2,1)} %bitcast.10), channel_id=1, source_target_pairs={{0,1},{1,0},{2,3},{3,2},{4,5},{5,4},{6,7},{7,6},{8,9},{9,8},{10,11... | collective-permute-start | bytes 884744 | tf_op jit(solution)/shard_map/ppermute | solution.py:34
  10.9 23.4 %collective-permute-start.2 = (bf16[2,576,128]{2,1,0:T(8,128)(2,1)S(1)}, bf16[2,576,128]{2,1,0:T(8,128)(2,1)S(1)}, u32[]{:S(2)}, u32[]{:S(2)}) collective-permute-start(bf16[2,576,128]{2,1,0:T(8,128)(2,1)S(1)} %collective-permute-done.1.refs_2_), channel_id=1, source_target_pairs={{0,1},{1,0},{2,3},{3,2},{4,5},{5,4},{6,7},{7,6},{8,9},{9,8},{10,11... | collective-permute-start | bytes 884744 | tf_op jit(solution)/shard_map/ppermute | solution.py:34
  10.9 10.8 %collective-permute-start.7 = (bf16[576,128]{1,0:T(8,128)(2,1)}, bf16[576,128]{1,0:T(8,128)(2,1)S(1)}, u32[]{:S(2)}, u32[]{:S(2)}) collective-permute-start(bf16[576,128]{1,0:T(8,128)(2,1)} %bitcast.12), channel_id=1, source_target_pairs={{0,8},{1,9},{2,10},{3,11},{4,12},{5,13},{6,14},{7,15},{8,0},{9,1},... | collective-permute-start | bytes 442376 | tf_op jit(solution)/shard_map/ppermute | solution.py:34
  14.9 1.9 %collective-permute-start.3 = (bf16[144,128]{1,0:T(8,128)(2,1)S(1)}, bf16[144,128]{1,0:T(8,128)(2,1)S(1)}, u32[]{:S(2)}, u32[]{:S(2)}) collective-permute-start(bf16[144,128]{1,0:T(8,128)(2,1)S(1)} %get-tuple-element.31.refs_2_), channel_id=1, source_target_pairs={{0,1},{1,0},{2,3},{3,2},{4,5},{5,4},{6,7},{7,6},{8,9},{9,8},{10,11... | collective-permute-start | bytes 110600 | tf_op jit(solution)/shard_map/ppermute | solution.py:34
  15.2 19.2 %collective-permute-start.6 = (bf16[576,128]{1,0:T(8,128)(2,1)}, bf16[576,128]{1,0:T(8,128)(2,1)S(1)}, u32[]{:S(2)}, u32[]{:S(2)}) collective-permute-start(bf16[576,128]{1,0:T(8,128)(2,1)} %bitcast.14), channel_id=1, source_target_pairs={{0,4},{1,5},{2,6},{3,7},{4,0},{5,1},{6,2},{7,3},{8,12},{9,13},{10,... | collective-permute-start | bytes 442376 | tf_op jit(solution)/shard_map/ppermute | solution.py:34
  16.7 5.8 %collective-permute-start.4 = (bf16[144,128]{1,0:T(8,128)(2,1)S(1)}, bf16[144,128]{1,0:T(8,128)(2,1)S(1)}, u32[]{:S(2)}, u32[]{:S(2)}) collective-permute-start(bf16[144,128]{1,0:T(8,128)(2,1)S(1)} %get-tuple-element.31.refs_2_), channel_id=1, source_target_pairs={{0,2},{1,3},{2,0},{3,1},{4,6},{5,7},{6,4},{7,5},{8,10},{9,11},{10,... | collective-permute-start | bytes 110600 | tf_op jit(solution)/shard_map/ppermute | solution.py:34
  21.7 15.2 %collective-permute-start.10 = (bf16[576,128]{1,0:T(8,128)(2,1)S(1)}, bf16[576,128]{1,0:T(8,128)(2,1)S(1)}, u32[]{:S(2)}, u32[]{:S(2)}) collective-permute-start(bf16[576,128]{1,0:T(8,128)(2,1)S(1)} %collective-permute-done.7.refs_8_), channel_id=1, source_target_pairs={{0,4},{1,5},{2,6},{3,7},{4,0},{5,1},{6,2},{7,3},{8,12},{9,13},{10,... | collective-permute-start | bytes 442376 | tf_op jit(solution)/shard_map/ppermute | solution.py:34
  22.5 5.6 %collective-permute-start.8 = (bf16[144,128]{1,0:T(8,128)(2,1)S(1)}, bf16[144,128]{1,0:T(8,128)(2,1)S(1)}, u32[]{:S(2)}, u32[]{:S(2)}) collective-permute-start(bf16[144,128]{1,0:T(8,128)(2,1)S(1)} %get-tuple-element.33.refs_9_.refs_8_), channel_id=1, source_target_pairs={{0,4},{1,5},{2,6},{3,7},{4,0},{5,1},{6,2},{7,3},{8,12},{9,13},{10,... | collective-permute-start | bytes 110600 | tf_op jit(solution)/shard_map/ppermute | solution.py:34
  28.1 4.9 %collective-permute-start.9 = (bf16[144,128]{1,0:T(8,128)(2,1)S(1)}, bf16[144,128]{1,0:T(8,128)(2,1)S(1)}, u32[]{:S(2)}, u32[]{:S(2)}) collective-permute-start(bf16[144,128]{1,0:T(8,128)(2,1)S(1)} %get-tuple-element.33.refs_9_.refs_8_), channel_id=1, source_target_pairs={{0,8},{1,9},{2,10},{3,11},{4,12},{5,13},{6,14},{7,15},{8,0},{9,1},... | collective-permute-start | bytes 110600 | tf_op jit(solution)/shard_map/ppermute | solution.py:34
  30.6 3.7 %collective-permute-start.5 = (bf16[144,128]{1,0:T(8,128)(2,1)S(1)}, bf16[144,128]{1,0:T(8,128)(2,1)S(1)}, u32[]{:S(2)}, u32[]{:S(2)}) collective-permute-start(bf16[144,128]{1,0:T(8,128)(2,1)S(1)} %collective-permute-done.4.refs_4_), channel_id=1, source_target_pairs={{0,1},{1,0},{2,3},{3,2},{4,5},{5,4},{6,7},{7,6},{8,9},{9,8},{10,11... | collective-permute-start | bytes 110600 | tf_op jit(solution)/shard_map/ppermute | solution.py:34
  32.9 4.0 %collective-permute-start.11 = (bf16[144,128]{1,0:T(8,128)(2,1)S(1)}, bf16[144,128]{1,0:T(8,128)(2,1)S(1)}, u32[]{:S(2)}, u32[]{:S(2)}) collective-permute-start(bf16[144,128]{1,0:T(8,128)(2,1)S(1)} %collective-permute-done.9.refs_11_.refs_9_), channel_id=1, source_target_pairs={{0,4},{1,5},{2,6},{3,7},{4,0},{5,1},{6,2},{7,3},{8,12},{9,13},{10,... | collective-permute-start | bytes 110600 | tf_op jit(solution)/shard_map/ppermute | solution.py:34
  37.6 2.2 %collective-permute-start.12 = (f32[4,4,128]{2,1,0:T(4,128)S(1)}, f32[4,4,128]{2,1,0:T(4,128)S(1)}, u32[]{:S(2)}, u32[]{:S(2)}) collective-permute-start(f32[4,4,128]{2,1,0:T(4,128)S(1)} %add.9.refs_0_), channel_id=1, source_target_pairs={{0,1},{1,0},{2,3},{3,2},{4,5},{5,4},{6,7},{7,6},{8,9},{9,8},{10,11... | collective-permute-start | bytes 24584 | tf_op jit(solution)/shard_map/ppermute | solution.py:34
  37.7 3.7 %collective-permute-start.13 = (f32[4,4,128]{2,1,0:T(4,128)S(1)}, f32[4,4,128]{2,1,0:T(4,128)S(1)}, u32[]{:S(2)}, u32[]{:S(2)}) collective-permute-start(f32[4,4,128]{2,1,0:T(4,128)S(1)} %add.9.refs_0_), channel_id=1, source_target_pairs={{0,2},{1,3},{2,0},{3,1},{4,6},{5,7},{6,4},{7,5},{8,10},{9,11},{10,... | collective-permute-start | bytes 24584 | tf_op jit(solution)/shard_map/ppermute | solution.py:34
  39.1 3.1 %collective-permute-start.14 = (f32[4,4,128]{2,1,0:T(4,128)S(1)}, f32[4,4,128]{2,1,0:T(4,128)S(1)}, u32[]{:S(2)}, u32[]{:S(2)}) collective-permute-start(f32[4,4,128]{2,1,0:T(4,128)S(1)} %add.9.refs_0_), channel_id=1, source_target_pairs={{0,3},{1,2},{2,1},{3,0},{4,7},{5,6},{6,5},{7,4},{8,11},{9,10},{10,... | collective-permute-start | bytes 24584 | tf_op jit(solution)/shard_map/ppermute | solution.py:34
  43.9 5.8 %collective-permute-start.18 = (f32[2,136,128]{2,1,0:T(8,128)S(1)}, f32[2,136,128]{2,1,0:T(8,128)S(1)}, u32[]{:S(2)}, u32[]{:S(2)}) collective-permute-start(f32[2,136,128]{2,1,0:T(8,128)S(1)} %get-tuple-element.53), channel_id=1, source_target_pairs={{0,2},{1,3},{2,0},{3,1},{4,6},{5,7},{6,4},{7,5},{8,10},{9,11},{10,... | collective-permute-start | bytes 417800 | tf_op jit(solution)/shard_map/ppermute | solution.py:34
  44.6 8.5 %collective-permute-start.15 = (bf16[128,128]{1,0:T(8,128)(2,1)S(1)}, bf16[128,128]{1,0:T(8,128)(2,1)S(1)}, u32[]{:S(2)}, u32[]{:S(2)}) collective-permute-start(bf16[128,128]{1,0:T(8,128)(2,1)S(1)} %get-tuple-element.49), channel_id=1, source_target_pairs={{0,4},{1,5},{2,6},{3,7},{4,0},{5,1},{6,2},{7,3},{8,12},{9,13},{10,... | collective-permute-start | bytes 98312 | tf_op jit(solution)/shard_map/ppermute | solution.py:34
  46.1 3.9 %collective-permute-start.16 = (bf16[128,128]{1,0:T(8,128)(2,1)S(1)}, bf16[128,128]{1,0:T(8,128)(2,1)S(1)}, u32[]{:S(2)}, u32[]{:S(2)}) collective-permute-start(bf16[128,128]{1,0:T(8,128)(2,1)S(1)} %get-tuple-element.51), channel_id=1, source_target_pairs={{0,4},{1,5},{2,6},{3,7},{4,0},{5,1},{6,2},{7,3},{8,12},{9,13},{10,... | collective-permute-start | bytes 98312 | tf_op jit(solution)/shard_map/ppermute | solution.py:34
  49.7 5.3 %collective-permute-start.19 = (f32[136,128]{1,0:T(8,128)S(1)}, f32[136,128]{1,0:T(8,128)S(1)}, u32[]{:S(2)}, u32[]{:S(2)}) collective-permute-start(f32[136,128]{1,0:T(8,128)S(1)} %get-tuple-element.57), channel_id=1, source_target_pairs={{0,1},{1,0},{2,3},{3,2},{4,5},{5,4},{6,7},{7,6},{8,9},{9,8},{10,11... | collective-permute-start | bytes 208904 | tf_op jit(solution)/shard_map/ppermute | solution.py:34
  50.0 5.0 %collective-permute-start.17 = (bf16[128,128]{1,0:T(8,128)(2,1)S(1)}, bf16[128,128]{1,0:T(8,128)(2,1)S(1)}, u32[]{:S(2)}, u32[]{:S(2)}) collective-permute-start(bf16[128,128]{1,0:T(8,128)(2,1)S(1)} %add_convert_fusion), channel_id=1, source_target_pairs={{0,8},{1,9},{2,10},{3,11},{4,12},{5,13},{6,14},{7,15},{8,0},{9,1},... | collective-permute-start | bytes 98312 | tf_op jit(solution)/shard_map/ppermute | solution.py:34

commit v6 on v5

--- a/solution.py
+++ b/solution.py
@@ -97,23 +97,14 @@
     return jnp.concatenate([*latent, codes_ref[groups * group_width :, :]], axis=0)
 
 
-def lay_kernel(*refs):
-    queries, main_ref = refs[:-1], refs[-1]
-    own_rows, _, head_count = queries[0].shape
-    for r, query in enumerate(queries):
-        for i in range(own_rows):
-            t = r * own_rows + i
-            main_ref[t * head_count : (t + 1) * head_count, :] = jnp.transpose(query[i])
-
-
 def score_kernel(offsets, row_parts, groups, first, *refs):
     parts = len(offsets)
     if first:
-        early_ref, query, iqueries = refs[0], refs[1], refs[2 : 2 + row_parts]
-        refs = refs[2 + row_parts :]
+        queries, iqueries = refs[:row_parts], refs[row_parts : 2 * row_parts]
+        refs = refs[2 * row_parts :]
         codes, blocks, refs = refs[:parts], refs[parts : 2 * parts], refs[2 * parts :]
         exp_ref, index_ref, sums_ref, main_ref, flat_ref, column_ref, pos_ref, side_ref = refs
-        own_rows, head_count = query.shape[0], query.shape[2]
+        own_rows, head_count = queries[0].shape[0], queries[0].shape[2]
         lines = flat_ref.shape[0] // row_parts
         index_heads = lines // own_rows
         for r in range(row_parts):
@@ -122,22 +113,22 @@
             side = side + tail[2 * own_rows : 3 * own_rows]
             side_ref[r * own_rows : (r + 1) * own_rows, :] = side
             flat_ref[r * lines : (r + 1) * lines, :] = iqueries[r][:lines, :]
-        for i in range(own_rows):
-            main_ref[i * head_count : (i + 1) * head_count, :] = jnp.transpose(query[i])
+            for i in range(own_rows):
+                t = r * own_rows + i
+                main_ref[t * head_count : (t + 1) * head_count, :] = jnp.transpose(queries[r][i])
         side = side_ref[...]
         columns = jnp.transpose(side)
         column_ref[...] = columns[:index_heads, :]
         pos_ref[...] = jnp.broadcast_to(side[:, index_heads : index_heads + 1], pos_ref.shape)
     else:
-        early_ref, main_ref, flat_ref, column_ref, pos_ref = refs[:5]
-        codes, blocks = refs[5 : 5 + parts], refs[5 + parts : 5 + 2 * parts]
-        exp_ref, index_ref, sums_ref = refs[5 + 2 * parts :]
+        main_ref, flat_ref, column_ref, pos_ref = refs[:4]
+        codes, blocks = refs[4 : 4 + parts], refs[4 + parts : 4 + 2 * parts]
+        exp_ref, index_ref, sums_ref = refs[4 + 2 * parts :]
     rows = pos_ref.shape[0]
     own_rows = rows // row_parts
     index_heads = column_ref.shape[0]
     index_width = flat_ref.shape[1]
-    early_rows = early_ref.shape[0]
-    head_count = (early_rows + main_ref.shape[0]) // rows
+    head_count = main_ref.shape[0] // rows
     own_keys = blocks[0].shape[1]
     index_scale = float(index_heads * index_width) ** (-0.5)
     me = lax.axis_index("ctx")
@@ -147,9 +138,7 @@
     latent = jnp.concatenate([latent_of(c, b, groups) for c, b in zip(codes, blocks)], axis=1)
     ikeys = jnp.concatenate([b[:own_keys, :] for b in blocks], axis=0)
     dots = contract(flat_ref[...], ikeys, (1, 1))
-    scores = jnp.concatenate(
-        [contract(early_ref[...], latent, (1, 0)), contract(main_ref[...], latent, (1, 0))], axis=0
-    )
+    scores = contract(main_ref[...], latent, (1, 0))
     sums_ref[...] = jnp.zeros_like(sums_ref)
     for t in range(rows):
         r, i = divmod(t, own_rows)
@@ -345,9 +334,6 @@
         pieces = [list(range(key_parts - 1)), [key_parts - 1]]
     else:
         pieces = [list(range(k, k + step)) for k in range(0, key_parts, step)]
-    (main_early,) = kernel_call(
-        lay_kernel, (struct(((rows - own_rows) * head_count, latent_width), bf16),), queries[:-1]
-    )
     exps, indexes, sums, laid = [], [], None, None
     for n, piece in enumerate(pieces):
         wide = len(piece) * own_keys
@@ -358,7 +344,7 @@
         )
         if n == 0:
             shapes += (
-                struct((own_rows * head_count, latent_width), bf16),
+                struct((rows * head_count, latent_width), bf16),
                 struct((rows * index_heads, index_width), bf16),
                 struct((index_heads, rows), f32),
                 struct((rows, LANES), f32),
@@ -367,14 +353,14 @@
             functools.partial(score_kernel, tuple(piece), row_parts, groups, n == 0),
             shapes,
             (
-                *(laid or (main_early, queries[-1], *iqueries)),
+                *(laid or (*queries, *iqueries)),
                 *(codes[k] for k in piece),
                 *(blocks[k] for k in piece),
             ),
             scratch=(pltpu.VMEM((rows, LANES), f32),) if n == 0 else (),
             flops=2 * rows * head_count * latent_width * wide,
         )
-        laid = laid or (main_early, *out[3:])
+        laid = laid or out[3:]
         exps.append(out[0])
         indexes.append(out[1])
         sums = out[2] if sums is None else sums + out[2]
@@ -395,7 +381,7 @@
         heads, masked = kernel_call(
             prepare_kernel,
             (wide, wide),
-            (*laid[2:4], *(blocks[k] for k in ids[1::2])),
+            (*laid[1:3], *(blocks[k] for k in ids[1::2])),
             flops=grads_flops,
         )
         early = None
@@ -408,11 +394,11 @@
             scratch = (pltpu.VMEM((rows, head_count), f32),)
             if part:
                 kernel = first_grad_kernel
-                operands = (*sums, laid[2], masked, *stored)
+                operands = (*sums, laid[1], masked, *stored)
                 shapes += (more, struct((rows, half * own_keys), f32))
             else:
                 kernel = grad_kernel
-                operands = (*sums, *laid[2:4], *stored, *(blocks[k] for k in mine))
+                operands = (*sums, *laid[1:3], *stored, *(blocks[k] for k in mine))
                 operands += (*early, heads, *(blocks[k] for k in ids[1::2]))
                 shapes += (struct((row_parts // 2, tall, index_width), f32),) * 2
                 scratch = (pltpu.VMEM(more.shape, bf16), *scratch)

time: 55.9 us -> 54.8 us (0.980)
  starting transfers between devices: 23.1 us -> 18.1 us
  waiting for transfers between devices: 25.8 us -> 29.7 us
    ppermute x20, starting transfers between devices: 23.1 us -> 18.1 us  [swap(): return lax.ppermute(array, 'ctx', [(i, i ^ mask) for i in range(count)])]
    ppermute x20, waiting for transfers between devices: 25.8 us -> 29.7 us  [swap(): return lax.ppermute(array, 'ctx', [(i, i ^ mask) for i in range(count)])]
    pallas_call x7 -> x6, Pallas kernels: 4.91 us -> 4.91 us  [kernel_call(): pl.pallas_call(kernel, out_shape=tuple(shapes), scratch_shapes=list(scrat...]
  transfers between devices with their start and end apart: 20 -> 20, of which waited for: 10 -> 11; matrix products, arithmetic and copies ran while one was open for 0% -> 0% of each run, Pallas kernels for 5% -> 5%
where the time goes in v6:
time: 54.8 us; the launch traced here: 54.6 us
  waiting for transfers between devices  29.7 us (54%)
  starting transfers between devices  18.1 us (33%)
  Pallas kernels  6.04 us (11%)
  between operations  0.73 us (1%)
    ppermute x20, waiting for transfers between devices, swap(): return lax.ppermute(array, 'ctx', [(i, i ^ mask) for i in range(count)])  29.7 us
    ppermute x20, starting transfers between devices, swap(): return lax.ppermute(array, 'ctx', [(i, i ^ mask) for i in range(count)])  18.1 us
    pallas_call x6, Pallas kernels, kernel_call(): pl.pallas_call(kernel, out_shape=tuple(shapes), scratch_shapes=list(scrat...  4.91 us
    pallas_call x1, Pallas kernels, body(): pl.pallas_call(pack_kernel, out_shape=(struct((own_keys + 16, own_keys),...  1.13 us
  transfers between devices with their start and end apart: 20, of which 11 were waited for; matrix products, arithmetic and copies ran while one was open for 0% of the time, Pallas kernels for 5%

profile of v6, /device:TPU:0, one launch (start us, length us, event | category | flops | bytes accessed | tf_op | source)
XLA Modules:
  0.0 54.6 jit_solution(5443478708643438674)
XLA Ops:
  0.6 3.0 %collective-permute-start.1 = (bf16[2,576,128]{2,1,0:T(8,128)(2,1)}, bf16[2,576,128]{2,1,0:T(8,128)(2,1)S(1)}, u32[]{:S(2)}, u32[]{:S(2)}) collective-permute-start(bf16[2,576,128]{2,1,0:T(8,128)(2,1)} %bitcast.9), channel_id=1, source_target_pairs={{0,2},{1,3},{2,0},{3,1},{4,6},{5,7},{6,4},{7,5},{8,10},{9,11},{10,... | collective-permute-start | bytes 884744 | tf_op jit(solution)/shard_map/ppermute | solution.py:34
  3.7 0.0 collective-permute-start
  3.7 7.2 %collective-permute-done.1.refs_2_ = bf16[2,576,128]{2,1,0:T(8,128)(2,1)S(1)} collective-permute-done((bf16[2,576,128]{2,1,0:T(8,128)(2,1)}, bf16[2,576,128]{2,1,0:T(8,128)(2,1)S(1)}, u32[]{:S(2)}, u32[]{:S(2)}) %collective-permute-start.1) | collective-permute-done | bytes 294944 | tf_op jit(solution)/shard_map/ppermute | solution.py:34
  10.9 0.0 collective-permute-start.2
  10.9 2.8 %collective-permute-start.7 = (bf16[576,128]{1,0:T(8,128)(2,1)}, bf16[576,128]{1,0:T(8,128)(2,1)S(1)}, u32[]{:S(2)}, u32[]{:S(2)}) collective-permute-start(bf16[576,128]{1,0:T(8,128)(2,1)} %bitcast.12), channel_id=1, source_target_pairs={{0,8},{1,9},{2,10},{3,11},{4,12},{5,13},{6,14},{7,15},{8,0},{9,1},... | collective-permute-start | bytes 442376 | tf_op jit(solution)/shard_map/ppermute | solution.py:34
  13.7 1.1 %pack.1 = (bf16[144,128]{1,0:T(8,128)(2,1)S(1)}, bf16[144,128]{1,0:T(8,128)(2,1)S(1)}, bf16[2,576,128]{2,1,0:T(8,128)(2,1)S(1)}, bf16[576,128]{1,0:T(8,128)(2,1)S(1)}) custom-call(s32[4,128]{1,0:T(4,128)} %bitcast.16, bf16[128,128]{1,0:T(8,128)(2,1)} %keys_hbm.1, f32[2,64]{1,0:T(2,128)} %weight_hbm.1, s32[2]{0:T(128)} %pos_hbm.1, ...), custom_call_target="tpu_custom_call" | custom-call | tf_op jit(solution)/shard_map/pack/pallas_call | solution.py:307
  14.9 0.3 collective-permute-start.3
  15.2 1.5 %collective-permute-start.4 = (bf16[144,128]{1,0:T(8,128)(2,1)S(1)}, bf16[144,128]{1,0:T(8,128)(2,1)S(1)}, u32[]{:S(2)}, u32[]{:S(2)}) collective-permute-start(bf16[144,128]{1,0:T(8,128)(2,1)S(1)} %get-tuple-element.31.refs_4_), channel_id=1, source_target_pairs={{0,2},{1,3},{2,0},{3,1},{4,6},{5,7},{6,4},{7,5},{8,10},{9,11},{10,... | collective-permute-start | bytes 110600 | tf_op jit(solution)/shard_map/ppermute | solution.py:34
  16.6 0.0 collective-permute-done.3.refs_5_
  16.6 1.6 %collective-permute-start.6 = (bf16[576,128]{1,0:T(8,128)(2,1)}, bf16[576,128]{1,0:T(8,128)(2,1)S(1)}, u32[]{:S(2)}, u32[]{:S(2)}) collective-permute-start(bf16[576,128]{1,0:T(8,128)(2,1)} %bitcast.14), channel_id=1, source_target_pairs={{0,4},{1,5},{2,6},{3,7},{4,0},{5,1},{6,2},{7,3},{8,12},{9,13},{10,... | collective-permute-start | bytes 442376 | tf_op jit(solution)/shard_map/ppermute | solution.py:34
  18.2 0.9 %collective-permute-done.4.refs_6_ = bf16[144,128]{1,0:T(8,128)(2,1)S(1)} collective-permute-done((bf16[144,128]{1,0:T(8,128)(2,1)S(1)}, bf16[144,128]{1,0:T(8,128)(2,1)S(1)}, u32[]{:S(2)}, u32[]{:S(2)}) %collective-permute-start.4) | collective-permute-done | bytes 36896 | tf_op jit(solution)/shard_map/ppermute | solution.py:34
  19.1 1.6 %collective-permute-start.8 = (bf16[144,128]{1,0:T(8,128)(2,1)S(1)}, bf16[144,128]{1,0:T(8,128)(2,1)S(1)}, u32[]{:S(2)}, u32[]{:S(2)}) collective-permute-start(bf16[144,128]{1,0:T(8,128)(2,1)S(1)} %get-tuple-element.33.refs_11_.refs_8_), channel_id=1, source_target_pairs={{0,4},{1,5},{2,6},{3,7},{4,0},{5,1},{6,2},{7,3},{8,12},{9,13},{10,... | collective-permute-start | bytes 110600 | tf_op jit(solution)/shard_map/ppermute | solution.py:34
  20.7 1.0 %collective-permute-done.7.refs_10_ = bf16[576,128]{1,0:T(8,128)(2,1)S(1)} collective-permute-done((bf16[576,128]{1,0:T(8,128)(2,1)}, bf16[576,128]{1,0:T(8,128)(2,1)S(1)}, u32[]{:S(2)}, u32[]{:S(2)}) %collective-permute-start.7) | collective-permute-done | bytes 147488 | tf_op jit(solution)/shard_map/ppermute | solution.py:34
  21.7 0.8 %collective-permute-start.10 = (bf16[576,128]{1,0:T(8,128)(2,1)S(1)}, bf16[576,128]{1,0:T(8,128)(2,1)S(1)}, u32[]{:S(2)}, u32[]{:S(2)}) collective-permute-start(bf16[576,128]{1,0:T(8,128)(2,1)S(1)} %collective-permute-done.7.refs_10_), channel_id=1, source_target_pairs={{0,4},{1,5},{2,6},{3,7},{4,0},{5,1},{6,2},{7,3},{8,12},{9,13},{10,... | collective-permute-start | bytes 442376 | tf_op jit(solution)/shard_map/ppermute | solution.py:34
  22.5 3.2 %collective-permute-done.8.refs_12_.refs_0_.refs_13_ = bf16[144,128]{1,0:T(8,128)(2,1)S(1)} collective-permute-done((bf16[144,128]{1,0:T(8,128)(2,1)S(1)}, bf16[144,128]{1,0:T(8,128)(2,1)S(1)}, u32[]{:S(2)}, u32[]{:S(2)}) %collective-permute-start.8) | collective-permute-done | bytes 36896 | tf_op jit(solution)/shard_map/ppermute | solution.py:34
  25.7 0.2 collective-permute-start.9
  25.9 4.6 %collective-permute-done.9.refs_13_.refs_9_ = bf16[144,128]{1,0:T(8,128)(2,1)S(1)} collective-permute-done((bf16[144,128]{1,0:T(8,128)(2,1)S(1)}, bf16[144,128]{1,0:T(8,128)(2,1)S(1)}, u32[]{:S(2)}, u32[]{:S(2)}) %collective-permute-start.9) | collective-permute-done | bytes 36896 | tf_op jit(solution)/shard_map/ppermute | solution.py:34
  30.5 0.0 collective-permute-start.5
  30.5 1.2 %collective-permute-done.5.refs_7_ = bf16[144,128]{1,0:T(8,128)(2,1)S(1)} collective-permute-done((bf16[144,128]{1,0:T(8,128)(2,1)S(1)}, bf16[144,128]{1,0:T(8,128)(2,1)S(1)}, u32[]{:S(2)}, u32[]{:S(2)}) %collective-permute-start.5) | collective-permute-done | bytes 36896 | tf_op jit(solution)/shard_map/ppermute | solution.py:34
  31.7 0.1 collective-permute-start.11
  31.9 0.0 collective-permute-done.6.refs_9_
  31.9 0.0 collective-permute-done.refs_1_
  31.9 0.0 collective-permute-done.2.refs_3_
  31.9 1.6 %shard_map.94 = (f32[8,128,384]{2,1,0:T(8,128)S(1)}, f32[8,384]{1,0:T(8,128)S(1)}, f32[4,4,128]{2,1,0:T(4,128)S(1)}, bf16[1024,576]{1,0:T(8,128)(2,1)S(1)}, bf16...) custom-call(bf16[2,576,128]{2,1,0:T(8,128)(2,1)S(1)} %get-tuple-element.30.refs_0_, ...), custom_call_target="tpu_custom_call" | custom-call | flops 452984832 | bytes 4790272 | tf_op jit(solution)/shard_map/pallas_call | solution.py:20
  33.5 2.2 %collective-permute-done.11.refs_5_.refs_1_.refs_14_ = bf16[144,128]{1,0:T(8,128)(2,1)S(1)} collective-permute-done((bf16[144,128]{1,0:T(8,128)(2,1)S(1)}, bf16[144,128]{1,0:T(8,128)(2,1)S(1)}, u32[]{:S(2)}, u32[]{:S(2)}) %collective-permute-start.11) | collective-permute-done | bytes 36896 | tf_op jit(solution)/shard_map/ppermute | solution.py:34
  35.7 0.0 collective-permute-done.10.refs_4_
  35.7 0.7 %shard_map.95 = (f32[8,128,128]{2,1,0:T(8,128)S(1)}, f32[8,128]{1,0:T(8,128)S(1)}, f32[4,4,128]{2,1,0:T(4,128)S(1)}) custom-call(bf16[1024,576]{1,0:T(8,128)(2,1)S(1)} %get-tuple-element.35.refs_0_, bf16[512,128]{1,0:T(8,128)(2,1)S(1)} %get-tuple-element.36.refs_1_.flat_ref.refs_4_, f32[64,8]{1,0:T(8,128)S(1)} %get-tuple-element.37.refs_2_.column_ref.refs_5_, ...), custom_call_target="tpu_custom_call" | custom-call | flops 150994944 | bytes 2037760 | tf_op jit(solution)/shard_map/pallas_call | solution.py:20
  36.4 0.1 collective-permute-start.12
  36.5 1.5 %collective-permute-start.13 = (f32[4,4,128]{2,1,0:T(4,128)S(1)}, f32[4,4,128]{2,1,0:T(4,128)S(1)}, u32[]{:S(2)}, u32[]{:S(2)}) collective-permute-start(f32[4,4,128]{2,1,0:T(4,128)S(1)} %add.9.refs_0_), channel_id=1, source_target_pairs={{0,2},{1,3},{2,0},{3,1},{4,6},{5,7},{6,4},{7,5},{8,10},{9,11},{10,... | collective-permute-start | bytes 24584 | tf_op jit(solution)/shard_map/ppermute | solution.py:34
  38.0 0.3 collective-permute-start.14
  38.3 0.2 shard_map.96
  38.6 0.0 collective-permute-done.12.refs_1_
  38.6 1.6 %collective-permute-done.13.refs_2_ = f32[4,4,128]{2,1,0:T(4,128)S(1)} collective-permute-done((f32[4,4,128]{2,1,0:T(4,128)S(1)}, f32[4,4,128]{2,1,0:T(4,128)S(1)}, u32[]{:S(2)}, u32[]{:S(2)}) %collective-permute-start.13) | collective-permute-done | bytes 8224 | tf_op jit(solution)/shard_map/ppermute | solution.py:34
  40.2 0.9 %collective-permute-done.14.refs_3_ = f32[4,4,128]{2,1,0:T(4,128)S(1)} collective-permute-done((f32[4,4,128]{2,1,0:T(4,128)S(1)}, f32[4,4,128]{2,1,0:T(4,128)S(1)}, u32[]{:S(2)}, u32[]{:S(2)}) %collective-permute-start.14) | collective-permute-done | bytes 8224 | tf_op jit(solution)/shard_map/ppermute | solution.py:34
  41.1 0.7 %shard_map.97 = (bf16[128,128]{1,0:T(8,128)(2,1)S(1)}, bf16[128,128]{1,0:T(8,128)(2,1)S(1)}, bf16[512,256]{1,0:T(8,128)(2,1)S(1)}, f32[8,256]{1,0:T(8,128)S(1)}) custom-call(f32[4,4,128]{2,1,0:T(4,128)S(1)} %add.9.refs_0_, f32[4,4,128]{2,1,0:T(4,128)S(1)} %collective-permute-done.12.refs_1_, f32[4,4,128]{2,1,0:T(4,128)S(1)} %collective-permute-done.13.refs_2_, ...), custom_call_target="tpu_custom_call" | custom-call | flops 67108864 | bytes 3137536 | tf_op jit(solution)/shard_map/pallas_call | solution.py:20
  41.8 1.0 %shard_map.98 = (f32[128,128]{1,0:T(8,128)S(1)}, f32[128,128]{1,0:T(8,128)S(1)}, f32[2,136,128]{2,1,0:T(8,128)S(1)}, f32[2,136,128]{2,1,0:T(8,128)S(1)}) custom-call(f32[4,4,128]{2,1,0:T(4,128)S(1)} %add.9.refs_0_, f32[4,4,128]{2,1,0:T(4,128)S(1)} %collective-permute-done.12.refs_1_, f32[4,4,128]{2,1,0:T(4,128)S(1)} %collective-permute-done.13.refs_2_, ...), custom_call_target="tpu_custom_call" | custom-call | flops 67108864 | bytes 3102720 | tf_op jit(solution)/shard_map/pallas_call | solution.py:20
  42.8 0.7 %collective-permute-start.18 = (f32[2,136,128]{2,1,0:T(8,128)S(1)}, f32[2,136,128]{2,1,0:T(8,128)S(1)}, u32[]{:S(2)}, u32[]{:S(2)}) collective-permute-start(f32[2,136,128]{2,1,0:T(8,128)S(1)} %get-tuple-element.53), channel_id=1, source_target_pairs={{0,2},{1,3},{2,0},{3,1},{4,6},{5,7},{6,4},{7,5},{8,10},{9,11},{10,... | collective-permute-start | bytes 417800 | tf_op jit(solution)/shard_map/ppermute | solution.py:34
  43.5 0.1 collective-permute-start.15
  43.6 1.9 %collective-permute-start.16 = (bf16[128,128]{1,0:T(8,128)(2,1)S(1)}, bf16[128,128]{1,0:T(8,128)(2,1)S(1)}, u32[]{:S(2)}, u32[]{:S(2)}) collective-permute-start(bf16[128,128]{1,0:T(8,128)(2,1)S(1)} %get-tuple-element.51), channel_id=1, source_target_pairs={{0,4},{1,5},{2,6},{3,7},{4,0},{5,1},{6,2},{7,3},{8,12},{9,13},{10,... | collective-permute-start | bytes 98312 | tf_op jit(solution)/shard_map/ppermute | solution.py:34
  45.5 3.0 %collective-permute-done.18 = f32[2,136,128]{2,1,0:T(8,128)S(1)} collective-permute-done((f32[2,136,128]{2,1,0:T(8,128)S(1)}, f32[2,136,128]{2,1,0:T(8,128)S(1)}, u32[]{:S(2)}, u32[]{:S(2)}) %collective-permute-start.18) | collective-permute-done | bytes 139296 | tf_op jit(solution)/shard_map/ppermute | solution.py:34
  48.6 0.1 collective-permute-start.19
  48.7 0.0 collective-permute-done.16
  48.7 1.4 %collective-permute-start.17 = (bf16[128,128]{1,0:T(8,128)(2,1)S(1)}, bf16[128,128]{1,0:T(8,128)(2,1)S(1)}, u32[]{:S(2)}, u32[]{:S(2)}) collective-permute-start(bf16[128,128]{1,0:T(8,128)(2,1)S(1)} %add_convert_fusion), channel_id=1, source_target_pairs={{0,8},{1,9},{2,10},{3,11},{4,12},{5,13},{6,14},{7,15},{8,0},{9,1},... | collective-permute-start | bytes 98312 | tf_op jit(solution)/shard_map/ppermute | solution.py:34
  50.1 0.0 collective-permute-done.15.refs_1_
  50.1 3.8 %collective-permute-done.17.refs_2_ = bf16[128,128]{1,0:T(8,128)(2,1)S(1)} collective-permute-done((bf16[128,128]{1,0:T(8,128)(2,1)S(1)}, bf16[128,128]{1,0:T(8,128)(2,1)S(1)}, u32[]{:S(2)}, u32[]{:S(2)}) %collective-permute-start.17) | collective-permute-done | bytes 32800 | tf_op jit(solution)/shard_map/ppermute | solution.py:34
  54.0 0.0 collective-permute-done.19.refs_4_
  54.0 0.7 %shard_map.99 = (f32[128,128]{1,0:T(8,128)}, f32[2,64]{1,0:T(2,128)}, f32[128,128]{1,0:T(8,128)}) custom-call(f32[128,128]{1,0:T(8,128)S(1)} %get-tuple-element.48.refs_0_, bf16[128,128]{1,0:T(8,128)(2,1)S(1)} %collective-permute-done.15.refs_1_, bf16[128,128]{1,0:T(8,128)(2,1)S(1)} %collective-permute-done.17.refs_2_, ...), custom_call_target="tpu_custom_call" | custom-call | bytes 401920 | tf_op jit(solution)/shard_map/pallas_call | solution.py:20
  (4 shorter events, 0.0 us)
Async XLA Ops:
  0.6 10.2 %collective-permute-start.1 = (bf16[2,576,128]{2,1,0:T(8,128)(2,1)}, bf16[2,576,128]{2,1,0:T(8,128)(2,1)S(1)}, u32[]{:S(2)}, u32[]{:S(2)}) collective-permute-start(bf16[2,576,128]{2,1,0:T(8,128)(2,1)} %bitcast.9), channel_id=1, source_target_pairs={{0,2},{1,3},{2,0},{3,1},{4,6},{5,7},{6,4},{7,5},{8,10},{9,11},{10,... | collective-permute-start | bytes 884744 | tf_op jit(solution)/shard_map/ppermute | solution.py:34
  3.7 28.2 %collective-permute-start = (bf16[2,576,128]{2,1,0:T(8,128)(2,1)}, bf16[2,576,128]{2,1,0:T(8,128)(2,1)S(1)}, u32[]{:S(2)}, u32[]{:S(2)}) collective-permute-start(bf16[2,576,128]{2,1,0:T(8,128)(2,1)} %bitcast.10), channel_id=1, source_target_pairs={{0,1},{1,0},{2,3},{3,2},{4,5},{5,4},{6,7},{7,6},{8,9},{9,8},{10,11... | collective-permute-start | bytes 884744 | tf_op jit(solution)/shard_map/ppermute | solution.py:34
  10.9 21.0 %collective-permute-start.2 = (bf16[2,576,128]{2,1,0:T(8,128)(2,1)S(1)}, bf16[2,576,128]{2,1,0:T(8,128)(2,1)S(1)}, u32[]{:S(2)}, u32[]{:S(2)}) collective-permute-start(bf16[2,576,128]{2,1,0:T(8,128)(2,1)S(1)} %collective-permute-done.1.refs_2_), channel_id=1, source_target_pairs={{0,1},{1,0},{2,3},{3,2},{4,5},{5,4},{6,7},{7,6},{8,9},{9,8},{10,11... | collective-permute-start | bytes 884744 | tf_op jit(solution)/shard_map/ppermute | solution.py:34
  10.9 10.8 %collective-permute-start.7 = (bf16[576,128]{1,0:T(8,128)(2,1)}, bf16[576,128]{1,0:T(8,128)(2,1)S(1)}, u32[]{:S(2)}, u32[]{:S(2)}) collective-permute-start(bf16[576,128]{1,0:T(8,128)(2,1)} %bitcast.12), channel_id=1, source_target_pairs={{0,8},{1,9},{2,10},{3,11},{4,12},{5,13},{6,14},{7,15},{8,0},{9,1},... | collective-permute-start | bytes 442376 | tf_op jit(solution)/shard_map/ppermute | solution.py:34
  14.9 1.8 %collective-permute-start.3 = (bf16[144,128]{1,0:T(8,128)(2,1)S(1)}, bf16[144,128]{1,0:T(8,128)(2,1)S(1)}, u32[]{:S(2)}, u32[]{:S(2)}) collective-permute-start(bf16[144,128]{1,0:T(8,128)(2,1)S(1)} %get-tuple-element.31.refs_4_), channel_id=1, source_target_pairs={{0,1},{1,0},{2,3},{3,2},{4,5},{5,4},{6,7},{7,6},{8,9},{9,8},{10,11... | collective-permute-start | bytes 110600 | tf_op jit(solution)/shard_map/ppermute | solution.py:34
  15.2 4.0 %collective-permute-start.4 = (bf16[144,128]{1,0:T(8,128)(2,1)S(1)}, bf16[144,128]{1,0:T(8,128)(2,1)S(1)}, u32[]{:S(2)}, u32[]{:S(2)}) collective-permute-start(bf16[144,128]{1,0:T(8,128)(2,1)S(1)} %get-tuple-element.31.refs_4_), channel_id=1, source_target_pairs={{0,2},{1,3},{2,0},{3,1},{4,6},{5,7},{6,4},{7,5},{8,10},{9,11},{10,... | collective-permute-start | bytes 110600 | tf_op jit(solution)/shard_map/ppermute | solution.py:34
  16.6 15.2 %collective-permute-start.6 = (bf16[576,128]{1,0:T(8,128)(2,1)}, bf16[576,128]{1,0:T(8,128)(2,1)S(1)}, u32[]{:S(2)}, u32[]{:S(2)}) collective-permute-start(bf16[576,128]{1,0:T(8,128)(2,1)} %bitcast.14), channel_id=1, source_target_pairs={{0,4},{1,5},{2,6},{3,7},{4,0},{5,1},{6,2},{7,3},{8,12},{9,13},{10,... | collective-permute-start | bytes 442376 | tf_op jit(solution)/shard_map/ppermute | solution.py:34
  19.1 6.5 %collective-permute-start.8 = (bf16[144,128]{1,0:T(8,128)(2,1)S(1)}, bf16[144,128]{1,0:T(8,128)(2,1)S(1)}, u32[]{:S(2)}, u32[]{:S(2)}) collective-permute-start(bf16[144,128]{1,0:T(8,128)(2,1)S(1)} %get-tuple-element.33.refs_11_.refs_8_), channel_id=1, source_target_pairs={{0,4},{1,5},{2,6},{3,7},{4,0},{5,1},{6,2},{7,3},{8,12},{9,13},{10,... | collective-permute-start | bytes 110600 | tf_op jit(solution)/shard_map/ppermute | solution.py:34
  21.7 14.0 %collective-permute-start.10 = (bf16[576,128]{1,0:T(8,128)(2,1)S(1)}, bf16[576,128]{1,0:T(8,128)(2,1)S(1)}, u32[]{:S(2)}, u32[]{:S(2)}) collective-permute-start(bf16[576,128]{1,0:T(8,128)(2,1)S(1)} %collective-permute-done.7.refs_10_), channel_id=1, source_target_pairs={{0,4},{1,5},{2,6},{3,7},{4,0},{5,1},{6,2},{7,3},{8,12},{9,13},{10,... | collective-permute-start | bytes 442376 | tf_op jit(solution)/shard_map/ppermute | solution.py:34
  25.7 4.9 %collective-permute-start.9 = (bf16[144,128]{1,0:T(8,128)(2,1)S(1)}, bf16[144,128]{1,0:T(8,128)(2,1)S(1)}, u32[]{:S(2)}, u32[]{:S(2)}) collective-permute-start(bf16[144,128]{1,0:T(8,128)(2,1)S(1)} %get-tuple-element.33.refs_11_.refs_8_), channel_id=1, source_target_pairs={{0,8},{1,9},{2,10},{3,11},{4,12},{5,13},{6,14},{7,15},{8,0},{9,1},... | collective-permute-start | bytes 110600 | tf_op jit(solution)/shard_map/ppermute | solution.py:34
  30.5 1.2 %collective-permute-start.5 = (bf16[144,128]{1,0:T(8,128)(2,1)S(1)}, bf16[144,128]{1,0:T(8,128)(2,1)S(1)}, u32[]{:S(2)}, u32[]{:S(2)}) collective-permute-start(bf16[144,128]{1,0:T(8,128)(2,1)S(1)} %collective-permute-done.4.refs_6_), channel_id=1, source_target_pairs={{0,1},{1,0},{2,3},{3,2},{4,5},{5,4},{6,7},{7,6},{8,9},{9,8},{10,11... | collective-permute-start | bytes 110600 | tf_op jit(solution)/shard_map/ppermute | solution.py:34
  31.7 4.0 %collective-permute-start.11 = (bf16[144,128]{1,0:T(8,128)(2,1)S(1)}, bf16[144,128]{1,0:T(8,128)(2,1)S(1)}, u32[]{:S(2)}, u32[]{:S(2)}) collective-permute-start(bf16[144,128]{1,0:T(8,128)(2,1)S(1)} %collective-permute-done.9.refs_13_.refs_9_), channel_id=1, source_target_pairs={{0,4},{1,5},{2,6},{3,7},{4,0},{5,1},{6,2},{7,3},{8,12},{9,13},{10,... | collective-permute-start | bytes 110600 | tf_op jit(solution)/shard_map/ppermute | solution.py:34
  36.4 2.2 %collective-permute-start.12 = (f32[4,4,128]{2,1,0:T(4,128)S(1)}, f32[4,4,128]{2,1,0:T(4,128)S(1)}, u32[]{:S(2)}, u32[]{:S(2)}) collective-permute-start(f32[4,4,128]{2,1,0:T(4,128)S(1)} %add.9.refs_0_), channel_id=1, source_target_pairs={{0,1},{1,0},{2,3},{3,2},{4,5},{5,4},{6,7},{7,6},{8,9},{9,8},{10,11... | collective-permute-start | bytes 24584 | tf_op jit(solution)/shard_map/ppermute | solution.py:34
  36.5 3.7 %collective-permute-start.13 = (f32[4,4,128]{2,1,0:T(4,128)S(1)}, f32[4,4,128]{2,1,0:T(4,128)S(1)}, u32[]{:S(2)}, u32[]{:S(2)}) collective-permute-start(f32[4,4,128]{2,1,0:T(4,128)S(1)} %add.9.refs_0_), channel_id=1, source_target_pairs={{0,2},{1,3},{2,0},{3,1},{4,6},{5,7},{6,4},{7,5},{8,10},{9,11},{10,... | collective-permute-start | bytes 24584 | tf_op jit(solution)/shard_map/ppermute | solution.py:34
  38.0 3.1 %collective-permute-start.14 = (f32[4,4,128]{2,1,0:T(4,128)S(1)}, f32[4,4,128]{2,1,0:T(4,128)S(1)}, u32[]{:S(2)}, u32[]{:S(2)}) collective-permute-start(f32[4,4,128]{2,1,0:T(4,128)S(1)} %add.9.refs_0_), channel_id=1, source_target_pairs={{0,3},{1,2},{2,1},{3,0},{4,7},{5,6},{6,5},{7,4},{8,11},{9,10},{10,... | collective-permute-start | bytes 24584 | tf_op jit(solution)/shard_map/ppermute | solution.py:34
  42.8 5.8 %collective-permute-start.18 = (f32[2,136,128]{2,1,0:T(8,128)S(1)}, f32[2,136,128]{2,1,0:T(8,128)S(1)}, u32[]{:S(2)}, u32[]{:S(2)}) collective-permute-start(f32[2,136,128]{2,1,0:T(8,128)S(1)} %get-tuple-element.53), channel_id=1, source_target_pairs={{0,2},{1,3},{2,0},{3,1},{4,6},{5,7},{6,4},{7,5},{8,10},{9,11},{10,... | collective-permute-start | bytes 417800 | tf_op jit(solution)/shard_map/ppermute | solution.py:34
  43.5 6.6 %collective-permute-start.15 = (bf16[128,128]{1,0:T(8,128)(2,1)S(1)}, bf16[128,128]{1,0:T(8,128)(2,1)S(1)}, u32[]{:S(2)}, u32[]{:S(2)}) collective-permute-start(bf16[128,128]{1,0:T(8,128)(2,1)S(1)} %get-tuple-element.49), channel_id=1, source_target_pairs={{0,4},{1,5},{2,6},{3,7},{4,0},{5,1},{6,2},{7,3},{8,12},{9,13},{10,... | collective-permute-start | bytes 98312 | tf_op jit(solution)/shard_map/ppermute | solution.py:34
  43.6 5.1 %collective-permute-start.16 = (bf16[128,128]{1,0:T(8,128)(2,1)S(1)}, bf16[128,128]{1,0:T(8,128)(2,1)S(1)}, u32[]{:S(2)}, u32[]{:S(2)}) collective-permute-start(bf16[128,128]{1,0:T(8,128)(2,1)S(1)} %get-tuple-element.51), channel_id=1, source_target_pairs={{0,4},{1,5},{2,6},{3,7},{4,0},{5,1},{6,2},{7,3},{8,12},{9,13},{10,... | collective-permute-start | bytes 98312 | tf_op jit(solution)/shard_map/ppermute | solution.py:34
  48.6 5.3 %collective-permute-start.19 = (f32[136,128]{1,0:T(8,128)S(1)}, f32[136,128]{1,0:T(8,128)S(1)}, u32[]{:S(2)}, u32[]{:S(2)}) collective-permute-start(f32[136,128]{1,0:T(8,128)S(1)} %get-tuple-element.57), channel_id=1, source_target_pairs={{0,1},{1,0},{2,3},{3,2},{4,5},{5,4},{6,7},{7,6},{8,9},{9,8},{10,11... | collective-permute-start | bytes 208904 | tf_op jit(solution)/shard_map/ppermute | solution.py:34
  48.7 5.2 %collective-permute-start.17 = (bf16[128,128]{1,0:T(8,128)(2,1)S(1)}, bf16[128,128]{1,0:T(8,128)(2,1)S(1)}, u32[]{:S(2)}, u32[]{:S(2)}) collective-permute-start(bf16[128,128]{1,0:T(8,128)(2,1)S(1)} %add_convert_fusion), channel_id=1, source_target_pairs={{0,8},{1,9},{2,10},{3,11},{4,12},{5,13},{6,14},{7,15},{8,0},{9,1},... | collective-permute-start | bytes 98312 | tf_op jit(solution)/shard_map/ppermute | solution.py:34
